TPU v7x, 32 devices: a whole 2x2x4 slice. The times are simulated.
32 devices in a mesh: dp: 4 (over z), expert: 8 (over y, x, core).
Axes of the slice: x: 2, y: 2, z: 4, core: 2. Of those that a mesh axis runs over, the one named last changes fastest.
Arguments:
- tokens: bfloat16 [2, 2048, 1536], P(None, ('dp', 'expert')), may hold values from -6 to 6
- segments: int32 [2, 32, 64], P(None, ('dp', 'expert')), may hold values from 0 to 1, never falling along the last dimension, each value on 1 to 56 neighbouring positions
- routes: int32 [2, 2048, 8], P(None, ('dp', 'expert')), may hold values from 0 to 23, all different within a row; in each aligned block of 64 rows (0 to 63, 64 to 127, ..., all dimensions but the last counted through in order) at most 32 rows name the same one
- cotangent: bfloat16 [2, 2048, 1536], P(None, ('dp', 'expert')), may hold values from -6 to 6
- gain_attn: bfloat16 [1536], P(('dp', 'expert')), may hold values from 0.5 to 1.5
- attn_in: bfloat16 [1536, 2560], P(('dp', 'expert')), may hold values from -0.15625 to 0.15625
- attn_out: bfloat16 [1536, 1536], P(('dp', 'expert')), may hold values from -1.25 to 1.25
- gain_ffn: bfloat16 [1536], P(('dp', 'expert')), may hold values from 0.5 to 1.5
- router: bfloat16 [1536, 24], P(('dp', 'expert')), may hold values from -0.078125 to 0.078125
- expert_in: bfloat16 [24, 1536, 1024], P('expert', 'dp'), may hold values from -0.15625 to 0.15625
- expert_out: bfloat16 [24, 512, 1536], P('expert', 'dp'), may hold values from -1 to 1
Outputs:
- output: bfloat16 [2, 2048, 1536], P(None, ('dp', 'expert'))
- grad_tokens: float32 [2, 2048, 1536], P(None, ('dp', 'expert'))
- grad_gain_attn: float32 [1536], P(('dp', 'expert'))
- grad_attn_in: float32 [1536, 2560], P(('dp', 'expert'))
- grad_attn_out: float32 [1536, 1536], P(('dp', 'expert'))
- grad_gain_ffn: float32 [1536], P(('dp', 'expert'))
- grad_router: float32 [1536, 24], P(('dp', 'expert'))
- grad_expert_in: float32 [24, 1536, 1024], P('expert', 'dp')
- grad_expert_out: float32 [24, 512, 1536], P('expert', 'dp')
Inputs may be any that keep to these rules, and one draw needn't show every extreme that they name: `routes`: in each aligned block of 64 rows (one pack), no expert is named by more than 32 pairs, a bound that some block reaches; a row names 8 different experts. `segments`: each pack holds 2 whole sequences numbered in order, each of 1 to 56 tokens.
All inputs are finite; a program needn't handle non-finite values.
Results may differ from a plain program's by a relative error of at most 0.014.
The roundings to bfloat16 on the way count: a program that leaves them out, or rounds other values in their place, can miss the bound.
Values may be sent and summed in bfloat16 or wider, within the bound.
A program may use at most 192 MiB of HBM per device.

v0:
```python
import jax
import jax.numpy as jnp
from jax import lax
from jax.sharding import PartitionSpec as P

D = 1536
HEADS = 24
KV_HEADS = 8
HEAD = 64
FF = 512
TOP_K = 8


norm_eps = 1e-06
rope_base = 10000.0
neg_large = -1e30
highest = lax.Precision.HIGHEST


def rope_tables(segment, half_width):
    row_count = segment.shape[0]
    places = jnp.arange(row_count, dtype=jnp.int32)
    same_seq = segment[:, None] == segment[None, :]
    seq_start = jnp.min(jnp.where(same_seq, places[None, :], row_count), axis=1)
    offset = (places - seq_start).astype(jnp.float32)
    frequencies = rope_base ** (-jnp.arange(half_width, dtype=jnp.float32) / half_width)
    angles = offset[:, None] * frequencies[None, :]
    causal = same_seq & (places[None, :] <= places[:, None])
    return (jnp.cos(angles), jnp.sin(angles), causal)


def rotate(operand, cosine, sine_table):
    half_width = operand.shape[-1] // 2
    front_part = operand[..., :half_width]
    back_part = operand[..., half_width:]
    return jnp.concatenate(
        [
            front_part * cosine - back_part * sine_table,
            back_part * cosine + front_part * sine_table,
        ],
        axis=-1,
    )


def unrotate(gradient, cosine, sine_table):
    half_width = gradient.shape[-1] // 2
    front_part = gradient[..., :half_width]
    back_part = gradient[..., half_width:]
    return jnp.concatenate(
        [
            front_part * cosine + back_part * sine_table,
            back_part * cosine - front_part * sine_table,
        ],
        axis=-1,
    )


def slot_targets(route_now, expert_count, capacity):
    flat_ids = route_now.reshape(-1)
    onehot = (flat_ids[:, None] == jnp.arange(expert_count, dtype=jnp.int32)[None, :]).astype(
        jnp.int32
    )
    earlier = jnp.cumsum(onehot, axis=0) - onehot
    slot_index = jnp.sum(earlier * onehot, axis=1)
    return flat_ids * capacity + slot_index


def dense_fetch(gain_attn, attn_in, attn_out, gain_ffn, router):
    return (
        lax.all_gather(gain_attn, ("dp", "expert"), axis=0, tiled=True),
        lax.all_gather(attn_in, ("dp", "expert"), axis=0, tiled=True),
        lax.all_gather(attn_out, ("dp", "expert"), axis=0, tiled=True),
        lax.all_gather(gain_ffn, ("dp", "expert"), axis=0, tiled=True),
        lax.all_gather(router, ("dp", "expert"), axis=0, tiled=True),
    )


def expert_fetch(expert_in, expert_out):
    return (
        lax.all_gather(expert_in, "dp", axis=1, tiled=True),
        lax.all_gather(expert_out, "dp", axis=1, tiled=True),
    )


def dense_reduce(grad_set):
    return (
        lax.psum_scatter(grad_set[0], ("dp", "expert"), scatter_dimension=0, tiled=True),
        lax.psum_scatter(grad_set[1], ("dp", "expert"), scatter_dimension=0, tiled=True),
        lax.psum_scatter(grad_set[2], ("dp", "expert"), scatter_dimension=0, tiled=True),
        lax.psum_scatter(grad_set[3], ("dp", "expert"), scatter_dimension=0, tiled=True),
        lax.psum_scatter(grad_set[4], ("dp", "expert"), scatter_dimension=0, tiled=True),
    )


def expert_reduce(grad_set):
    return (
        lax.psum_scatter(grad_set[0], "dp", scatter_dimension=1, tiled=True),
        lax.psum_scatter(grad_set[1], "dp", scatter_dimension=1, tiled=True),
    )


def attention_scores(queries, key_rot, causal):
    score_scale = HEAD ** (-0.5)
    scores = (
        jnp.einsum("tkgh,skh->kgts", queries, key_rot, preferred_element_type=jnp.float32)
        * score_scale
    )
    return jnp.where(causal[None, None], scores, neg_large)


def forward_micro(tokens_now, segment, route_now, dense_set, expert_set, shapes):
    expert_count, capacity, group_count, local_experts = shapes
    gain_attn, qkv_weight, out_weight, gain_ffn, router_weight = dense_set
    expert_up, expert_down = expert_set
    row_count = tokens_now.shape[0]
    groups = HEADS // KV_HEADS
    q_width = HEADS * HEAD
    k_width = KV_HEADS * HEAD
    inputs = tokens_now.astype(jnp.float32)
    inv_first = lax.rsqrt(jnp.mean(inputs * inputs, axis=1, keepdims=True) + norm_eps)
    normed_first = (inputs * inv_first * gain_attn.astype(jnp.float32)).astype(jnp.bfloat16)
    qkv_full = jnp.dot(normed_first, qkv_weight, preferred_element_type=jnp.float32)
    cosine, sine_table, causal = rope_tables(segment, HEAD // 2)
    queries = rotate(
        qkv_full[:, :q_width].reshape(row_count, KV_HEADS, groups, HEAD),
        cosine[:, None, None, :],
        sine_table[:, None, None, :],
    ).astype(jnp.bfloat16)
    key_rot = rotate(
        qkv_full[:, q_width : q_width + k_width].reshape(row_count, KV_HEADS, HEAD),
        cosine[:, None, :],
        sine_table[:, None, :],
    ).astype(jnp.bfloat16)
    values = (
        qkv_full[:, q_width + k_width :].reshape(row_count, KV_HEADS, HEAD).astype(jnp.bfloat16)
    )
    scores = attention_scores(queries, key_rot, causal)
    score_peak = jnp.max(scores, axis=-1, keepdims=True)
    exp_scores = jnp.exp(scores - score_peak)
    exp_total = jnp.sum(exp_scores, axis=-1, keepdims=True)
    log_total = score_peak + jnp.log(exp_total)
    soft_probs = (exp_scores / exp_total).astype(jnp.bfloat16)
    attn_mixed = jnp.einsum(
        "kgts,skh->tkgh", soft_probs, values, preferred_element_type=jnp.float32
    )
    attn_mixed = attn_mixed.reshape(row_count, q_width).astype(jnp.bfloat16)
    middle = inputs + jnp.dot(attn_mixed, out_weight, preferred_element_type=jnp.float32)
    inv_second = lax.rsqrt(jnp.mean(middle * middle, axis=1, keepdims=True) + norm_eps)
    normed_second = (middle * inv_second * gain_ffn.astype(jnp.float32)).astype(jnp.bfloat16)
    logits = jnp.dot(normed_second, router_weight, preferred_element_type=jnp.float32)
    chosen = (
        route_now[:, :, None] == jnp.arange(expert_count, dtype=jnp.int32)[None, None, :]
    ).astype(jnp.float32)
    picked_logits = jnp.sum(chosen * logits[:, None, :], axis=-1)
    gate_values = jax.nn.softmax(picked_logits, axis=-1)
    targets = slot_targets(route_now, expert_count, capacity)
    source_rows = jnp.repeat(normed_second, TOP_K, axis=0)
    buffer = jnp.zeros((expert_count * capacity, D), jnp.bfloat16).at[targets].set(source_rows)
    send_rows = buffer.reshape(group_count, local_experts, capacity, D)
    received = lax.all_to_all(send_rows, "expert", split_axis=0, concat_axis=0, tiled=True)
    gate_up = jnp.einsum("secd,edf->secf", received, expert_up, preferred_element_type=jnp.float32)
    hidden = (jax.nn.silu(gate_up[..., :FF]) * gate_up[..., FF:]).astype(jnp.bfloat16)
    expert_result = jnp.einsum(
        "secf,efd->secd", hidden, expert_down, preferred_element_type=jnp.float32
    ).astype(jnp.bfloat16)
    returned = lax.all_to_all(expert_result, "expert", split_axis=0, concat_axis=0, tiled=True)
    picked = returned.reshape(expert_count * capacity, D)[targets].reshape(row_count, TOP_K, D)
    moe_sum = jnp.einsum(
        "tk,tkd->td", gate_values, picked, precision=highest, preferred_element_type=jnp.float32
    )
    result = (middle + moe_sum).astype(jnp.bfloat16)
    saved_state = (
        inputs,
        inv_first,
        normed_first,
        queries,
        key_rot,
        values,
        log_total,
        causal,
        cosine,
        sine_table,
        attn_mixed,
        middle,
        inv_second,
        normed_second,
        chosen,
        gate_values,
        targets,
        received,
        gate_up,
        hidden,
        picked,
    )
    return (result, saved_state)


def backward_micro(saved_state, cotan_now, dense_set, expert_set, shapes):
    expert_count, capacity, group_count, local_experts = shapes
    (
        inputs,
        inv_first,
        normed_first,
        queries,
        key_rot,
        values,
        log_total,
        causal,
        cosine,
        sine_table,
        attn_mixed,
        middle,
        inv_second,
        normed_second,
        chosen,
        gate_values,
        targets,
        received,
        gate_up,
        hidden,
        picked,
    ) = saved_state
    gain_attn, qkv_weight, out_weight, gain_ffn, router_weight = dense_set
    expert_up, expert_down = expert_set
    row_count = inputs.shape[0]
    groups = HEADS // KV_HEADS
    q_width = HEADS * HEAD
    k_width = KV_HEADS * HEAD
    score_scale = HEAD ** (-0.5)
    upstream = cotan_now.astype(jnp.float32)
    grad_gates = jnp.einsum(
        "td,tkd->tk", upstream, picked, precision=highest, preferred_element_type=jnp.float32
    )
    grad_picked = gate_values * (
        grad_gates - jnp.sum(gate_values * grad_gates, axis=-1, keepdims=True)
    )
    grad_logits = jnp.sum(chosen * grad_picked[:, :, None], axis=1).astype(jnp.bfloat16)
    grad_router = jnp.einsum(
        "td,te->de", normed_second, grad_logits, preferred_element_type=jnp.float32
    )
    grad_second = jnp.einsum(
        "te,de->td", grad_logits, router_weight, preferred_element_type=jnp.float32
    )
    grad_slots = (
        (gate_values[:, :, None] * upstream[:, None, :])
        .astype(jnp.bfloat16)
        .reshape(row_count * TOP_K, D)
    )
    grad_buffer = jnp.zeros((expert_count * capacity, D), jnp.bfloat16).at[targets].set(grad_slots)
    grad_buffer = grad_buffer.reshape(group_count, local_experts, capacity, D)
    grad_result = lax.all_to_all(grad_buffer, "expert", split_axis=0, concat_axis=0, tiled=True)
    grad_hidden = jnp.einsum(
        "secd,efd->secf", grad_result, expert_down, preferred_element_type=jnp.float32
    )
    grad_down = jnp.einsum(
        "secf,secd->efd", hidden, grad_result, preferred_element_type=jnp.float32
    )
    gate_part = gate_up[..., :FF]
    up_part = gate_up[..., FF:]
    gate_sigmoid = jax.nn.sigmoid(gate_part)
    grad_gate = grad_hidden * up_part * gate_sigmoid * (1.0 + gate_part * (1.0 - gate_sigmoid))
    grad_up_part = grad_hidden * (gate_part * gate_sigmoid)
    grad_gate_up = jnp.concatenate([grad_gate, grad_up_part], axis=-1).astype(jnp.bfloat16)
    grad_up = jnp.einsum(
        "secd,secf->edf", received, grad_gate_up, preferred_element_type=jnp.float32
    )
    grad_rows = jnp.einsum(
        "secf,edf->secd", grad_gate_up, expert_up, preferred_element_type=jnp.float32
    ).astype(jnp.bfloat16)
    grad_back = lax.all_to_all(grad_rows, "expert", split_axis=0, concat_axis=0, tiled=True)
    grad_choice = grad_back.reshape(expert_count * capacity, D)[targets].reshape(
        row_count, TOP_K, D
    )
    grad_second = grad_second + jnp.sum(grad_choice, axis=1, dtype=jnp.float32)
    unit_second = middle * inv_second
    pull_second = grad_second * gain_ffn.astype(jnp.float32)
    grad_gain_ffn = jnp.sum(grad_second * unit_second, axis=0)
    grad_middle = upstream + inv_second * (
        pull_second - unit_second * jnp.mean(pull_second * unit_second, axis=1, keepdims=True)
    )
    grad_branch = grad_middle.astype(jnp.bfloat16)
    grad_out_weight = jnp.einsum(
        "tc,td->cd", attn_mixed, grad_branch, preferred_element_type=jnp.float32
    )
    grad_mixed = jnp.einsum(
        "td,cd->tc", grad_branch, out_weight, preferred_element_type=jnp.float32
    )
    grad_mixed = grad_mixed.astype(jnp.bfloat16).reshape(row_count, KV_HEADS, groups, HEAD)
    scores = attention_scores(queries, key_rot, causal)
    soft_probs = jnp.exp(scores - log_total)
    grad_values = jnp.einsum(
        "kgts,tkgh->skh",
        soft_probs.astype(jnp.bfloat16),
        grad_mixed,
        preferred_element_type=jnp.float32,
    )
    grad_probs = jnp.einsum(
        "tkgh,skh->kgts", grad_mixed, values, preferred_element_type=jnp.float32
    )
    grad_scores = soft_probs * (
        grad_probs - jnp.sum(soft_probs * grad_probs, axis=-1, keepdims=True)
    )
    grad_scores = grad_scores.astype(jnp.bfloat16)
    grad_query = (
        jnp.einsum("kgts,skh->tkgh", grad_scores, key_rot, preferred_element_type=jnp.float32)
        * score_scale
    )
    grad_key = (
        jnp.einsum("kgts,tkgh->skh", grad_scores, queries, preferred_element_type=jnp.float32)
        * score_scale
    )
    grad_query = unrotate(grad_query, cosine[:, None, None, :], sine_table[:, None, None, :])
    grad_key = unrotate(grad_key, cosine[:, None, :], sine_table[:, None, :])
    grad_qkv = jnp.concatenate(
        [
            grad_query.reshape(row_count, q_width),
            grad_key.reshape(row_count, k_width),
            grad_values.reshape(row_count, k_width),
        ],
        axis=1,
    ).astype(jnp.bfloat16)
    grad_qkv_weight = jnp.einsum(
        "tc,tq->cq", normed_first, grad_qkv, preferred_element_type=jnp.float32
    )
    grad_first = jnp.einsum("tq,cq->tc", grad_qkv, qkv_weight, preferred_element_type=jnp.float32)
    unit_first = inputs * inv_first
    pull_first = grad_first * gain_attn.astype(jnp.float32)
    grad_gain_attn = jnp.sum(grad_first * unit_first, axis=0)
    grad_inputs = grad_middle + inv_first * (
        pull_first - unit_first * jnp.mean(pull_first * unit_first, axis=1, keepdims=True)
    )
    dense_grads = (grad_gain_attn, grad_qkv_weight, grad_out_weight, grad_gain_ffn, grad_router)
    expert_grads = (grad_up, grad_down)
    return (grad_inputs, dense_grads, expert_grads)


def add_pair(left_part, right_part):
    return left_part + right_part


def per_device(
    tokens,
    segments,
    routes,
    cotangent,
    gain_attn,
    attn_in,
    attn_out,
    gain_ffn,
    router,
    expert_in,
    expert_out,
):
    local_experts = expert_in.shape[0]
    group_count = lax.axis_size("expert")
    expert_count = local_experts * group_count
    micro_count = tokens.shape[0]
    row_count = tokens.shape[1]
    capacity = (row_count * TOP_K * 5 // (4 * expert_count) + 7) // 8 * 8
    shapes = (expert_count, capacity, group_count, local_experts)
    outputs = []
    grad_list = []
    dense_total = None
    expert_total = None
    for micro_index in range(micro_count):
        dense_set = dense_fetch(gain_attn, attn_in, attn_out, gain_ffn, router)
        expert_set = expert_fetch(expert_in, expert_out)
        result, saved_state = forward_micro(
            tokens[micro_index],
            segments[micro_index, 0],
            routes[micro_index],
            dense_set,
            expert_set,
            shapes,
        )
        dense_set = dense_fetch(gain_attn, attn_in, attn_out, gain_ffn, router)
        expert_set = expert_fetch(expert_in, expert_out)
        grad_inputs, dense_grads, expert_grads = backward_micro(
            saved_state, cotangent[micro_index], dense_set, expert_set, shapes
        )
        dense_grads = dense_reduce(dense_grads)
        expert_grads = expert_reduce(expert_grads)
        if dense_total is None:
            dense_total = dense_grads
            expert_total = expert_grads
        else:
            dense_total = jax.tree.map(add_pair, dense_total, dense_grads)
            expert_total = jax.tree.map(add_pair, expert_total, expert_grads)
        outputs.append(result)
        grad_list.append(grad_inputs)
    return (
        jnp.stack(outputs, axis=0),
        jnp.stack(grad_list, axis=0),
        dense_total[0],
        dense_total[1],
        dense_total[2],
        dense_total[3],
        dense_total[4],
        expert_total[0],
        expert_total[1],
    )


def solution(mesh):
    placed = (
        P(None, ("dp", "expert"), None),
        P(None, ("dp", "expert"), None),
        P(None, ("dp", "expert"), None),
        P(None, ("dp", "expert"), None),
        P(("dp", "expert")),
        P(("dp", "expert"), None),
        P(("dp", "expert"), None),
        P(("dp", "expert")),
        P(("dp", "expert"), None),
        P("expert", "dp", None),
        P("expert", "dp", None),
    )
    return jax.shard_map(
        per_device,
        mesh=mesh,
        in_specs=placed,
        out_specs=(
            P(None, ("dp", "expert"), None),
            P(None, ("dp", "expert"), None),
            P(("dp", "expert")),
            P(("dp", "expert"), None),
            P(("dp", "expert"), None),
            P(("dp", "expert")),
            P(("dp", "expert"), None),
            P("expert", "dp", None),
            P("expert", "dp", None),
        ),
        check_vma=False,
    )
```

profile of v0, /device:TPU:11, one launch (start us, length us, event | category | flops | bytes accessed | tf_op | source)
XLA Modules:
  0.0 1641.5 jit_solution(18050383298706318492)
XLA Ops:
  12.5 39.9 %all-reduce.5 = (bf16[1536]{0:T(1024)(128)(2,1)S(1)}, bf16[1536]{0:T(1024)(128)(2,1)S(1)}) all-reduce(bf16[1536]{0:T(1024)(128)(2,1)S(1)} %dynamic-update-slice, bf16[1536]{0:T(1024)(128)(2,1)S(1)} %dynamic-update-slice.1), channel_id=1, replica_groups=mesh['dp'=4,'expert'=8] {'dp','expert'}, use_global_device_ids=true, to_apply=%add | all-reduce | flops 3072 | bytes 12288
  55.4 32.6 %all-gather.6.cloned.1.call-done = bf16[1536,2560]{1,0:T(8,128)(2,1)} async-done(((bf16[48,2560]{1,0:T(8,128)(2,1)}), bf16[1536,2560]{1,0:T(8,128)(2,1)}) %all-gather.6.cloned.1.call-update) | async-done | bytes 7864336 | tf_op jit(solution)/shard_map/all_gather | solution.py:71
  88.0 4.7 fusion.174
  97.5 56.1 %all-gather.8.cloned.1.call-done = bf16[1536,1536]{1,0:T(8,128)(2,1)} async-done(((bf16[48,1536]{1,0:T(8,128)(2,1)}), bf16[1536,1536]{1,0:T(8,128)(2,1)}) %all-gather.8.cloned.1.call-update) | async-done | bytes 4718608 | tf_op jit(solution)/shard_map/all_gather | solution.py:72
  153.6 3.4 multiply_reduce_fusion.7
  157.9 4.7 scatter_custom_fusion
  162.6 15.9 all-to-all-start
  178.5 138.7 %all-gather.10.cloned.1.call-done = bf16[3,1536,1024]{2,1,0:T(8,128)(2,1)} async-done(((bf16[3,384,1024]{2,1,0:T(8,128)(2,1)}), bf16[3,1536,1024]{2,1,0:T(8,128)(2,1)}) %all-gather.10.cloned.1.call-update) | async-done | bytes 9437200 | tf_op jit(solution)/shard_map/all_gather | solution.py:80
  317.2 5.9 fusion.49
  325.3 81.2 %all-gather.12.cloned.1.call-done = bf16[3,512,1536]{2,1,0:T(8,128)(2,1)} async-done(((bf16[3,128,1536]{2,1,0:T(8,128)(2,1)}), bf16[3,512,1536]{2,1,0:T(8,128)(2,1)}) %all-gather.12.cloned.1.call-update) | async-done | bytes 4718608 | tf_op jit(solution)/shard_map/all_gather | solution.py:81
  406.5 3.7 fusion.33
  411.8 4.5 all-to-all-start.1
  416.3 54.2 %all-gather = bf16[32,48,24]{1,2,0:T(8,128)(2,1)S(1)} all-gather(bf16[1,48,24]{1,2,0:T(8,128)(2,1)} %bitcast.410), channel_id=1, replica_groups=mesh['dp'=4,'expert'=8] {'dp','expert'}, dimensions={0}, use_global_device_ids=true | all-gather | bytes 76032 | tf_op jit(solution)/shard_map/all_gather | solution.py:74
  487.6 4.9 scatter_custom_fusion.2
  492.4 6.5 all-to-all-start.4
  501.6 4.7 fusion.171
  510.8 16.1 all-to-all-done.4
  527.0 5.6 fusion.69
  532.6 10.8 fusion.39
  545.0 5.6 all-to-all-start.5
  556.2 4.3 multiply_reduce_fusion.6
  561.6 16.8 %all-to-all-done.5 = bf16[8,3,32,1536]{3,2,1,0:T(8,128)(2,1)S(1)} async-done(((bf16[8,3,32,1536]{3,2,1,0:T(8,128)(2,1)}), bf16[8,3,32,1536]{3,2,1,0:T(8,128)(2,1)S(1)}, u32[]{:S(2)}, u32[]{:S(2)}) %all-to-all-start.5) | async-done | bytes 2359328 | tf_op jit(solution)/shard_map/all_to_all | solution.py:270
  586.9 4.1 scatter_custom_fusion.1
  591.0 32.0 %all_to_all.40 = bf16[8,3,32,1536]{3,2,1,0:T(8,128)(2,1)S(1)} all-to-all(bf16[8,3,32,1536]{3,2,1,0:T(8,128)(2,1)S(1)} %bitcast.385), channel_id=1, replica_groups=mesh['dp'=4,'expert'=8] {'expert'}, dimensions={0} | all-to-all | bytes 4718592 | tf_op jit(solution)/shard_map/all_to_all | solution.py:160
  623.1 6.0 fusion.54
  632.7 5.4 all-to-all-start.3
  644.4 21.5 %all-to-all-done.3 = bf16[8,3,32,1536]{3,2,1,0:T(8,128)(2,1)S(1)} async-done(((bf16[8,3,32,1536]{3,2,1,0:T(8,128)(2,1)}), bf16[8,3,32,1536]{3,2,1,0:T(8,128)(2,1)S(1)}, u32[]{:S(2)}, u32[]{:S(2)}) %all-to-all-start.3) | async-done | bytes 2359328 | tf_op jit(solution)/shard_map/all_to_all | solution.py:166
  672.8 4.2 scatter_custom_fusion.3
  677.1 32.2 %all_to_all.41 = bf16[8,3,32,1536]{3,2,1,0:T(8,128)(2,1)S(1)} all-to-all(bf16[8,3,32,1536]{3,2,1,0:T(8,128)(2,1)S(1)} %bitcast.384), channel_id=1, replica_groups=mesh['dp'=4,'expert'=8] {'expert'}, dimensions={0} | all-to-all | bytes 4718592 | tf_op jit(solution)/shard_map/all_to_all | solution.py:251
  709.3 5.0 fusion.65
  718.9 5.2 all-to-all-start.7
  727.2 3.6 fusion.79
  739.5 3.6 fusion.73
  743.0 8.9 all-to-all-done.7
  762.2 5.0 convolution_add_fusion.1
  771.7 5.1 bitcast_add_fusion.1
  778.2 4.0 convolution_convert_fusion
  783.4 4.5 convolution_convert_fusion.1
  809.0 7.8 convolution_add_fusion
  817.0 11.3 fusion.84
  828.3 16.2 bitcast_add_fusion
  846.1 5.7 fusion.148
  851.8 6.3 fusion.128
  858.1 44.4 %all-reduce.4 = (f32[1536]{0:T(1024)S(1)}, f32[1536]{0:T(1024)S(1)}) all-reduce(f32[1536]{0:T(1024)S(1)} %add.251, f32[1536]{0:T(1024)S(1)} %add.254), channel_id=9, replica_groups=mesh['dp'=4,'expert'=8] {'dp','expert'}, use_global_device_ids=true, to_apply=%region_39.40.clone | all-reduce | flops 3072 | bytes 24576
  905.7 71.7 %reduce-scatter.10.cloned.1.call-done = f32[48,1536]{1,0:T(8,128)} async-done(((f32[1536,1536]{1,0:T(8,128)}), f32[48,1536]{1,0:T(8,128)}) %reduce-scatter.10.cloned.1.call-update) | async-done | bytes 294928 | tf_op jit(solution)/shard_map/reduce_scatter | solution.py:89
  977.4 165.3 %reduce-scatter.14.cloned.1.call-done = f32[3,128,1536]{2,1,0:T(8,128)} async-done(((f32[3,512,1536]{2,1,0:T(8,128)}), f32[3,128,1536]{2,1,0:T(8,128)}) %reduce-scatter.14.cloned.1.call-update) | async-done | bytes 2359312 | tf_op jit(solution)/shard_map/reduce_scatter | solution.py:98
  1142.6 177.4 %reduce-scatter.8.cloned.1.call-done = f32[48,2560]{1,0:T(8,128)} async-done(((f32[1536,2560]{1,0:T(8,128)}), f32[48,2560]{1,0:T(8,128)}) %reduce-scatter.8.cloned.1.call-update) | async-done | bytes 491536 | tf_op jit(solution)/shard_map/reduce_scatter | solution.py:88
  1320.0 314.8 %reduce-scatter.12.cloned.1.call-done = f32[3,384,1024]{2,1,0:T(8,128)} async-done(((f32[3,1536,1024]{2,1,0:T(8,128)}), f32[3,384,1024]{2,1,0:T(8,128)}) %reduce-scatter.12.cloned.1.call-update) | async-done | bytes 4718608 | tf_op jit(solution)/shard_map/reduce_scatter | solution.py:97
  (406 shorter events, 133.7 us)
Async XLA Ops:
  7.2 5.0 copy-start.99
  7.2 80.8 %all-gather.6.cloned.1.call-start = ((), (), s32[]{:S(2)}) async-start(), calls=%async_computation.13 | async-start | bytes 8110080 | tf_op jit(solution)/shard_map/all_gather | solution.py:71
  8.0 145.6 %all-gather.8.cloned.1.call-start = ((), (), s32[]{:S(2)}) async-start(), calls=%async_computation.14 | async-start | bytes 4866048 | tf_op jit(solution)/shard_map/all_gather | solution.py:72
  8.7 308.5 %all-gather.10.cloned.1.call-start = ((), (), s32[]{:S(2)}) async-start(), calls=%async_computation.15 | async-start | bytes 11796480 | tf_op jit(solution)/shard_map/all_gather | solution.py:80
  9.4 397.1 %all-gather.12.cloned.1.call-start = ((), (), s32[]{:S(2)}) async-start(), calls=%async_computation.16 | async-start | bytes 5898240 | tf_op jit(solution)/shard_map/all_gather | solution.py:81
  54.5 38.3 %copy-start.82 = (f32[64]{0:T(128)}, f32[64]{0:T(128)S(1)}, u32[]{:S(2)}) copy-start(f32[64]{0:T(128)S(1)} %get-tuple-element.98) | copy-start | bytes 772
  54.6 103.3 %copy-start.86 = (s32[512,1]{0,1:T(1,128)}, s32[512,1]{0,1:T(1,128)S(1)}, u32[]{:S(2)}) copy-start(s32[512,1]{0,1:T(1,128)S(1)} %compare_select_fusion.3) | copy-start | bytes 6148
  55.4 39.3 %copy-start.43 = (f32[64,32]{1,0:T(8,128)}, f32[64,32]{1,0:T(8,128)S(1)}, u32[]{:S(2)}) copy-start(f32[64,32]{1,0:T(8,128)S(1)} %get-tuple-element.74) | copy-start | bytes 24580
  55.4 39.3 %copy-start.45 = (f32[64,32]{1,0:T(8,128)}, f32[64,32]{1,0:T(8,128)S(1)}, u32[]{:S(2)}) copy-start(f32[64,32]{1,0:T(8,128)S(1)} %get-tuple-element.75) | copy-start | bytes 24580
  97.0 60.0 %copy-start.59 = (f32[8,3,64]{2,1,0:T(4,128)}, f32[8,3,64]{2,1,0:T(4,128)S(1)}, u32[]{:S(2)}) copy-start(f32[8,3,64]{2,1,0:T(4,128)S(1)} %get-tuple-element.82) | copy-start | bytes 18436
  97.1 59.8 %copy-start.63 = (f32[8,3,64]{2,1,0:T(4,128)}, f32[8,3,64]{2,1,0:T(4,128)S(1)}, u32[]{:S(2)}) copy-start(f32[8,3,64]{2,1,0:T(4,128)S(1)} %fusion.110) | copy-start | bytes 18436
  97.5 59.5 %copy-start.22 = (bf16[8,64,3,64]{3,1,2,0:T(8,128)(2,1)}, bf16[8,64,3,64]{3,1,2,0:T(8,128)(2,1)S(1)}, u32[]{:S(2)}) copy-start(bf16[8,64,3,64]{3,1,2,0:T(8,128)(2,1)S(1)} %convolution_convert_fusion.3) | copy-start | bytes 589828
  157.0 5.5 copy-start.91
  162.6 154.7 %all-to-all-start = ((bf16[8,3,32,1536]{3,2,1,0:T(8,128)(2,1)}), bf16[8,3,32,1536]{3,2,1,0:T(8,128)(2,1)}, u32[]{:S(2)}, u32[]{:S(2)}) async-start(bf16[8,3,32,1536]{3,2,1,0:T(8,128)(2,1)} %bitcast.16), calls=%async_computation | async-start | bytes 4718592 | tf_op jit(solution)/shard_map/all_to_all | solution.py:160
  325.3 85.0 %copy-start.18 = (bf16[8,3,32,512]{3,2,0,1:T(8,128)(2,1)}, bf16[8,3,32,512]{3,2,0,1:T(8,128)(2,1)S(1)}, u32[]{:S(2)}) copy-start(bf16[8,3,32,512]{3,2,0,1:T(8,128)(2,1)S(1)} %multiply_convert_fusion.1) | copy-start | bytes 2359300
  411.8 69.4 %all-to-all-start.1 = ((bf16[8,3,32,1536]{3,2,1,0:T(8,128)(2,1)}), bf16[8,3,32,1536]{3,2,1,0:T(8,128)(2,1)S(1)}, u32[]{:S(2)}, u32[]{:S(2)}) async-start(bf16[8,3,32,1536]{3,2,1,0:T(8,128)(2,1)} %copy.188), calls=%async_computation.1 | async-start | bytes 4718592 | tf_op jit(solution)/shard_map/all_to_all | solution.py:166
  487.4 5.1 copy-start.67
  492.4 6.6 copy-start.85
  492.4 6.8 copy-start.84
  492.4 9.2 copy-start.80
  492.4 34.5 %all-to-all-start.4 = ((bf16[8,3,32,1536]{3,2,1,0:T(8,128)(2,1)}), bf16[8,3,32,1536]{3,2,1,0:T(8,128)(2,1)}, u32[]{:S(2)}, u32[]{:S(2)}) async-start(bf16[8,3,32,1536]{3,2,1,0:T(8,128)(2,1)} %bitcast.55), calls=%async_computation.4 | async-start | bytes 4718592 | tf_op jit(solution)/shard_map/all_to_all | solution.py:251
  532.6 10.8 copy-start.100
  532.6 10.8 copy-start.101
  545.0 33.4 %all-to-all-start.5 = ((bf16[8,3,32,1536]{3,2,1,0:T(8,128)(2,1)}), bf16[8,3,32,1536]{3,2,1,0:T(8,128)(2,1)S(1)}, u32[]{:S(2)}, u32[]{:S(2)}) async-start(bf16[8,3,32,1536]{3,2,1,0:T(8,128)(2,1)} %copy.203), calls=%async_computation.5 | async-start | bytes 4718592 | tf_op jit(solution)/shard_map/all_to_all | solution.py:270
  556.1 4.9 copy-start.68
  556.2 4.8 copy-start.74
  556.2 4.8 copy-start.93
  556.2 4.8 copy-start.76
  591.0 38.6 %slice-start = ((s8[4718592]{0:T(1024)(128)(4,1)}), s8[4194304]{0:T(1024)(128)(4,1)S(1)}, s32[]{:S(2)}) async-start(s8[4718592]{0:T(1024)(128)(4,1)} %bitcast.382), calls=%async_computation.22 | async-start | bytes 8388608
  623.1 6.1 copy-start.24
  623.1 6.6 slice-start.1
  632.7 33.3 %all-to-all-start.3 = ((bf16[8,3,32,1536]{3,2,1,0:T(8,128)(2,1)}), bf16[8,3,32,1536]{3,2,1,0:T(8,128)(2,1)S(1)}, u32[]{:S(2)}, u32[]{:S(2)}) async-start(bf16[8,3,32,1536]{3,2,1,0:T(8,128)(2,1)} %copy.200), calls=%async_computation.3 | async-start | bytes 4718592 | tf_op jit(solution)/shard_map/all_to_all | solution.py:166
  677.1 32.2 %copy-start.16 = (f32[8,3,32,1024]{3,2,0,1:T(8,128)S(1)}, f32[8,3,32,1024]{3,2,0,1:T(8,128)}, u32[]{:S(2)}) copy-start(f32[8,3,32,1024]{3,2,0,1:T(8,128)} %copy-done.15) | copy-start | bytes 9437188
  677.1 37.2 %slice-start.2 = ((s8[9437184]{0:T(1024)(128)(4,1)}), s8[4194304]{0:T(1024)(128)(4,1)S(1)}, s32[]{:S(2)}) async-start(s8[9437184]{0:T(1024)(128)(4,1)} %bitcast.411), calls=%async_computation.24 | async-start | bytes 8388608
  709.3 5.0 copy-start.26
  709.3 5.1 slice-start.3
  709.3 5.1 slice-start.4
  718.9 33.1 %all-to-all-start.7 = ((bf16[8,3,32,1536]{3,2,1,0:T(8,128)(2,1)}), bf16[8,3,32,1536]{3,2,1,0:T(8,128)(2,1)S(1)}, u32[]{:S(2)}, u32[]{:S(2)}) async-start(bf16[8,3,32,1536]{3,2,1,0:T(8,128)(2,1)} %copy.219), calls=%async_computation.7 | async-start | bytes 4718592 | tf_op jit(solution)/shard_map/all_to_all | solution.py:270
  724.1 120.5 %reduce-scatter.16.cloned.1.call-start = ((), (), s32[]{:S(2)}) async-start(), calls=%async_computation.21 | async-start | bytes 811008
  739.2 238.2 %reduce-scatter.10.cloned.1.call-start = ((), (), s32[]{:S(2)}) async-start(), calls=%async_computation.18 | async-start | bytes 9732096 | tf_op jit(solution)/shard_map/reduce_scatter | solution.py:89
  767.3 375.3 %reduce-scatter.14.cloned.1.call-start = ((), (), s32[]{:S(2)}) async-start(), calls=%async_computation.20 | async-start | bytes 11796480 | tf_op jit(solution)/shard_map/reduce_scatter | solution.py:98
  776.8 543.2 %reduce-scatter.8.cloned.1.call-start = ((), (), s32[]{:S(2)}) async-start(), calls=%async_computation.17 | async-start | bytes 16220160 | tf_op jit(solution)/shard_map/reduce_scatter | solution.py:88
  816.8 818.0 %reduce-scatter.12.cloned.1.call-start = ((), (), s32[]{:S(2)}) async-start(), calls=%async_computation.19 | async-start | bytes 23592960 | tf_op jit(solution)/shard_map/reduce_scatter | solution.py:97
  817.0 11.4 copy-start.25
  846.0 5.8 copy-start.50
  846.0 5.8 copy-start.52
  851.8 51.9 %copy-start.47 = (bf16[1,64,1536]{2,1,0:T(8,128)(2,1)S(1)}, bf16[1,64,1536]{2,1,0:T(8,128)(2,1)}, u32[]{:S(2)}) copy-start(bf16[1,64,1536]{2,1,0:T(8,128)(2,1)} %get-tuple-element.53) | copy-start | bytes 589828
  851.8 51.8 %copy-start.48 = (bf16[1,64,1536]{2,1,0:T(8,128)(2,1)S(1)}, bf16[1,64,1536]{2,1,0:T(8,128)(2,1)}, u32[]{:S(2)}) copy-start(bf16[1,64,1536]{2,1,0:T(8,128)(2,1)} %get-tuple-element.54) | copy-start | bytes 589828
  (76 other events, 197.8 us)
Sparse Core Ops, SparseCore 0:
  11.0 77.0 all-gather.5
  90.9 62.5 all-gather.7
  155.1 162.0 all-gather.9
  318.7 87.8 all-gather.11
  739.3 97.2 reduce-scatter.15
  842.9 134.4 reduce-scatter.9
  980.4 162.1 reduce-scatter.13
  1150.2 169.7 reduce-scatter.7
  1323.1 311.7 reduce-scatter.11
where the time goes:
time: 1660 us; the launch traced here: 1640 us
  waiting for transfers between devices  1100 us (66%)
  blocking collectives  203 us (12%)
  matrix products  163 us (10%)
  local copies, waits for them, and re-layouts  60.9 us (4%)
  other arithmetic  51.6 us (3%)
  starting transfers between devices  44.3 us (3%)
    reduce_scatter x1, waiting for transfers between devices, expert_reduce(): lax.psum_scatter(grad_set[0], 'dp', scatter_dimension=1, tiled=True)  315 us
    reduce_scatter x1, waiting for transfers between devices, dense_reduce(): lax.psum_scatter(grad_set[1], ('dp', 'expert'), scatter_dimension=0, tile...  177 us
    reduce_scatter x1, waiting for transfers between devices, expert_reduce(): lax.psum_scatter(grad_set[1], 'dp', scatter_dimension=1, tiled=True)  165 us
    all_gather x1, waiting for transfers between devices, expert_fetch(): lax.all_gather(expert_in, 'dp', axis=1, tiled=True)  139 us
    unnamed x2, blocking collectives  84.2 us
    all_gather x1, waiting for transfers between devices, expert_fetch(): lax.all_gather(expert_out, 'dp', axis=1, tiled=True)  81.2 us
    reduce_scatter x1, waiting for transfers between devices, dense_reduce(): lax.psum_scatter(grad_set[2], ('dp', 'expert'), scatter_dimension=0, tile...  71.7 us
    all_gather x1, waiting for transfers between devices, dense_fetch(): lax.all_gather(attn_out, ('dp', 'expert'), axis=0, tiled=True)  56.1 us
  transfers between devices with their start and end apart: 15, of which 12 were waited for; matrix products, arithmetic and copies ran while one was open for 12% of the time, Pallas kernels for 0%

commit v1 on v0

--- a/solution.py
+++ b/solution.py
@@ -1,7 +1,13 @@
+import functools
+
 import jax
 import jax.numpy as jnp
 from jax import lax
+from jax.experimental import pallas as pl
+from jax.experimental.pallas import tpu as pltpu
 from jax.sharding import PartitionSpec as P
+
+MESH = pl.DeviceIdType.MESH
 
 D = 1536
 HEADS = 24
@@ -401,6 +407,506 @@
     )
 
 
+def gather_kernel(n, by_rows, in_ref, out_ref, local_sem, send_sem, recv_z, recv_x, recv_y, recv_d, recv_s):
+    d = lax.axis_index("dp"); e = lax.axis_index("expert")
+    c = lax.rem(e, 2); x = lax.rem(lax.div(e, 2), 2); y = lax.div(e, 4)
+    sib = e + 1 - 2 * c
+    ex = e + 2 - 4 * x
+    ey = e + 4 - 8 * y
+    exy = ex + 4 - 8 * y
+    rows, cols = in_ref.shape
+    F = (pl.ds(0, rows), pl.ds(0, cols))
+    if by_rows:
+        A = (pl.ds(0, rows // 2), F[1]); B = (pl.ds(rows // 2, rows - rows // 2), F[1])
+    else:
+        ca = (cols // 128 + 1) // 2 * 128
+        A = (F[0], pl.ds(0, ca)); B = (F[0], pl.ds(ca, cols - ca))
+    barrier = pltpu.get_barrier_semaphore()
+    for dev in ((d, sib), (d, ex), (d, ey)):
+        pl.semaphore_signal(barrier, inc=1, device_id=dev, device_id_type=MESH)
+    @pl.when(d > 0)
+    def _():
+        pl.semaphore_signal(barrier, inc=1, device_id=(d - 1, e), device_id_type=MESH)
+    @pl.when(d < n - 1)
+    def _():
+        pl.semaphore_signal(barrier, inc=1, device_id=(d + 1, e), device_id_type=MESH)
+    pl.semaphore_wait(barrier, 3 + jnp.minimum(d, 1) + jnp.minimum(n - 1 - d, 1))
+
+    def copy(zz, ee, rows, dev, slot, sem, own=None):
+        dst = out_ref.at[zz * 8 + ee].at[rows]
+        src = dst if own is None else own.at[rows]
+        return pltpu.make_async_remote_copy(src, dst, send_sem.at[zz, slot], sem,
+            device_id=dev, device_id_type=MESH)
+
+    def column(zz, own=None):
+        copy(zz, e, F, (d, ex), 2, recv_x.at[zz], own).start()
+        copy(zz, e, F, (d, ey), 3, recv_y.at[zz], own).start()
+        copy(zz, e, F, (d, sib), 4, recv_s.at[zz, 0], own).start()
+
+    def down(zz, own=None):
+        return copy(zz, e, F, (d - 1, e), 0, recv_z.at[zz], own)
+    def up(zz, own=None):
+        return copy(zz, e, F, (d + 1, e), 1, recv_z.at[zz], own)
+
+    def plane(zz):
+        copy(zz, ex, F, (d, ex), 2, recv_x.at[zz]).wait_recv()
+        copy(zz, ex, A, (d, ey), 5, recv_d.at[zz, 0]).start()
+        copy(zz, ex, F, (d, sib), 6, recv_s.at[zz, 1]).start()
+        copy(zz, ey, F, (d, ey), 3, recv_y.at[zz]).wait_recv()
+        copy(zz, ey, B, (d, ex), 7, recv_d.at[zz, 1]).start()
+        copy(zz, ey, F, (d, sib), 8, recv_s.at[zz, 2]).start()
+
+    def diag(zz):
+        copy(zz, exy, A, (d, ey), 5, recv_d.at[zz, 0]).wait_recv()
+        copy(zz, exy, A, (d, sib), 9, recv_s.at[zz, 3]).start()
+        copy(zz, exy, B, (d, ex), 7, recv_d.at[zz, 1]).wait_recv()
+        copy(zz, exy, B, (d, sib), 10, recv_s.at[zz, 4]).start()
+
+    own_copy = pltpu.make_async_copy(in_ref, out_ref.at[d * 8 + e], local_sem)
+    @pl.when(d > 0)
+    def _(): down(d, in_ref).start()
+    @pl.when(d < n - 1)
+    def _(): up(d, in_ref).start()
+    column(d, in_ref)
+    own_copy.start()
+
+    def each(k, fn):
+        if k < 0 or k > n - 1: return
+        if k == 0:
+            fn(d, 0); return
+        @pl.when(d - k >= 0)
+        def _(): fn(d - k, -1)
+        @pl.when(d + k <= n - 1)
+        def _(): fn(d + k, 1)
+
+    def first(zz, sign):
+        if sign == -1:
+            up(zz).wait_recv()
+            @pl.when(d < n - 1)
+            def _(): up(zz).start()
+        else:
+            down(zz).wait_recv()
+            @pl.when(d > 0)
+            def _(): down(zz).start()
+        column(zz)
+
+    for k in range(1, n + 2):
+        each(k, first)
+        each(k - 1, lambda zz, s: plane(zz))
+        each(k - 2, lambda zz, s: diag(zz))
+
+    own_copy.wait()
+    es = sib; exs = sib + 2 - 4 * x; eys = sib + 4 - 8 * y; exys = exs + 4 - 8 * y
+    for zz in range(n):
+        copy(zz, es, F, (d, sib), 4, recv_s.at[zz, 0]).wait_recv()
+        copy(zz, exs, F, (d, sib), 6, recv_s.at[zz, 1]).wait_recv()
+        copy(zz, eys, F, (d, sib), 8, recv_s.at[zz, 2]).wait_recv()
+        copy(zz, exys, A, (d, sib), 9, recv_s.at[zz, 3]).wait_recv()
+        copy(zz, exys, B, (d, sib), 10, recv_s.at[zz, 4]).wait_recv()
+        for slot, rows in ((2, F), (3, F), (4, F), (5, A), (6, F), (7, B), (8, F), (9, A), (10, B)):
+            copy(zz, e, rows, (d, sib), slot, recv_s.at[zz, 0]).wait_send()
+        @pl.when((d > 0) & (zz >= d))
+        def _(): down(zz).wait_send()
+        @pl.when((d < n - 1) & (zz <= d))
+        def _(): up(zz).wait_send()
+
+def all_gather(block, n, cid, by_rows, space=pl.ANY):
+    R, C = block.shape
+    D = pltpu.SemaphoreType.DMA
+    return pl.pallas_call(
+        functools.partial(gather_kernel, n, by_rows),
+        out_shape=jax.ShapeDtypeStruct((n * 8, R, C), block.dtype),
+        in_specs=[pl.BlockSpec(memory_space=space)],
+        out_specs=pl.BlockSpec(memory_space=space),
+        scratch_shapes=[D, D((n, 11)), D((n,)), D((n,)), D((n,)), D((n, 2)), D((n, 5))],
+        compiler_params=pltpu.CompilerParams(collective_id=cid, has_side_effects=True, vmem_limit_bytes=60 << 20),
+        name="gather_blocks",
+    )(block)
+
+
+def reduce_kernel(n, by_rows, in_ref, out_ref, acc, rc, rx1, ry1, ry2, rx2, rdn, rup,
+                  loc_sem, ss_c, sr_c, ss_1, sr_x1, sr_y1, ss_2, sr_y2, sr_x2, ss_z, sr_dn, sr_up):
+    d = lax.axis_index("dp"); e = lax.axis_index("expert")
+    c = lax.rem(e, 2); x = lax.rem(lax.div(e, 2), 2); y = lax.div(e, 4)
+    sib = (d, e + 1 - 2 * c); nx = (d, e + 2 - 4 * x); ny = (d, e + 4 - 8 * y)
+    rows, cols = in_ref.shape[1:]
+    if by_rows:
+        ca = rows // 2
+        A = (pl.ds(0, ca), pl.ds(0, cols)); B = (pl.ds(ca, rows - ca), pl.ds(0, cols))
+        sa, sb = (ca, cols), (rows - ca, cols)
+    else:
+        ca = (cols // 128 + 1) // 2 * 128
+        A = (pl.ds(0, rows), pl.ds(0, ca)); B = (pl.ds(0, rows), pl.ds(ca, cols - ca))
+        sa, sb = (rows, ca), (rows, cols - ca)
+    barrier = pltpu.get_barrier_semaphore()
+    for dev in (sib, nx, ny):
+        pl.semaphore_signal(barrier, inc=1, device_id=dev, device_id_type=MESH)
+    @pl.when(d > 0)
+    def _():
+        pl.semaphore_signal(barrier, inc=1, device_id=(d - 1, e), device_id_type=MESH)
+    @pl.when(d < n - 1)
+    def _():
+        pl.semaphore_signal(barrier, inc=1, device_id=(d + 1, e), device_id_type=MESH)
+    pl.semaphore_wait(barrier, 3 + jnp.minimum(d, 1) + jnp.minimum(n - 1 - d, 1))
+
+    low = d < n - d
+    m = jnp.where(low, d, n - 1 - d)
+    def target(i):
+        t = jnp.where(i < n - 1 - m, n - 1 - i, jnp.where(i < n - 1, i - (n - 1 - m), m))
+        return jnp.where(low, t, n - 1 - t)
+
+    def rcopy(src, dst, ss, rs, dev):
+        return pltpu.make_async_remote_copy(src, dst, ss, rs, device_id=dev, device_id_type=MESH)
+
+    def add(dst, src, shape):
+        step = 16
+        @pl.loop(0, shape[0] // step)
+        def _(r):
+            w = pl.ds(pl.multiple_of(r * step, step), step)
+            dst[w, :] = (dst[w, :].astype(jnp.float32) + src[w, :].astype(jnp.float32)).astype(jnp.bfloat16)
+
+    def core_copy(zz, yy, xx):
+        b = zz * 8 + yy * 4 + xx * 2
+        return (rcopy(in_ref.at[b + 1 - c], rc.at[zz, yy, xx], ss_c.at[zz, yy, xx], sr_c.at[zz, yy, xx], sib),
+                pltpu.make_async_copy(in_ref.at[b + c], acc.at[zz, yy, xx], loc_sem.at[zz, yy, xx]))
+    def x1(zz, yy):
+        return rcopy(acc.at[zz, yy, 1 - x].at[A], rx1.at[zz, yy], ss_1.at[zz, yy], sr_x1.at[zz, yy], nx)
+    def y1(zz, xx):
+        return rcopy(acc.at[zz, 1 - y, xx].at[B], ry1.at[zz, xx], ss_1.at[zz, 2 + xx], sr_y1.at[zz, xx], ny)
+    def y2(zz):
+        return rcopy(acc.at[zz, 1 - y, x].at[A], ry2.at[zz], ss_2.at[zz, 0], sr_y2.at[zz], ny)
+    def x2(zz):
+        return rcopy(acc.at[zz, y, 1 - x].at[B], rx2.at[zz], ss_2.at[zz, 1], sr_x2.at[zz], nx)
+    def dn(zz):
+        return rcopy(acc.at[zz, y, x], rdn.at[zz], ss_z.at[zz], sr_dn.at[zz], (d - 1, e))
+    def up(zz):
+        return rcopy(acc.at[zz, y, x], rup.at[zz], ss_z.at[zz], sr_up.at[zz], (d + 1, e))
+
+    def s0(zz):
+        for yy in range(2):
+            for xx in range(2):
+                r, l = core_copy(zz, yy, xx)
+                r.start(); l.start()
+    def s1(zz):
+        for yy in range(2):
+            for xx in range(2):
+                r, l = core_copy(zz, yy, xx)
+                l.wait(); r.wait_recv()
+                add(acc.at[zz, yy, xx], rc.at[zz, yy, xx], (rows, cols))
+        for k in range(2):
+            x1(zz, k).start(); y1(zz, k).start()
+    def s2(zz):
+        for k in (1, 0):
+            yy = jnp.where(k == 1, 1 - y, y); xx = jnp.where(k == 1, 1 - x, x)
+            x1(zz, yy).wait_recv()
+            add(acc.at[zz, yy, x].at[A], rx1.at[zz, yy], sa)
+            if k == 1: y2(zz).start()
+            y1(zz, xx).wait_recv()
+            add(acc.at[zz, y, xx].at[B], ry1.at[zz, xx], sb)
+            if k == 1: x2(zz).start()
+    def s3(zz, last):
+        y2(zz).wait_recv()
+        add(acc.at[zz, y, x].at[A], ry2.at[zz], sa)
+        x2(zz).wait_recv()
+        add(acc.at[zz, y, x].at[B], rx2.at[zz], sb)
+        if not last:
+            @pl.when((zz < d) & (d < n - 1))
+            def _():
+                dn(zz).wait_recv()
+                add(acc.at[zz, y, x], rdn.at[zz], (rows, cols))
+            @pl.when(zz < d)
+            def _(): dn(zz).start()
+            @pl.when((zz > d) & (d > 0))
+            def _():
+                up(zz).wait_recv()
+                add(acc.at[zz, y, x], rup.at[zz], (rows, cols))
+            @pl.when(zz > d)
+            def _(): up(zz).start()
+        else:
+            def store(w): out_ref[w, :] = acc[d, y, x, w, :].astype(jnp.float32)
+            def more(w, src): out_ref[w, :] = out_ref[w, :] + src[d, w, :].astype(jnp.float32)
+            def over(fn):
+                @pl.loop(0, rows // 16)
+                def _(r): fn(pl.ds(pl.multiple_of(r * 16, 16), 16))
+            over(store)
+            @pl.when(d < n - 1)
+            def _():
+                dn(d).wait_recv()
+                over(lambda w: more(w, rdn))
+            @pl.when(d > 0)
+            def _():
+                up(d).wait_recv()
+                over(lambda w: more(w, rup))
+
+    for i in range(n):
+        s0(target(i))
+    for i in range(n + 2):
+        if i < n: s1(target(i))
+        if 0 <= i - 1 < n: s2(target(i - 1))
+        if 0 <= i - 2 < n: s3(target(i - 2), i - 2 == n - 1)
+    for zz in range(n):
+        for yy in range(2):
+            for xx in range(2):
+                core_copy(zz, yy, xx)[0].wait_send()
+        for k in range(2):
+            x1(zz, k).wait_send(); y1(zz, k).wait_send()
+        y2(zz).wait_send(); x2(zz).wait_send()
+        @pl.when(zz < d)
+        def _(): dn(zz).wait_send()
+        @pl.when(zz > d)
+        def _(): up(zz).wait_send()
+
+def reduce_scatter(parts, n, cid, by_rows):
+    _, R, C = parts.shape
+    D = pltpu.SemaphoreType.DMA
+    V = lambda *s: pltpu.VMEM(s, parts.dtype)
+    if by_rows:
+        sa = sb = (R // 2, C)
+    else:
+        ca = (C // 128 + 1) // 2 * 128
+        sa, sb = (R, ca), (R, C - ca)
+    return pl.pallas_call(
+        functools.partial(reduce_kernel, n, by_rows),
+        out_shape=jax.ShapeDtypeStruct((R, C), jnp.float32),
+        in_specs=[pl.BlockSpec(memory_space=pl.ANY)],
+        out_specs=pl.BlockSpec(memory_space=pltpu.VMEM),
+        scratch_shapes=[V(n, 2, 2, R, C), V(n, 2, 2, R, C), V(n, 2, *sa), V(n, 2, *sb), V(n, *sa), V(n, *sb), V(n, R, C), V(n, R, C),
+                        D((n, 2, 2)), D((n, 2, 2)), D((n, 2, 2)), D((n, 4)), D((n, 2)), D((n, 2)), D((n, 2)), D((n,)), D((n,)), D((n,)), D((n,)), D((n,))],
+        compiler_params=pltpu.CompilerParams(collective_id=cid, has_side_effects=True, vmem_limit_bytes=60 << 20),
+        name="reduce_blocks",
+    )(parts)
+
+
+def moe_kernel(x_ref, cot_ref, up_ref, upt_ref, down_ref, downt_ref, pick_ref, place_ref,
+               out_ref, gx_ref, gup_ref, gdown_ref, acc_up, acc_down):
+    step = pl.program_id(0)
+    f = down_ref.shape[0]
+    x = x_ref[:, :, :D].reshape(-1, D)
+    gate_cols = x_ref[:, :, D:].reshape(x.shape[0], -1)
+    cot = cot_ref[...].reshape(-1, D)
+    f32 = jnp.float32
+    mix = jnp.dot(gate_cols, pick_ref[...], preferred_element_type=f32)
+    gate_up = jnp.dot(x, up_ref[...], preferred_element_type=f32)
+    back = jnp.dot(cot, downt_ref[...], preferred_element_type=f32)
+    gate = gate_up[:, :f]
+    up = gate_up[:, f:]
+    sig = 1.0 / (1.0 + jnp.exp(-gate))
+    act = gate * sig
+    hidden = (act * up).astype(jnp.bfloat16).astype(f32)
+    prod = hidden * back
+    high = prod.astype(jnp.bfloat16)
+    low = (prod - high.astype(f32)).astype(jnp.bfloat16)
+    place = place_ref[...]
+    sums = jnp.dot(high, place, preferred_element_type=f32) + jnp.dot(low, place, preferred_element_type=f32)
+    mixed = (mix * hidden).astype(jnp.bfloat16)
+    out_ref[...] = jnp.dot(mixed, down_ref[...], preferred_element_type=f32).astype(jnp.bfloat16).reshape(out_ref.shape)
+    gh = mix * back
+    g_gate = gh * up * sig * (1.0 + gate * (1.0 - sig))
+    g_up = gh * act
+    gg = jnp.concatenate([g_gate, g_up], axis=1).astype(jnp.bfloat16)
+    gx = jnp.dot(gg, upt_ref[...], preferred_element_type=f32).astype(jnp.bfloat16)
+    gx_ref[:, :, :D] = gx.reshape(x_ref.shape[0], x_ref.shape[1], D)
+    gx_ref[:, :, D:] = sums.astype(jnp.bfloat16).reshape(x_ref.shape[0], x_ref.shape[1], -1)
+    t_dims = (((0,), (0,)), ((), ()))
+    d_up = lax.dot_general(gg, x, t_dims, preferred_element_type=f32)
+    d_down = lax.dot_general(mixed, cot, t_dims, preferred_element_type=f32)
+
+    @pl.when(step == 0)
+    def _():
+        acc_up[...] = d_up
+        acc_down[...] = d_down
+
+    @pl.when(step > 0)
+    def _():
+        acc_up[...] += d_up
+        acc_down[...] += d_down
+
+    @pl.when(step == pl.num_programs(0) - 1)
+    def _():
+        n = gup_ref.shape[0]
+        w = D // n
+        for q in range(n):
+            gup_ref[q] = acc_up[:, q * w:(q + 1) * w].astype(jnp.bfloat16)
+        gdown_ref[...] = acc_down[...]
+
+
+def moe_call(x_all, cot_all, up, upt, down, downt, pick, place, n, group):
+    blocks, rows, width = x_all.shape
+    f = down.shape[0]
+    once = dict(pipeline_mode=pl.Buffered(1))
+    full = lambda a: pl.BlockSpec(a.shape, lambda i: (0,) * a.ndim, **once)
+    return pl.pallas_call(
+        moe_kernel,
+        grid=(blocks // group,),
+        out_shape=(
+            jax.ShapeDtypeStruct((blocks, rows, D), jnp.bfloat16),
+            jax.ShapeDtypeStruct((blocks, rows, width), jnp.bfloat16),
+            jax.ShapeDtypeStruct((n, 2 * f, D // n), jnp.bfloat16),
+            jax.ShapeDtypeStruct((f, D), jnp.float32),
+        ),
+        in_specs=[pl.BlockSpec((group, rows, width), lambda i: (i, 0, 0)),
+                  pl.BlockSpec((group, rows, D), lambda i: (i, 0, 0)),
+                  full(up), full(upt), full(down), full(downt), full(pick), full(place)],
+        out_specs=[pl.BlockSpec((group, rows, D), lambda i: (i, 0, 0)),
+                   pl.BlockSpec((group, rows, width), lambda i: (i, 0, 0)),
+                   pl.BlockSpec((n, 2 * f, D // n), lambda i: (0, 0, 0), **once),
+                   pl.BlockSpec((f, D), lambda i: (0, 0), **once)],
+        scratch_shapes=[pltpu.VMEM((2 * f, D), jnp.float32), pltpu.VMEM((f, D), jnp.float32)],
+        compiler_params=pltpu.CompilerParams(vmem_limit_bytes=60 << 20),
+        cost_estimate=pl.CostEstimate(flops=2 * blocks * rows * D * f * 9, bytes_accessed=blocks * rows * D * 8, transcendentals=0),
+        name="expert_layer",
+    )(x_all, cot_all, up, upt, down, downt, pick, place)
+
+
+def attention_forward(tokens, segment, gain, w_in, w_out):
+    row_count = tokens.shape[0]
+    groups = HEADS // KV_HEADS
+    q_width = HEADS * HEAD
+    k_width = KV_HEADS * HEAD
+    inputs = tokens.astype(jnp.float32)
+    inv_first = lax.rsqrt(jnp.mean(inputs * inputs, axis=1, keepdims=True) + norm_eps)
+    normed_first = (inputs * inv_first * gain).astype(jnp.bfloat16)
+    qkv_full = jnp.dot(normed_first, w_in, preferred_element_type=jnp.float32)
+    cosine, sine_table, causal = rope_tables(segment, HEAD // 2)
+    queries = rotate(
+        qkv_full[:, :q_width].reshape(row_count, KV_HEADS, groups, HEAD),
+        cosine[:, None, None, :],
+        sine_table[:, None, None, :],
+    ).astype(jnp.bfloat16)
+    key_rot = rotate(
+        qkv_full[:, q_width : q_width + k_width].reshape(row_count, KV_HEADS, HEAD),
+        cosine[:, None, :],
+        sine_table[:, None, :],
+    ).astype(jnp.bfloat16)
+    values = (
+        qkv_full[:, q_width + k_width :].reshape(row_count, KV_HEADS, HEAD).astype(jnp.bfloat16)
+    )
+    scores = attention_scores(queries, key_rot, causal)
+    probs = jax.nn.softmax(scores, axis=-1)
+    attn_mixed = jnp.einsum(
+        "kgts,skh->tkgh", probs.astype(jnp.bfloat16), values, preferred_element_type=jnp.float32
+    )
+    attn_mixed = attn_mixed.reshape(row_count, q_width).astype(jnp.bfloat16)
+    middle = inputs + jnp.dot(attn_mixed, w_out, preferred_element_type=jnp.float32)
+    return middle, (inputs, inv_first, normed_first, queries, key_rot, values, probs, cosine, sine_table, attn_mixed)
+
+
+def attention_backward(saved, grad_middle, gain, w_in, w_out):
+    inputs, inv_first, normed_first, queries, key_rot, values, probs, cosine, sine_table, attn_mixed = saved
+    row_count = inputs.shape[0]
+    groups = HEADS // KV_HEADS
+    score_scale = HEAD ** (-0.5)
+    f32 = jnp.float32
+    grad_branch = grad_middle.astype(jnp.bfloat16)
+    grad_out = jnp.einsum("tc,td->cd", attn_mixed, grad_branch, preferred_element_type=f32)
+    grad_mixed = jnp.einsum("td,cd->tc", grad_branch, w_out, preferred_element_type=f32)
+    grad_mixed = grad_mixed.astype(jnp.bfloat16).reshape(row_count, KV_HEADS, groups, HEAD)
+    grad_values = jnp.einsum("kgts,tkgh->skh", probs.astype(jnp.bfloat16), grad_mixed, preferred_element_type=f32)
+    grad_probs = jnp.einsum("tkgh,skh->kgts", grad_mixed, values, preferred_element_type=f32)
+    grad_scores = (probs * (grad_probs - jnp.sum(probs * grad_probs, axis=-1, keepdims=True))).astype(jnp.bfloat16)
+    grad_query = jnp.einsum("kgts,skh->tkgh", grad_scores, key_rot, preferred_element_type=f32) * score_scale
+    grad_key = jnp.einsum("kgts,tkgh->skh", grad_scores, queries, preferred_element_type=f32) * score_scale
+    grad_query = unrotate(grad_query, cosine[:, None, None, :], sine_table[:, None, None, :])
+    grad_key = unrotate(grad_key, cosine[:, None, :], sine_table[:, None, :])
+    grad_qkv = jnp.concatenate(
+        [grad_query.reshape(row_count, -1), grad_key.reshape(row_count, -1), grad_values.reshape(row_count, -1)],
+        axis=1,
+    ).astype(jnp.bfloat16)
+    grad_in = jnp.einsum("tc,tq->cq", normed_first, grad_qkv, preferred_element_type=f32)
+    grad_first = jnp.einsum("tq,cq->tc", grad_qkv, w_in, preferred_element_type=f32)
+    unit = inputs * inv_first
+    pull = grad_first * gain
+    grad_gain = jnp.sum(grad_first * unit, axis=0)
+    grad_inputs = grad_middle + inv_first * (pull - unit * jnp.mean(pull * unit, axis=1, keepdims=True))
+    return grad_inputs, grad_gain, grad_in, grad_out
+
+
+def per_device_fast(n, tokens, segments, routes, cotangent, gain_attn, attn_in, attn_out, gain_ffn, router, expert_in, expert_out):
+    f32, bf16 = jnp.float32, jnp.bfloat16
+    micro, rows = tokens.shape[:2]
+    total = micro * rows
+    held = expert_in.shape[0]
+    experts = held * 8
+    f = FF // n
+    shard = attn_in.shape[0]
+    widths = (attn_in.shape[1], attn_out.shape[1], experts, 1, 1)
+    used = sum(widths)
+    wide = (used + 127) // 128 * 128
+    x = tokens.reshape(total, D)
+    cot = cotangent.reshape(total, D)
+
+    dense = jnp.concatenate(
+        [attn_in, attn_out, router, gain_attn[:, None], gain_ffn[:, None], jnp.zeros((shard, wide - used), bf16)], axis=1)
+    dense = all_gather(dense, n, 0, False).reshape(-1, wide)
+    w_in = dense[:, : widths[0]]
+    w_out = dense[:, widths[0] : widths[0] + widths[1]]
+    tail = dense[:, widths[0] + widths[1] :]
+    w_router = tail[:, :experts]
+    gain_first = tail[:, experts].astype(f32)[None, :]
+    gain_second = tail[:, experts + 1].astype(f32)[None, :]
+    cot_all = all_gather(cot, n, 1, True)
+
+    ups = expert_in.reshape(held, D // n, 2, n, f).transpose(3, 1, 2, 0, 4).reshape(n, D // n, 2 * held * f)
+    up = lax.all_to_all(ups, "dp", split_axis=0, concat_axis=0, tiled=True).reshape(D, 2 * held * f)
+    down = expert_out.reshape(held * f, D)
+
+    segment = (segments[:, 0, :] + 2 * rows * jnp.arange(micro, dtype=jnp.int32)[:, None]).reshape(total)
+    middle, saved = attention_forward(x, segment, gain_first, w_in, w_out)
+    inv_second = lax.rsqrt(jnp.mean(middle * middle, axis=1, keepdims=True) + norm_eps)
+    normed_second = (middle * inv_second * gain_second).astype(bf16)
+    logits = jnp.dot(normed_second, w_router, preferred_element_type=f32)
+    route = routes.reshape(total, TOP_K)
+    chosen = jnp.any(route[:, :, None] == jnp.arange(experts, dtype=jnp.int32)[None, None, :], axis=1)
+    masked = jnp.where(chosen, logits, neg_large)
+    raised = jnp.where(chosen, jnp.exp(masked - jnp.max(masked, axis=1, keepdims=True)), 0.0)
+    gates = raised / jnp.sum(raised, axis=1, keepdims=True)
+
+    high = gates.astype(bf16)
+    low = (gates - high.astype(f32)).astype(bf16)
+    x_all = all_gather(
+        jnp.concatenate([normed_second, high, low, jnp.zeros((total, 128 - 2 * experts), bf16)], axis=1), n, 2, True)
+
+    first = lax.axis_index("expert") * held
+    lane = jnp.arange(128, dtype=jnp.int32)[:, None]
+    owner = (first + jnp.arange(held * f, dtype=jnp.int32) // f)[None, :]
+    pick = ((lane == owner) | (lane == owner + experts)).astype(bf16)
+    place = (lane == owner).astype(bf16).T
+    out_parts, grad_parts, grad_up, grad_down = moe_call(x_all, cot_all, up, up.T, down, down.T, pick, place, n, 2)
+
+    moe_sum = reduce_scatter(out_parts, n, 3, True)
+    result = (middle + moe_sum).astype(bf16)
+    grad_sum = reduce_scatter(grad_parts, n, 4, True)
+    grad_up = lax.all_to_all(grad_up, "dp", split_axis=0, concat_axis=0, tiled=True)
+    grad_up = grad_up.reshape(n, 2, held, f, D // n).transpose(2, 4, 1, 0, 3).reshape(held, D // n, 2 * FF).astype(f32)
+
+    upstream = cot.astype(f32)
+    grad_gates = grad_sum[:, D : D + experts]
+    grad_logits = (gates * (grad_gates - jnp.sum(gates * grad_gates, axis=1, keepdims=True))).astype(bf16)
+    grad_router = jnp.einsum("td,te->de", normed_second, grad_logits, preferred_element_type=f32)
+    grad_second = jnp.einsum("te,de->td", grad_logits, w_router, preferred_element_type=f32) + grad_sum[:, :D]
+    unit = middle * inv_second
+    pull = grad_second * gain_second
+    grad_gain_ffn = jnp.sum(grad_second * unit, axis=0)
+    grad_middle = upstream + inv_second * (pull - unit * jnp.mean(pull * unit, axis=1, keepdims=True))
+    grad_inputs, grad_gain_attn, grad_in, grad_out = attention_backward(saved, grad_middle, gain_first, w_in, w_out)
+    parts = jnp.concatenate(
+        [grad_in, grad_out, grad_router, grad_gain_attn[:, None], grad_gain_ffn[:, None], jnp.zeros((D, wide - used), f32)],
+        axis=1).astype(bf16)
+    sums = reduce_scatter(parts.reshape(-1, shard, wide), n, 5, False)
+    a, b = widths[0], widths[0] + widths[1]
+    return (
+        result.reshape(micro, rows, D),
+        grad_inputs.reshape(micro, rows, D),
+        sums[:, b + experts],
+        sums[:, :a],
+        sums[:, a:b],
+        sums[:, b + experts + 1],
+        sums[:, b : b + experts],
+        grad_up,
+        grad_down.reshape(held, f, D),
+    )
+
+
 def solution(mesh):
     placed = (
         P(None, ("dp", "expert"), None),
@@ -415,8 +921,10 @@
         P("expert", "dp", None),
         P("expert", "dp", None),
     )
+    fast = mesh.shape["expert"] == 8 and FF // mesh.shape["dp"] % 128 == 0
+    body = functools.partial(per_device_fast, mesh.shape["dp"]) if fast else per_device
     return jax.shard_map(
-        per_device,
+        body,
         mesh=mesh,
         in_specs=placed,
         out_specs=(

time: 1660 us -> 675 us (0.41)
  waiting for transfers between devices: 1100 us -> 0.01 us
  Pallas kernels: 0 us -> 504 us
  blocking collectives: 203 us -> 0 us
  matrix products: 163 us -> 43.9 us
  starting transfers between devices: 44.3 us -> 10.3 us
  other arithmetic: 51.6 us -> 22.6 us
  local copies, waits for them, and re-layouts: 60.9 us -> 87.6 us
    reduce_scatter x4 -> x0, waiting for transfers between devices: 729 us -> none  [the longest x1 315 us: expert_reduce(): lax.psum_scatter(grad_set[0], 'dp', scatter_dimension=1, tiled=True)]
    pallas_call x0 -> x7, Pallas kernels: none -> 504 us  [the longest x3 227 us: all_gather(): pl.pallas_call(functools.partial(gather_kernel, n, by_rows), out_shape=ja...]
    all_gather x4 -> x0, waiting for transfers between devices: 309 us -> none  [the longest x1 139 us: expert_fetch(): lax.all_gather(expert_in, 'dp', axis=1, tiled=True)]
    dot_general x46 -> x14, matrix products: 163 us -> 41 us  [the longest x1 7.5 us: attention_backward(): jnp.einsum('tq,cq->tc', grad_qkv, w_in, preferred_element_type=f32)]
    unnamed x2 -> x0, blocking collectives: 84.2 us -> none
    all_to_all x2 -> x0, blocking collectives: 64.2 us -> none  [the longest x1 32.2 us: backward_micro(): lax.all_to_all(grad_buffer, 'expert', split_axis=0, concat_axis=0, tiled=...]
    all_to_all x6 -> x2, waiting for transfers between devices: 63.3 us -> 0.01 us  [the longest x1 0.01 us: per_device_fast(): lax.all_to_all(ups, 'dp', split_axis=0, concat_axis=0, tiled=True)]
    all_gather x1 -> x0, blocking collectives: 54.2 us -> none  [dense_fetch(): lax.all_gather(router, ('dp', 'expert'), axis=0, tiled=True)]
  transfers between devices with their start and end apart: 15 -> 2, of which waited for: 12 -> 0; matrix products, arithmetic and copies ran while one was open for 12% -> 16% of each run, Pallas kernels for 0% -> 44%
where the time goes in v1:
time: 675 us; the launch traced here: 669 us
  Pallas kernels  504 us (75%)
  local copies, waits for them, and re-layouts  87.6 us (13%)
  matrix products  43.9 us (7%)
  other arithmetic  22.6 us (3%)
  starting transfers between devices  10.3 us (2%)
    pallas_call x3, Pallas kernels, all_gather(): pl.pallas_call(functools.partial(gather_kernel, n, by_rows), out_shape=ja...  227 us
    pallas_call x3, Pallas kernels, reduce_scatter(): pl.pallas_call(functools.partial(reduce_kernel, n, by_rows), out_shape=ja...  202 us
    pallas_call x1, Pallas kernels, moe_call(): pl.pallas_call(moe_kernel, grid=(blocks // group,), out_shape=(jax.ShapeD...  74 us
    concatenate x3, local copies, waits for them, and re-layouts, per_device_fast(): jnp.concatenate([grad_in, grad_out, grad_router, grad_gain_attn[:, None],...  22.5 us
  transfers between devices with their start and end apart: 2, of which 0 were waited for; matrix products, arithmetic and copies ran while one was open for 16% of the time, Pallas kernels for 44%

profile of v1, /device:TPU:11, one launch (start us, length us, event | category | flops | bytes accessed | tf_op | source)
XLA Modules:
  0.0 669.5 jit_solution(12987468253593695275)
XLA Ops:
  0.6 4.5 reshape.343
  5.2 3.7 copy.117
  8.9 4.9 all-to-all-start
  16.0 99.6 %gather_blocks.3 = bf16[32,48,4224]{2,1,0:T(8,128)(2,1)} custom-call(bf16[48,4224]{1,0:T(8,128)(2,1)} %concatenate.37.in_ref), custom_call_target="tpu_custom_call" | custom-call | tf_op jit(solution)/shard_map/gather_blocks/pallas_call | solution.py:516
  115.6 2.1 fusion.54
  118.5 4.6 fusion.3
  125.4 1.4 copy.110
  131.2 1.8 copy.109
  133.0 1.7 copy.108
  138.1 1.4 compare_and_fusion
  139.5 1.7 subtract_convert_fusion.3
  142.0 2.9 fusion.55
  144.9 1.7 convolution_convert_fusion.3
  146.7 3.4 multiply_reduce_fusion.4
  151.0 1.3 fusion.56
  153.9 1.9 concatenate.40.in_ref
  155.8 68.1 %gather_blocks.4.x_ref = bf16[32,128,1664]{2,1,0:T(8,128)(2,1)} custom-call(bf16[128,1664]{1,0:T(8,128)(2,1)} %concatenate.40.in_ref), custom_call_target="tpu_custom_call" | custom-call | tf_op jit(solution)/shard_map/gather_blocks/pallas_call | solution.py:516
  223.8 2.4 copy.119
  226.2 59.8 %gather_blocks.5.cot_ref = bf16[32,128,1536]{2,1,0:T(8,128)(2,1)} custom-call(bf16[128,1536]{1,0:T(8,128)(2,1)} %bitcast.134), custom_call_target="tpu_custom_call" | custom-call | tf_op jit(solution)/shard_map/gather_blocks/pallas_call | solution.py:516
  286.0 1.9 copy.128
  289.4 1.7 copy.145
  291.1 4.3 copy.120.up_ref
  295.4 74.0 %expert_layer.1 = (bf16[32,128,1536]{2,1,0:T(8,128)(2,1)}, bf16[32,128,1664]{2,1,0:T(8,128)(2,1)}, bf16[4,768,384]{2,1,0:T(8,128)(2,1)}, f32[384,1536]{1,0:T(8,128)}) custom-call(bf16[32,128,1664]{2,1,0:T(8,128)(2,1)} %gather_blocks.4.x_ref, bf16[32,128,1536]{2,1,0:T(8,128)(2,1)} %gather_blocks.5.cot_ref, bf16[1536,768]{1,0:T(8,128)(2,1)} %copy.120.up_ref, ...), custom_call_target="tpu_custom_call" | custom-call | flops 43486543872 | bytes 50331648 | tf_op jit(solution)/shard_map/expert_layer/pallas_call | solution.py:738
  369.4 69.4 %reduce_blocks.4 = f32[128,1664]{1,0:T(8,128)} custom-call(bf16[32,128,1664]{2,1,0:T(8,128)(2,1)} %get-tuple-element.14.in_ref), custom_call_target="tpu_custom_call" | custom-call | tf_op jit(solution)/shard_map/reduce_blocks/pallas_call | solution.py:668
  441.0 2.4 multiply_reduce_fusion
  444.3 65.4 %reduce_blocks.3 = f32[128,1536]{1,0:T(8,128)} custom-call(bf16[32,128,1536]{2,1,0:T(8,128)(2,1)} %get-tuple-element.13.in_ref), custom_call_target="tpu_custom_call" | custom-call | tf_op jit(solution)/shard_map/reduce_blocks/pallas_call | solution.py:668
  509.7 2.2 multiply_add_fusion.1
  512.8 4.1 fusion.12
  519.9 5.4 all-to-all-start.1
  527.4 1.9 copy.125
  529.3 1.5 fusion.22
  532.4 2.0 fusion.23
  535.1 7.5 %multiply_reduce_fusion.1 = (bf16[1536]{0:T(1024)(128)(2,1)S(1)}, f32[128]{0:T(128)}, f32[128,1536]{1,0:T(8,128)}) fusion(bf16[2,64,1536]{2,1,0:T(8,128)(2,1)S(1)} %copy-done.2, f32[128]{0:T(128)} %copy-done.36, f32[1536]{0:T(1024)S(1)} %copy-done.26, bf16[1536,4224]{1,0:T(8,128)(2,1)} %bitcast.126, bf16[128,512]{1,0:T(8,128)(2,1)} %copy.127, ...), kind=kOutput, calls=%fused_computation.35 | convolution fusion | flops 1009973632 | bytes 9709568 | tf_op jit(solution)/shard_map/tq,cq->tc/dot_general | solution.py:816
  542.6 1.5 concatenate.48
  544.0 1.5 concatenate.49
  545.5 4.6 convolution_convert_fusion.1
  550.2 5.2 convolution_convert_fusion
  556.2 19.6 %concatenate.47.in_ref = bf16[32,48,4224]{2,1,0:T(8,128)(2,1)} concatenate(bf16[32,48,2560]{2,1,0:T(8,128)(2,1)} %convolution_convert_fusion, bf16[32,48,1536]{2,1,0:T(8,128)(2,1)} %convolution_convert_fusion.1, bf16[32,48,24]{2,1,0:T(8,128)(2,1)} %bitcast.138, bf16[32,48,1]{2,1,0:T(8,128)(2,1)} %concatenate.48, bf16[32,48,1]{2,1,0:T(8,128)(2,1)} %concatenate.49, ...), dimensions={2} | concatenate | bytes 25952256 | tf_op jit(solution)/shard_map/concatenate | solution.py:892
  575.8 67.5 %reduce_blocks.5 = f32[48,4224]{1,0:T(8,128)} custom-call(bf16[32,48,4224]{2,1,0:T(8,128)(2,1)} %concatenate.47.in_ref), custom_call_target="tpu_custom_call" | custom-call | tf_op jit(solution)/shard_map/reduce_blocks/pallas_call | solution.py:668
  643.4 1.8 slice.93
  645.2 1.7 slice.94
  646.9 1.3 slice.96
  648.2 1.4 copy.133
  649.6 1.5 slice_reduce_fusion
  651.2 2.3 multiply_add_fusion
  653.5 2.8 convert_bitcast_fusion
  656.2 6.7 %copy.132 = f32[3,384,2,4,128]{4,3,2,1,0:T(4,128)} copy(f32[3,384,2,4,128]{1,4,0,2,3:T(8,128)} %convert_bitcast_fusion) | data formatting | bytes 9437184 | tf_op jit(solution)/shard_map/convert_element_type | solution.py:880
  663.0 6.5 reshape.357
  (142 shorter events, 29.8 us)
Async XLA Ops:
  8.9 6.0 copy-start.32
  8.9 6.0 copy-start.39
  8.9 6.2 copy-start.40
  8.9 6.3 copy-start.18
  8.9 6.3 copy-start.19
  8.9 280.6 %all-to-all-start = ((bf16[4,384,768]{1,2,0:T(8,128)(2,1)}), bf16[4,384,768]{1,2,0:T(8,128)(2,1)S(1)}, u32[]{:S(2)}, u32[]{:S(2)}) async-start(bf16[4,384,768]{1,2,0:T(8,128)(2,1)} %bitcast.129), calls=%async_computation | async-start | bytes 4718592 | tf_op jit(solution)/shard_map/all_to_all | solution.py:850
  16.0 102.0 %copy-start.2 = (bf16[2,64,1536]{2,1,0:T(8,128)(2,1)S(1)}, bf16[2,64,1536]{2,1,0:T(8,128)(2,1)}, u32[]{:S(2)}) copy-start(bf16[2,64,1536]{2,1,0:T(8,128)(2,1)} %param.11) | copy-start | bytes 1179652
  118.0 5.0 copy-start.25
  118.3 4.8 copy-start.36
  118.4 4.6 copy-start.8
  123.1 5.6 copy-start.38
  123.1 13.4 %copy-start.31 = (s32[2,64,8]{1,2,0:T(8,128)S(1)}, s32[2,64,8]{1,2,0:T(8,128)}, u32[]{:S(2)}) copy-start(s32[2,64,8]{1,2,0:T(8,128)} %param.13) | copy-start | bytes 12292
  130.6 4.1 copy-start.35
  138.1 3.9 copy-start.13
  142.0 2.9 copy-start.23
  144.9 1.7 copy-start.27
  146.6 3.4 copy-start.14
  146.6 3.4 copy-start.21
  146.7 4.3 copy-start.20
  150.1 3.2 copy-start.33
  150.2 0.7 copy-start.3
  369.4 69.5 %copy-start.10 = (f32[128,24]{1,0:T(8,128)S(1)}, f32[128,24]{1,0:T(8,128)}, u32[]{:S(2)}) copy-start(f32[128,24]{1,0:T(8,128)} %get-tuple-element.61) | copy-start | bytes 36868
  369.4 70.4 %copy-start.4 = (bf16[128,1536]{1,0:T(8,128)(2,1)S(1)}, bf16[128,1536]{1,0:T(8,128)(2,1)}, u32[]{:S(2)}) copy-start(bf16[128,1536]{1,0:T(8,128)(2,1)} %copy-done.3) | copy-start | bytes 1179652
  369.4 71.5 %copy-start.22 = (f32[1536]{0:T(1024)S(1)}, f32[1536]{0:T(1024)}, u32[]{:S(2)}) copy-start(f32[1536]{0:T(1024)} %convert_reduce_fusion) | copy-start | bytes 18436
  369.4 71.5 %copy-start.34 = (f32[128]{0:T(128)S(1)}, f32[128]{0:T(128)}, u32[]{:S(2)}) copy-start(f32[128]{0:T(128)} %copy-done.33) | copy-start | bytes 1540
  444.3 65.4 %copy-start.5 = (bf16[2,64,1536]{2,1,0:T(8,128)(2,1)S(1)}, bf16[2,64,1536]{2,1,0:T(8,128)(2,1)}, u32[]{:S(2)}) copy-start(bf16[2,64,1536]{2,1,0:T(8,128)(2,1)} %param.14) | copy-start | bytes 1179652
  511.9 0.9 copy-start
  512.8 4.4 copy-start.9
  512.8 4.4 copy-start.24
  512.8 4.4 copy-start.28
  517.2 0.8 copy-start.15
  517.2 0.7 copy-start.29
  517.9 0.8 copy-start.16
  517.9 0.9 copy-start.17
  519.9 133.5 %all-to-all-start.1 = ((bf16[4,768,384]{2,1,0:T(8,128)(2,1)}), bf16[4,768,384]{2,1,0:T(8,128)(2,1)S(1)}, u32[]{:S(2)}, u32[]{:S(2)}) async-start(bf16[4,768,384]{2,1,0:T(8,128)(2,1)} %get-tuple-element.15), calls=%async_computation.1 | async-start | bytes 4718592 | tf_op jit(solution)/shard_map/all_to_all | solution.py:879
  532.4 2.7 copy-start.26
  535.1 9.0 %copy-start.30 = (bf16[1536]{0:T(1024)(128)(2,1)S(1)}, bf16[1536]{0:T(1024)(128)(2,1)}, u32[]{:S(2)}) copy-start(bf16[1536]{0:T(1024)(128)(2,1)} %get-tuple-element.53) | copy-start | bytes 9220
  535.1 10.4 %copy-start.1 = (f32[128,1536]{1,0:T(8,128)S(1)}, f32[128,1536]{1,0:T(8,128)}, u32[]{:S(2)}) copy-start(f32[128,1536]{1,0:T(8,128)} %copy-done) | copy-start | bytes 2359300
  545.5 4.7 copy-start.6
  545.5 4.7 copy-start.7
  545.5 4.7 copy-start.11
  545.5 4.7 copy-start.12
  575.8 75.3 %copy-start.41 = (f32[128]{0:T(128)S(1)}, f32[128]{0:T(128)}, u32[]{:S(2)}) copy-start(f32[128]{0:T(128)} %get-tuple-element.56) | copy-start | bytes 1540
  575.8 75.3 %copy-start.37 = (f32[128]{0:T(128)S(1)}, f32[128]{0:T(128)}, u32[]{:S(2)}) copy-start(f32[128]{0:T(128)} %copy-done.36) | copy-start | bytes 1540

commit v2 on v1

--- a/solution.py
+++ b/solution.py
@@ -677,85 +677,530 @@
     )(parts)
 
 
-def moe_kernel(x_ref, cot_ref, up_ref, upt_ref, down_ref, downt_ref, pick_ref, place_ref,
-               out_ref, gx_ref, gup_ref, gdown_ref, acc_up, acc_down):
-    step = pl.program_id(0)
-    f = down_ref.shape[0]
-    x = x_ref[:, :, :D].reshape(-1, D)
-    gate_cols = x_ref[:, :, D:].reshape(x.shape[0], -1)
-    cot = cot_ref[...].reshape(-1, D)
-    f32 = jnp.float32
-    mix = jnp.dot(gate_cols, pick_ref[...], preferred_element_type=f32)
-    gate_up = jnp.dot(x, up_ref[...], preferred_element_type=f32)
-    back = jnp.dot(cot, downt_ref[...], preferred_element_type=f32)
-    gate = gate_up[:, :f]
-    up = gate_up[:, f:]
-    sig = 1.0 / (1.0 + jnp.exp(-gate))
-    act = gate * sig
-    hidden = (act * up).astype(jnp.bfloat16).astype(f32)
-    prod = hidden * back
-    high = prod.astype(jnp.bfloat16)
-    low = (prod - high.astype(f32)).astype(jnp.bfloat16)
-    place = place_ref[...]
-    sums = jnp.dot(high, place, preferred_element_type=f32) + jnp.dot(low, place, preferred_element_type=f32)
-    mixed = (mix * hidden).astype(jnp.bfloat16)
-    out_ref[...] = jnp.dot(mixed, down_ref[...], preferred_element_type=f32).astype(jnp.bfloat16).reshape(out_ref.shape)
-    gh = mix * back
-    g_gate = gh * up * sig * (1.0 + gate * (1.0 - sig))
-    g_up = gh * act
-    gg = jnp.concatenate([g_gate, g_up], axis=1).astype(jnp.bfloat16)
-    gx = jnp.dot(gg, upt_ref[...], preferred_element_type=f32).astype(jnp.bfloat16)
-    gx_ref[:, :, :D] = gx.reshape(x_ref.shape[0], x_ref.shape[1], D)
-    gx_ref[:, :, D:] = sums.astype(jnp.bfloat16).reshape(x_ref.shape[0], x_ref.shape[1], -1)
-    t_dims = (((0,), (0,)), ((), ()))
-    d_up = lax.dot_general(gg, x, t_dims, preferred_element_type=f32)
-    d_down = lax.dot_general(mixed, cot, t_dims, preferred_element_type=f32)
-
-    @pl.when(step == 0)
-    def _():
-        acc_up[...] = d_up
-        acc_down[...] = d_down
-
-    @pl.when(step > 0)
-    def _():
-        acc_up[...] += d_up
-        acc_down[...] += d_down
-
-    @pl.when(step == pl.num_programs(0) - 1)
-    def _():
-        n = gup_ref.shape[0]
-        w = D // n
-        for q in range(n):
-            gup_ref[q] = acc_up[:, q * w:(q + 1) * w].astype(jnp.bfloat16)
-        gdown_ref[...] = acc_down[...]
-
-
-def moe_call(x_all, cot_all, up, upt, down, downt, pick, place, n, group):
-    blocks, rows, width = x_all.shape
-    f = down.shape[0]
-    once = dict(pipeline_mode=pl.Buffered(1))
-    full = lambda a: pl.BlockSpec(a.shape, lambda i: (0,) * a.ndim, **once)
+NN = (((1,), (0,)), ((), ()))
+NT = (((1,), (1,)), ((), ()))
+TN = (((0,), (0,)), ((), ()))
+
+
+def mm(a, b, dims=NN):
+    return lax.dot_general(a, b, dims, preferred_element_type=jnp.float32)
+
+
+class Place:
+    def __init__(self, n):
+        self.n = n
+        d = self.d = lax.axis_index("dp")
+        e = self.e = lax.axis_index("expert")
+        c, x, y = lax.rem(e, 2), lax.rem(lax.div(e, 2), 2), lax.div(e, 4)
+        self.sib = (d, e + 1 - 2 * c)
+        self.nx = (d, e + 2 - 4 * x)
+        self.ny = (d, e + 4 - 8 * y)
+        self.below = (d - 1, e)
+        self.above = (d + 1, e)
+        self.has_below = d > 0
+        self.has_above = d < n - 1
+
+    def meet(self, everyone=False):
+        barrier = pltpu.get_barrier_semaphore()
+        d, n = self.d, self.n
+        if everyone:
+            others = n - 1 + 3
+
+            @pl.loop(1, n)
+            def _(k):
+                pl.semaphore_signal(barrier, inc=1, device_id=(lax.rem(d + k, n), self.e), device_id_type=MESH)
+        else:
+            others = 3 + jnp.minimum(d, 1) + jnp.minimum(n - 1 - d, 1)
+
+            @pl.when(self.has_below)
+            def _():
+                pl.semaphore_signal(barrier, inc=1, device_id=self.below, device_id_type=MESH)
+
+            @pl.when(self.has_above)
+            def _():
+                pl.semaphore_signal(barrier, inc=1, device_id=self.above, device_id_type=MESH)
+
+        for dev in (self.sib, self.nx, self.ny):
+            pl.semaphore_signal(barrier, inc=1, device_id=dev, device_id_type=MESH)
+        pl.semaphore_wait(barrier, others)
+
+    def far(self, i):
+        n, d = self.n, self.d
+        low = d < n - d
+        m = jnp.where(low, d, n - 1 - d)
+        t = jnp.where(i < n - 1 - m, n - 1 - i, jnp.where(i < n - 1, i - (n - 1 - m), m))
+        return jnp.where(low, t, n - 1 - t)
+
+    def near(self, i):
+        return self.far(self.n - 1 - i)
+
+
+def send(src, dst, ss, rs, dev):
+    return pltpu.make_async_remote_copy(src, dst, ss, rs, device_id=dev, device_id_type=MESH)
+
+
+class Gather:
+    def __init__(self, at, own, buf, send_sem, recv_z, recv_x, recv_y, recv_d):
+        self.at, self.own, self.buf = at, own, buf
+        self.ss, self.rz, self.rx, self.ry, self.rd = send_sem, recv_z, recv_x, recv_y, recv_d
+        rows = own.shape[0]
+        self.A, self.B = pl.ds(0, rows // 2), pl.ds(rows // 2, rows // 2)
+
+    def source(self, zz, own):
+        return self.own if own else self.buf.at[zz, 0]
+
+    def down(self, zz, own=False):
+        return send(self.source(zz, own), self.buf.at[zz, 0], self.ss.at[zz, 0], self.rz.at[zz], self.at.below)
+
+    def up(self, zz, own=False):
+        return send(self.source(zz, own), self.buf.at[zz, 0], self.ss.at[zz, 1], self.rz.at[zz], self.at.above)
+
+    def to_x(self, zz, own=False):
+        return send(self.source(zz, own), self.buf.at[zz, 1], self.ss.at[zz, 2], self.rx.at[zz], self.at.nx)
+
+    def to_y(self, zz, own=False):
+        return send(self.source(zz, own), self.buf.at[zz, 2], self.ss.at[zz, 3], self.ry.at[zz], self.at.ny)
+
+    def turn_y(self, zz):
+        return send(self.buf.at[zz, 1, self.A], self.buf.at[zz, 3, self.A], self.ss.at[zz, 4], self.rd.at[zz, 0], self.at.ny)
+
+    def turn_x(self, zz):
+        return send(self.buf.at[zz, 2, self.B], self.buf.at[zz, 3, self.B], self.ss.at[zz, 5], self.rd.at[zz, 1], self.at.nx)
+
+    def begin(self):
+        d = self.at.d
+
+        @pl.when(self.at.has_below)
+        def _():
+            self.down(d, True).start()
+
+        @pl.when(self.at.has_above)
+        def _():
+            self.up(d, True).start()
+
+        self.to_x(d, True).start()
+        self.to_y(d, True).start()
+
+    def column(self, zz):
+        d = self.at.d
+
+        @pl.when(zz < d)
+        def _():
+            self.up(zz).wait_recv()
+
+            @pl.when(self.at.has_above)
+            def _():
+                self.up(zz).start()
+
+        @pl.when(zz > d)
+        def _():
+            self.down(zz).wait_recv()
+
+            @pl.when(self.at.has_below)
+            def _():
+                self.down(zz).start()
+
+        self.to_x(zz).start()
+        self.to_y(zz).start()
+
+    def plane(self, zz):
+        self.to_x(zz).wait_recv()
+        self.turn_y(zz).start()
+        self.to_y(zz).wait_recv()
+        self.turn_x(zz).start()
+
+    def corner(self, zz):
+        self.turn_y(zz).wait_recv()
+        self.turn_x(zz).wait_recv()
+
+    def finish(self):
+        d = self.at.d
+
+        @pl.loop(0, self.at.n)
+        def _(zz):
+            for copy in (self.to_x, self.to_y, self.turn_y, self.turn_x):
+                copy(zz).wait_send()
+
+            @pl.when((d > 0) & (zz >= d))
+            def _():
+                self.down(zz).wait_send()
+
+            @pl.when(self.at.has_above & (zz <= d))
+            def _():
+                self.up(zz).wait_send()
+
+
+def gather_sems(n):
+    D_ = pltpu.SemaphoreType.DMA
+    return [D_((n, 6)), D_((n,)), D_((n,)), D_((n,)), D_((n, 2))]
+
+
+def add_rows(dst, src):
+    rows = dst.shape[0]
+    step = 16
+
+    @pl.loop(0, rows // step)
+    def _(r):
+        w = pl.ds(pl.multiple_of(r * step, step), step)
+        dst[w, :] = (dst[w, :].astype(jnp.float32) + src[w, :].astype(jnp.float32)).astype(dst.dtype)
+
+
+class Reduce:
+    def __init__(self, at, buf, total, r1, r2, rz, ss_1, sr_1, ss_2, sr_2, ss_z, sr_z):
+        self.at, self.buf, self.total = at, buf, total
+        self.r1, self.r2, self.rz = r1, r2, rz
+        self.sems = (ss_1, sr_1, ss_2, sr_2, ss_z, sr_z)
+        rows = total.shape[0]
+        self.A, self.B = pl.ds(0, rows // 2), pl.ds(rows // 2, rows // 2)
+
+    def first(self, zz, k):
+        ss, sr = self.sems[0], self.sems[1]
+        slot, part, dev = ((3, self.A, self.at.nx), (3, self.B, self.at.ny), (1, self.A, self.at.nx), (2, self.B, self.at.ny))[k]
+        return send(self.buf.at[zz, slot, part], self.r1.at[zz, k], ss.at[zz, k], sr.at[zz, k], dev)
+
+    def second(self, zz, k):
+        ss, sr = self.sems[2], self.sems[3]
+        slot, part, dev = ((2, self.A, self.at.ny), (1, self.B, self.at.nx))[k]
+        return send(self.buf.at[zz, slot, part], self.r2.at[zz, k], ss.at[zz, k], sr.at[zz, k], dev)
+
+    def down(self, zz):
+        return send(self.buf.at[zz, 0], self.rz.at[zz], self.sems[4].at[zz], self.sems[5].at[zz], self.at.below)
+
+    def up(self, zz):
+        slot = jnp.where(zz == self.at.d + 1, self.at.n, zz)
+        return send(self.buf.at[zz, 0], self.rz.at[slot], self.sems[4].at[zz], self.sems[5].at[slot], self.at.above)
+
+    def arrive(self, slot):
+        return send(self.buf.at[0, 0], self.rz.at[slot], self.sems[4].at[0], self.sems[5].at[slot], self.at.nx)
+
+    def s1(self, zz):
+        for k in range(4):
+            self.first(zz, k).start()
+
+    def s2(self, zz):
+        self.first(zz, 0).wait_recv()
+        add_rows(self.buf.at[zz, 2, self.A], self.r1.at[zz, 0])
+        self.second(zz, 0).start()
+        self.first(zz, 1).wait_recv()
+        add_rows(self.buf.at[zz, 1, self.B], self.r1.at[zz, 1])
+        self.second(zz, 1).start()
+        self.first(zz, 2).wait_recv()
+        add_rows(self.buf.at[zz, 0, self.A], self.r1.at[zz, 2])
+        self.first(zz, 3).wait_recv()
+        add_rows(self.buf.at[zz, 0, self.B], self.r1.at[zz, 3])
+
+    def s3(self, zz):
+        self.second(zz, 0).wait_recv()
+        add_rows(self.buf.at[zz, 0, self.A], self.r2.at[zz, 0])
+        self.second(zz, 1).wait_recv()
+        add_rows(self.buf.at[zz, 0, self.B], self.r2.at[zz, 1])
+
+    def line(self, zz):
+        d = self.at.d
+
+        @pl.when(((zz < d) & self.at.has_above) | ((zz > d) & self.at.has_below))
+        def _():
+            self.arrive(zz).wait_recv()
+            add_rows(self.buf.at[zz, 0], self.rz.at[zz])
+
+        @pl.when(zz < d)
+        def _():
+            self.down(zz).start()
+
+        @pl.when(zz > d)
+        def _():
+            self.up(zz).start()
+
+    def last(self):
+        d, n, rows, step = self.at.d, self.at.n, self.total.shape[0], 16
+
+        def over(fn):
+            @pl.loop(0, rows // step)
+            def _(r):
+                fn(pl.ds(pl.multiple_of(r * step, step), step))
+
+        def own(w):
+            self.total[w, :] = self.buf[d, 0, w, :].astype(jnp.float32)
+
+        def more(slot):
+            def fn(w):
+                self.total[w, :] += self.rz[slot, w, :].astype(jnp.float32)
+
+            self.arrive(slot).wait_recv()
+            over(fn)
+
+        over(own)
+
+        @pl.when(self.at.has_above)
+        def _():
+            more(d)
+
+        @pl.when(self.at.has_below)
+        def _():
+            more(n)
+
+    def finish(self):
+        d = self.at.d
+
+        @pl.loop(0, self.at.n)
+        def _(zz):
+            for k in range(4):
+                self.first(zz, k).wait_send()
+            for k in range(2):
+                self.second(zz, k).wait_send()
+
+            @pl.when(zz != d)
+            def _():
+                self.arrive(zz)
+                send(self.buf.at[zz, 0], self.rz.at[zz], self.sems[4].at[zz], self.sems[5].at[zz], self.at.nx).wait_send()
+
+
+def reduce_scratch(n, rows, cols):
+    D_ = pltpu.SemaphoreType.DMA
+    V = lambda *s: pltpu.VMEM(s, jnp.bfloat16)
+    return [V(n, 4, rows // 2, cols), V(n, 2, rows // 2, cols), V(n + 1, rows, cols),
+            D_((n, 4)), D_((n, 4)), D_((n, 2)), D_((n, 2)), D_((n,)), D_((n + 1,))]
+
+
+def expert_kernel(n, x_ref, cot_ref, up_ref, down_ref, pick_ref, place_ref,
+                  out_ref, gx_ref, gup_ref, gdown_ref,
+                  xb, cb, gg, mixed, gb, wup, wdown, *rest):
+    f32, bf16 = jnp.float32, jnp.bfloat16
+    at = Place(n)
+    d = at.d
+    gather = Gather(at, x_ref, xb, *rest[:5])
+    grads = Reduce(at, gb, gx_ref, *rest[5:14])
+    outs = Reduce(at, gg, out_ref, *rest[14:23])
+    load_sem, core_ss, core_sr, free, a2a_ss, a2a_sr = rest[23:]
+    rows = x_ref.shape[0]
+    f2 = up_ref.shape[1]
+    f = f2 // 2
+    held = f // 128
+    loads = [
+        pltpu.make_async_copy(x_ref, xb.at[d, 0], load_sem.at[0]),
+        pltpu.make_async_copy(up_ref, wup.at[0], load_sem.at[1]),
+        pltpu.make_async_copy(down_ref, wdown.at[0], load_sem.at[2]),
+        pltpu.make_async_copy(cot_ref, cb, load_sem.at[3]),
+    ]
+    for load in loads:
+        load.start()
+    at.meet(True)
+    gather.begin()
+    swaps = [
+        send(up_ref, wup.at[1], core_ss.at[0], core_sr.at[0], at.sib),
+        send(down_ref, wdown.at[1], core_ss.at[1], core_sr.at[1], at.sib),
+    ]
+    for swap in swaps:
+        swap.start()
+    for load in loads:
+        load.wait()
+    for swap in swaps:
+        swap.wait_recv()
+    gather.plane(at.near(0))
+    gather.column(at.near(1))
+
+    def tokens(ref, zz, p, lo, width):
+        return ref[zz, pl.ds(2 * p, 2), :, pl.ds(lo, width)].reshape(2 * rows, width)
+
+    def half(zz, p):
+        pair = pl.ds(2 * p, 2)
+        x = tokens(xb, zz, p, 0, D)
+        cot = tokens(cb, zz, p, 0, D)
+        mix = mm(tokens(xb, zz, p, D, 128), pick_ref[...])
+        sums = jnp.zeros((2 * rows, 128), f32)
+        for h in range(2):
+            gate_up = mm(x, wup[h])
+            back = mm(cot, wdown[h], NT)
+            for j in range(held):
+                k = h * held + j
+                gate = gate_up[:, j * 256 : j * 256 + 128]
+                up = gate_up[:, j * 256 + 128 : j * 256 + 256]
+                b = back[:, j * 128 : (j + 1) * 128]
+                m = mix[:, k * 128 : (k + 1) * 128]
+                sig = 1.0 / (1.0 + jnp.exp(-gate))
+                act = gate * sig
+                hidden = (act * up).astype(bf16).astype(f32)
+                prod = hidden * b
+                high = prod.astype(bf16)
+                low = (prod - high.astype(f32)).astype(bf16)
+                sel = place_ref[k * 128 : (k + 1) * 128, :]
+                sums += mm(high, sel) + mm(low, sel)
+                mixed[zz, pair, :, pl.ds(k * 128, 128)] = (m * hidden).astype(bf16).reshape(2, rows, 128)
+                gh = m * b
+                gg[zz, pair, :, pl.ds(k * 256, 128)] = (
+                    (gh * up * sig * (1.0 + gate * (1.0 - sig))).astype(bf16).reshape(2, rows, 128))
+                gg[zz, pair, :, pl.ds(k * 256 + 128, 128)] = (gh * act).astype(bf16).reshape(2, rows, 128)
+        for q in range(D // 512):
+            cols = pl.ds(q * 512, 512)
+            part = mm(tokens(gg, zz, p, 0, f2), wup[0, cols, :], NT) + mm(tokens(gg, zz, p, f2, f2), wup[1, cols, :], NT)
+            gb[zz, pair, :, cols] = part.astype(bf16).reshape(2, rows, 512)
+        gb[zz, pair, :, pl.ds(D, 128)] = sums.astype(bf16).reshape(2, rows, 128)
+
+    @pl.loop(0, n)
+    def _(i):
+        zz = at.near(i)
+        half(zz, 0)
+
+        @pl.when(i + 1 < n)
+        def _():
+            gather.plane(at.near(i + 1))
+
+        @pl.when(i + 2 < n)
+        def _():
+            gather.column(at.near(i + 2))
+
+        gather.corner(zz)
+        half(zz, 1)
+        grads.s1(zz)
+
+        @pl.when(i >= 1)
+        def _():
+            grads.s2(at.near(i - 1))
+
+        @pl.when(i >= 2)
+        def _():
+            grads.s3(at.near(i - 2))
+
+    pl.semaphore_signal(free.at[0], inc=1, device_id=at.sib, device_id_type=MESH)
+
+    def grad_up(h, more):
+        @pl.loop(0, D // 256)
+        def _(q):
+            cols = pl.ds(pl.multiple_of(q * 256, 256), 256)
+            xs = xb[:, :, :, cols].reshape(n * 4 * rows, 256)
+            part = mm(xs, gg[:, :, :, pl.ds(h * f2, f2)].reshape(n * 4 * rows, f2), TN)
+            if more:
+                part += wup[h, cols, :].astype(f32)
+            wup[h, cols, :] = part.astype(bf16)
+
+    def grad_down(h):
+        for q in range(D // 512):
+            cols = pl.ds(q * 512, 512)
+            part = mm(mixed[:, :, :, pl.ds(h * f, f)].reshape(n * 4 * rows, f), cb[:, :, :, cols].reshape(n * 4 * rows, 512), TN)
+            if h == 0:
+                gdown_ref[:, cols] = part + wdown[0, :, cols].astype(f32)
+            else:
+                wdown[1, :, cols] = part.astype(bf16)
+
+    def output(zz):
+        @pl.loop(0, 2)
+        def _(p):
+            for q in range(D // 512):
+                cols = pl.ds(q * 512, 512)
+                part = mm(tokens(mixed, zz, p, 0, f), wdown[0, :, cols]) + mm(tokens(mixed, zz, p, f, f), wdown[1, :, cols])
+                gg[zz, pl.ds(2 * p, 2), :, cols] = part.astype(bf16).reshape(2, rows, 512)
+
+    grad_up(1, False)
+    pl.semaphore_wait(free.at[0], 1)
+    up_swap = send(wup.at[1], wup.at[0], core_ss.at[2], core_sr.at[2], at.sib)
+    for swap in swaps:
+        swap.wait_send()
+    up_swap.start()
+    grads.s2(at.near(n - 1))
+    grads.s3(at.near(n - 2))
+    up_swap.wait_recv()
+    grad_up(0, True)
+    share = D // n
+    own_share = pltpu.make_async_copy(wup.at[0, pl.ds(pl.multiple_of(d * share, share), share), :], gup_ref.at[d], load_sem.at[0])
+    own_share.start()
+
+    def exchange(k):
+        to = lax.rem(d + k, n)
+        return send(wup.at[0, pl.ds(pl.multiple_of(to * share, share), share), :], gup_ref.at[d], a2a_ss.at[k], a2a_sr.at[d], (to, at.e))
+
+    for k in range(1, n):
+        exchange(k).start()
+    grads.s3(at.near(n - 1))
+    for j in range(n + 3):
+        if j < n - 1:
+            grads.line(at.far(j))
+        if j < n:
+            output(at.far(j))
+            outs.s1(at.far(j))
+        if 0 <= j - 1 < n:
+            outs.s2(at.far(j - 1))
+        if 0 <= j - 2 < n:
+            outs.s3(at.far(j - 2))
+            if j - 2 < n - 1:
+                outs.line(at.far(j - 2))
+        if j == n - 1:
+            pl.semaphore_signal(free.at[1], inc=1, device_id=at.sib, device_id_type=MESH)
+            grad_down(1)
+            pl.semaphore_wait(free.at[1], 1)
+            down_swap = send(wdown.at[1], wdown.at[0], core_ss.at[3], core_sr.at[3], at.sib)
+            down_swap.start()
+        if j == n:
+            down_swap.wait_recv()
+            grad_down(0)
+    grads.last()
+    outs.last()
+    own_share.wait()
+    for k in range(1, n):
+        exchange(k).wait_send()
+        source = lax.rem(d + k, n)
+        send(wup.at[0, pl.ds(0, share), :], gup_ref.at[source], a2a_ss.at[k], a2a_sr.at[source], (source, at.e)).wait_recv()
+    up_swap.wait_send()
+    down_swap.wait_send()
+    gather.finish()
+    grads.finish()
+    outs.finish()
+
+
+def expert_layer(x, cot_all, up, down, pick, place, n, cid):
+    rows, wide = x.shape
+    f2 = up.shape[1]
+    f = f2 // 2
+    bf16 = jnp.bfloat16
+    V = lambda *s: pltpu.VMEM(s, bf16)
+    D_ = pltpu.SemaphoreType.DMA
+    any_, vm = pl.BlockSpec(memory_space=pl.ANY), pl.BlockSpec(memory_space=pltpu.VMEM)
     return pl.pallas_call(
-        moe_kernel,
-        grid=(blocks // group,),
+        functools.partial(expert_kernel, n),
         out_shape=(
-            jax.ShapeDtypeStruct((blocks, rows, D), jnp.bfloat16),
-            jax.ShapeDtypeStruct((blocks, rows, width), jnp.bfloat16),
-            jax.ShapeDtypeStruct((n, 2 * f, D // n), jnp.bfloat16),
+            jax.ShapeDtypeStruct((rows, D), jnp.float32),
+            jax.ShapeDtypeStruct((rows, wide), jnp.float32),
+            jax.ShapeDtypeStruct((n, D // n, f2), bf16),
             jax.ShapeDtypeStruct((f, D), jnp.float32),
         ),
-        in_specs=[pl.BlockSpec((group, rows, width), lambda i: (i, 0, 0)),
-                  pl.BlockSpec((group, rows, D), lambda i: (i, 0, 0)),
-                  full(up), full(upt), full(down), full(downt), full(pick), full(place)],
-        out_specs=[pl.BlockSpec((group, rows, D), lambda i: (i, 0, 0)),
-                   pl.BlockSpec((group, rows, width), lambda i: (i, 0, 0)),
-                   pl.BlockSpec((n, 2 * f, D // n), lambda i: (0, 0, 0), **once),
-                   pl.BlockSpec((f, D), lambda i: (0, 0), **once)],
-        scratch_shapes=[pltpu.VMEM((2 * f, D), jnp.float32), pltpu.VMEM((f, D), jnp.float32)],
-        compiler_params=pltpu.CompilerParams(vmem_limit_bytes=60 << 20),
-        cost_estimate=pl.CostEstimate(flops=2 * blocks * rows * D * f * 9, bytes_accessed=blocks * rows * D * 8, transcendentals=0),
+        in_specs=[any_, any_, any_, any_, vm, vm],
+        out_specs=[vm, vm, any_, vm],
+        scratch_shapes=[V(n, 4, rows, wide), V(n, 4, rows, D), V(n, 4, rows, 2 * f2), V(n, 4, rows, 2 * f), V(n, 4, rows, wide),
+                        V(2, D, f2), V(2, f, D)]
+        + gather_sems(n) + reduce_scratch(n, rows, wide) + reduce_scratch(n, rows, D)
+        + [D_((4,)), D_((4,)), D_((4,)), pltpu.SemaphoreType.REGULAR((2,)), D_((n,)), D_((n,))],
+        compiler_params=pltpu.CompilerParams(collective_id=cid, has_side_effects=True, vmem_limit_bytes=63 << 20),
         name="expert_layer",
-    )(x_all, cot_all, up, upt, down, downt, pick, place)
+    )(x, cot_all, up, down, pick, place)
+
+
+def column_kernel(n, own_ref, all_ref, load_sem, *sems):
+    at = Place(n)
+    gather = Gather(at, own_ref, all_ref, *sems)
+    load = pltpu.make_async_copy(own_ref, all_ref.at[at.d, 0], load_sem)
+    load.start()
+    at.meet()
+    gather.begin()
+    gather.plane(at.near(0))
+    for i in range(1, n + 1):
+        if i < n:
+            gather.column(at.near(i))
+            gather.plane(at.near(i))
+        gather.corner(at.near(i - 1))
+    load.wait()
+    gather.finish()
+
+
+def gather_columns(block, n, cid):
+    any_ = pl.BlockSpec(memory_space=pl.ANY)
+    return pl.pallas_call(
+        functools.partial(column_kernel, n),
+        out_shape=jax.ShapeDtypeStruct((n, 4) + block.shape, block.dtype),
+        in_specs=[any_],
+        out_specs=any_,
+        scratch_shapes=[pltpu.SemaphoreType.DMA] + gather_sems(n),
+        compiler_params=pltpu.CompilerParams(collective_id=cid, has_side_effects=True),
+        name="gather_columns",
+    )(block)
 
 
 def attention_forward(tokens, segment, gain, w_in, w_out):
@@ -844,9 +1289,9 @@
     w_router = tail[:, :experts]
     gain_first = tail[:, experts].astype(f32)[None, :]
     gain_second = tail[:, experts + 1].astype(f32)[None, :]
-    cot_all = all_gather(cot, n, 1, True)
-
-    ups = expert_in.reshape(held, D // n, 2, n, f).transpose(3, 1, 2, 0, 4).reshape(n, D // n, 2 * held * f)
+    cot_all = gather_columns(cot, n, 1)
+
+    ups = expert_in.reshape(held, D // n, 2, n, f).transpose(3, 1, 0, 2, 4).reshape(n, D // n, 2 * held * f)
     up = lax.all_to_all(ups, "dp", split_axis=0, concat_axis=0, tiled=True).reshape(D, 2 * held * f)
     down = expert_out.reshape(held * f, D)
 
@@ -863,21 +1308,18 @@
 
     high = gates.astype(bf16)
     low = (gates - high.astype(f32)).astype(bf16)
-    x_all = all_gather(
-        jnp.concatenate([normed_second, high, low, jnp.zeros((total, 128 - 2 * experts), bf16)], axis=1), n, 2, True)
-
-    first = lax.axis_index("expert") * held
+    dispatched = jnp.concatenate([normed_second, high, low, jnp.zeros((total, 128 - 2 * experts), bf16)], axis=1)
+
+    mine = lax.axis_index("expert")
+    order = jnp.stack([mine, mine + 1 - 2 * lax.rem(mine, 2)])
+    owner = (order[:, None] * held + jnp.arange(held, dtype=jnp.int32)[None, :]).reshape(-1)
+    owner = jnp.repeat(owner, f)[None, :]
     lane = jnp.arange(128, dtype=jnp.int32)[:, None]
-    owner = (first + jnp.arange(held * f, dtype=jnp.int32) // f)[None, :]
     pick = ((lane == owner) | (lane == owner + experts)).astype(bf16)
     place = (lane == owner).astype(bf16).T
-    out_parts, grad_parts, grad_up, grad_down = moe_call(x_all, cot_all, up, up.T, down, down.T, pick, place, n, 2)
-
-    moe_sum = reduce_scatter(out_parts, n, 3, True)
+    moe_sum, grad_sum, grad_up, grad_down = expert_layer(dispatched, cot_all, up, down, pick, place, n, 2)
     result = (middle + moe_sum).astype(bf16)
-    grad_sum = reduce_scatter(grad_parts, n, 4, True)
-    grad_up = lax.all_to_all(grad_up, "dp", split_axis=0, concat_axis=0, tiled=True)
-    grad_up = grad_up.reshape(n, 2, held, f, D // n).transpose(2, 4, 1, 0, 3).reshape(held, D // n, 2 * FF).astype(f32)
+    grad_up = grad_up.reshape(n, D // n, held, 2, f).transpose(2, 1, 3, 0, 4).reshape(held, D // n, 2 * FF).astype(f32)
 
     upstream = cot.astype(f32)
     grad_gates = grad_sum[:, D : D + experts]
@@ -892,7 +1334,7 @@
     parts = jnp.concatenate(
         [grad_in, grad_out, grad_router, grad_gain_attn[:, None], grad_gain_ffn[:, None], jnp.zeros((D, wide - used), f32)],
         axis=1).astype(bf16)
-    sums = reduce_scatter(parts.reshape(-1, shard, wide), n, 5, False)
+    sums = reduce_scatter(parts.reshape(-1, shard, wide), n, 3, False)
     a, b = widths[0], widths[0] + widths[1]
     return (
         result.reshape(micro, rows, D),
@@ -921,7 +1363,7 @@
         P("expert", "dp", None),
         P("expert", "dp", None),
     )
-    fast = mesh.shape["expert"] == 8 and FF // mesh.shape["dp"] % 128 == 0
+    fast = mesh.shape["expert"] == 8 and FF // mesh.shape["dp"] == 128
     body = functools.partial(per_device_fast, mesh.shape["dp"]) if fast else per_device
     return jax.shard_map(
         body,

time: 675 us -> 603 us (0.89)
  Pallas kernels: 504 us -> 481 us
  local copies, waits for them, and re-layouts: 87.6 us -> 71.6 us
  other arithmetic: 22.6 us -> 7.68 us
  matrix products: 43.9 us -> 34.2 us
    pallas_call x1 -> x2, Pallas kernels: 74 us -> 306 us  [the longest x1 243 us: expert_layer(): pl.pallas_call(functools.partial(expert_kernel, n), out_shape=(jax.ShapeD...]
    pallas_call x3 -> x1, Pallas kernels: 202 us -> 74.4 us  [reduce_scatter(): pl.pallas_call(functools.partial(reduce_kernel, n, by_rows), out_shape=ja...]
    pallas_call x3 -> x1, Pallas kernels: 227 us -> 101 us  [all_gather(): pl.pallas_call(functools.partial(gather_kernel, n, by_rows), out_shape=ja...]
    reshape x5 -> x2, local copies, waits for them, and re-layouts: 16.6 us -> 8.08 us  [per_device_fast(): expert_in.reshape(held, D // n, 2, n, f).transpose(3, 1, 0, 2, 4)]
    convert_element_type x2 -> x3, local copies, waits for them, and re-layouts: 13.2 us -> 20 us  [per_device_fast(): grad_up.reshape(n, D // n, held, 2, f).transpose(2, 1, 3, 0, 4)]
  transfers between devices with their start and end apart: 2 -> 1, of which waited for: 0 -> 0; matrix products, arithmetic and copies ran while one was open for 16% -> 3% of each run, Pallas kernels for 44% -> 27%
where the time goes in v2:
time: 603 us; the launch traced here: 601 us
  Pallas kernels  481 us (80%)
  local copies, waits for them, and re-layouts  71.6 us (12%)
  matrix products  34.2 us (6%)
  other arithmetic  7.68 us (1%)
    pallas_call x1, Pallas kernels, expert_layer(): pl.pallas_call(functools.partial(expert_kernel, n), out_shape=(jax.ShapeD...  243 us
    pallas_call x1, Pallas kernels, all_gather(): pl.pallas_call(functools.partial(gather_kernel, n, by_rows), out_shape=ja...  101 us
    pallas_call x1, Pallas kernels, reduce_scatter(): pl.pallas_call(functools.partial(reduce_kernel, n, by_rows), out_shape=ja...  74.4 us
    pallas_call x1, Pallas kernels, gather_columns(): pl.pallas_call(functools.partial(column_kernel, n), out_shape=jax.ShapeDt...  63 us
    concatenate x3, local copies, waits for them, and re-layouts, per_device_fast(): jnp.concatenate([grad_in, grad_out, grad_router, grad_gain_attn[:, None],...  20.9 us
    convert_element_type x3, local copies, waits for them, and re-layouts, per_device_fast(): grad_up.reshape(n, D // n, held, 2, f).transpose(2, 1, 3, 0, 4)  20 us
  transfers between devices with their start and end apart: 1, of which 0 were waited for; matrix products, arithmetic and copies ran while one was open for 3% of the time, Pallas kernels for 27%

profile of v2, /device:TPU:11, one launch (start us, length us, event | category | flops | bytes accessed | tf_op | source)
XLA Modules:
  0.0 600.7 jit_solution(6674346138580744607)
XLA Ops:
  0.6 5.6 reshape.355
  6.2 3.5 copy.83
  9.7 2.5 reshape.356
  12.2 4.9 all-to-all-start
  17.5 0.8 concatenate.41.in_ref
  18.3 100.6 %gather_blocks.1 = bf16[32,48,4224]{2,1,0:T(8,128)(2,1)} custom-call(bf16[48,4224]{1,0:T(8,128)(2,1)} %concatenate.41.in_ref), custom_call_target="tpu_custom_call" | custom-call | tf_op jit(solution)/shard_map/gather_blocks/pallas_call | solution.py:516
  119.0 1.5 fusion.50
  121.1 4.4 fusion.3
  125.6 1.0 copy-done.9
  126.7 0.5 broadcast.206
  127.2 0.7 reduce.12
  129.3 63.0 %gather_columns.1.cot_ref = bf16[4,4,128,1536]{3,2,1,0:T(8,128)(2,1)} custom-call(bf16[128,1536]{1,0:T(8,128)(2,1)} %bitcast.129), custom_call_target="tpu_custom_call" | custom-call | tf_op jit(solution)/shard_map/gather_columns/pallas_call | solution.py:1195
  192.6 0.9 copy.91
  193.9 0.7 fusion.51
  194.9 0.8 copy-done.7
  195.8 3.4 multiply_reduce_fusion.4
  199.3 1.5 fusion.52
  201.1 0.9 concatenate.44.x_ref
  202.1 0.8 fusion.30.place_ref
  203.0 0.7 fusion.29.pick_ref
  203.7 242.7 %expert_layer.1 = (f32[128,1536]{1,0:T(8,128)}, f32[128,1664]{1,0:T(8,128)}, bf16[4,384,768]{2,1,0:T(8,128)(2,1)}, f32[384,1536]{1,0:T(8,128)}) custom-call(bf16[128,1664]{1,0:T(8,128)(2,1)} %concatenate.44.x_ref, bf16[4,4,128,1536]{3,2,1,0:T(8,128)(2,1)} %gather_columns.1.cot_ref, bf16[1536,768]{1,0:T(8,128)(2,1)} %bitcast.16.up_ref, ...), custom_call_target="tpu_custom_call" | custom-call | tf_op jit(solution)/shard_map/expert_layer/pallas_call | solution.py:1157
  446.4 1.0 multiply_reduce_fusion.6
  447.5 1.8 multiply_reduce_fusion
  449.3 1.1 multiply_add_fusion.1
  450.4 4.1 fusion.12
  454.7 0.5 fusion.23
  455.6 0.4 fusion.16
  456.5 0.5 copy-done.12
  457.1 0.5 fusion.22
  458.1 1.1 convolution_convert_fusion.2
  459.9 0.5 copy-done.1
  460.4 6.5 %multiply_reduce_fusion.1 = (bf16[1536]{0:T(1024)(128)(2,1)S(1)}, f32[128]{0:T(128)}, f32[128,1536]{1,0:T(8,128)S(1)}) fusion(bf16[2,64,1536]{2,1,0:T(8,128)(2,1)S(1)} %copy-done.1, f32[128]{0:T(128)S(1)} %copy-done.30, f32[1536]{0:T(1024)S(1)} %convert_reduce_fusion.1, bf16[1536,4224]{1,0:T(8,128)(2,1)} %bitcast.123, bf16[128,512]{1,0:T(8,128)(2,1)S(1)} %copy.90, ...), kind=kOutput, calls=%fused_computation.34 | convolution fusion | flops 1009973632 | bytes 9709568 | tf_op jit(solution)/shard_map/tq,cq->tc/dot_general | solution.py:1261
  466.9 5.2 convolution_convert_fusion
  472.2 3.6 convolution_convert_fusion.1
  476.0 0.7 concatenate.52
  476.7 0.7 concatenate.53
  477.5 19.5 %concatenate.51.in_ref = bf16[32,48,4224]{2,1,0:T(8,128)(2,1)} concatenate(bf16[32,48,2560]{2,1,0:T(8,128)(2,1)} %convolution_convert_fusion, bf16[32,48,1536]{2,1,0:T(8,128)(2,1)} %convolution_convert_fusion.1, bf16[32,48,24]{2,1,0:T(8,128)(2,1)S(1)} %bitcast.132, bf16[32,48,1]{2,1,0:T(8,128)(2,1)S(1)} %concatenate.52, bf16[32,48,1]{2,1,0:T(8,128)(2,1)S(1)} %concatenate.53, ...), dimensions={2} | concatenate | bytes 25952256 | tf_op jit(solution)/shard_map/concatenate | solution.py:1334
  497.0 74.4 %reduce_blocks.1 = f32[48,4224]{1,0:T(8,128)} custom-call(bf16[32,48,4224]{2,1,0:T(8,128)(2,1)} %concatenate.51.in_ref), custom_call_target="tpu_custom_call" | custom-call | tf_op jit(solution)/shard_map/reduce_blocks/pallas_call | solution.py:668
  571.4 1.5 slice_reduce_fusion
  572.9 1.8 slice.93
  574.8 1.7 slice.94
  576.5 0.7 copy.96
  577.1 6.0 reshape.370
  583.1 7.5 %copy.95 = f32[3,384,2,4,128]{4,3,2,1,0:T(4,128)} copy(f32[3,384,2,4,128]{4,2,0,1,3:T(2,128)} %bitcast.116) | data formatting | bytes 9437184 | tf_op jit(solution)/shard_map/convert_element_type | solution.py:1322
  590.6 6.5 %reshape.369 = f32[3,384,1024]{2,1,0:T(8,128)} reshape(f32[3,384,2,4,128]{4,3,2,1,0:T(4,128)} %copy.95) | data formatting | bytes 9437184 | tf_op jit(solution)/shard_map/convert_element_type | solution.py:1322
  597.1 1.2 multiply_add_fusion
  598.3 0.8 copy-done.4
  599.1 1.4 copy.112
  (128 shorter events, 6.5 us)
Async XLA Ops:
  12.2 4.9 copy-start.26
  12.2 5.0 copy-start.32
  12.2 5.1 copy-start.33
  12.2 5.2 copy-start.19
  12.2 5.2 copy-start.20
  12.2 191.5 %all-to-all-start = ((bf16[4,384,768]{2,1,0:T(8,128)(2,1)}), bf16[4,384,768]{2,1,0:T(8,128)(2,1)}, u32[]{:S(2)}, u32[]{:S(2)}) async-start(bf16[4,384,768]{2,1,0:T(8,128)(2,1)} %reshape.356), calls=%async_computation | async-start | bytes 4718592 | tf_op jit(solution)/shard_map/all_to_all | solution.py:1295
  119.0 1.7 copy-start
  120.9 4.6 copy-start.29
  125.5 1.1 copy-start.9
  125.6 1.6 copy-start.31
  126.7 2.1 slice-start.1
  128.3 0.8 copy-start.25
  128.4 66.2 %copy-start.21 = (bf16[128,512]{0,1:T(8,128)(2,1)}, bf16[128,512]{0,1:T(8,128)(2,1)S(1)}, u32[]{:S(2)}) copy-start(bf16[128,512]{0,1:T(8,128)(2,1)S(1)} %copy.74) | copy-start | bytes 393220
  193.7 0.8 copy-start.17
  193.8 0.7 copy-start.11
  193.9 0.8 copy-start.13
  194.6 1.1 copy-start.7
  194.6 1.1 copy-start.23
  195.8 3.4 copy-start.15
  199.3 1.8 copy-start.2
  446.4 2.9 copy-start.6
  446.4 2.9 copy-start.10
  447.5 2.9 copy-start.27
  450.4 4.3 copy-start.8
  450.4 4.3 copy-start.24
  454.7 0.9 copy-start.22
  456.1 0.9 copy-start.12
  456.1 1.0 copy-start.14
  456.1 1.5 copy-start.18
  457.1 1.0 copy-start.3
  457.1 1.0 copy-start.28
  459.4 1.0 copy-start.1
  459.4 1.0 copy-start.30
  460.4 6.5 %copy-start.5 = (bf16[1536,128]{1,0:T(8,128)(2,1)S(1)}, bf16[1536,128]{1,0:T(8,128)(2,1)}, u32[]{:S(2)}) copy-start(bf16[1536,128]{1,0:T(8,128)(2,1)} %copy.91) | copy-start | bytes 1179652
  466.9 5.3 copy-start.16
  571.3 5.1 copy-start.34
  571.4 5.1 slice-start
  597.1 1.9 copy-start.4

commit v3 on v0

--- a/solution.py
+++ b/solution.py
@@ -1,7 +1,13 @@
+import functools
+
 import jax
 import jax.numpy as jnp
 from jax import lax
+from jax.experimental import pallas as pl
+from jax.experimental.pallas import tpu as pltpu
 from jax.sharding import PartitionSpec as P
+
+MESH = pl.DeviceIdType.MESH
 
 D = 1536
 HEADS = 24
@@ -401,6 +407,1062 @@
     )
 
 
+NN = (((1,), (0,)), ((), ()))
+NT = (((1,), (1,)), ((), ()))
+TN = (((0,), (0,)), ((), ()))
+
+
+def mm(a, b, dims=NN):
+    return lax.dot_general(a, b, dims, preferred_element_type=jnp.float32)
+
+
+class Place:
+    def __init__(self, n):
+        self.n = n
+        d = self.d = lax.axis_index("dp")
+        e = self.e = lax.axis_index("expert")
+        c, x, y = lax.rem(e, 2), lax.rem(lax.div(e, 2), 2), lax.div(e, 4)
+        self.sib = (d, e + 1 - 2 * c)
+        self.nx = (d, e + 2 - 4 * x)
+        self.ny = (d, e + 4 - 8 * y)
+        self.diag = self.nx[1] + 4 - 8 * y
+        self.c, self.x, self.y = c, x, y
+        self.below = (d - 1, e)
+        self.above = (d + 1, e)
+        self.has_below = d > 0
+        self.has_above = d < n - 1
+
+    def meet(self, everyone=False):
+        barrier = pltpu.get_barrier_semaphore()
+        d, n = self.d, self.n
+        if everyone:
+            others = n - 1 + 3
+
+            @pl.loop(1, n)
+            def _(k):
+                pl.semaphore_signal(barrier, inc=1, device_id=(lax.rem(d + k, n), self.e), device_id_type=MESH)
+        else:
+            others = 3 + jnp.minimum(d, 1) + jnp.minimum(n - 1 - d, 1)
+
+            @pl.when(self.has_below)
+            def _():
+                pl.semaphore_signal(barrier, inc=1, device_id=self.below, device_id_type=MESH)
+
+            @pl.when(self.has_above)
+            def _():
+                pl.semaphore_signal(barrier, inc=1, device_id=self.above, device_id_type=MESH)
+
+        for dev in (self.sib, self.nx, self.ny):
+            pl.semaphore_signal(barrier, inc=1, device_id=dev, device_id_type=MESH)
+        pl.semaphore_wait(barrier, others)
+
+    def far(self, i):
+        n, d = self.n, self.d
+        low = d < n - d
+        m = jnp.where(low, d, n - 1 - d)
+        t = jnp.where(i < n - 1 - m, n - 1 - i, jnp.where(i < n - 1, i - (n - 1 - m), m))
+        return jnp.where(low, t, n - 1 - t)
+
+    def near(self, i):
+        return self.far(self.n - 1 - i)
+
+
+def send(src, dst, ss, rs, dev):
+    return pltpu.make_async_remote_copy(src, dst, ss, rs, device_id=dev, device_id_type=MESH)
+
+
+class Gather:
+    def __init__(self, at, own, buf, send_sem, recv_z, recv_x, recv_y, recv_d):
+        self.at, self.own, self.buf = at, own, buf
+        self.ss, self.rz, self.rx, self.ry, self.rd = send_sem, recv_z, recv_x, recv_y, recv_d
+        rows = own.shape[0]
+        self.A, self.B = pl.ds(0, rows // 2), pl.ds(rows // 2, rows // 2)
+
+    def source(self, zz, own):
+        return self.own if own else self.buf.at[zz, 0]
+
+    def down(self, zz, own=False):
+        return send(self.source(zz, own), self.buf.at[zz, 0], self.ss.at[zz, 0], self.rz.at[zz], self.at.below)
+
+    def up(self, zz, own=False):
+        return send(self.source(zz, own), self.buf.at[zz, 0], self.ss.at[zz, 1], self.rz.at[zz], self.at.above)
+
+    def to_x(self, zz, own=False):
+        return send(self.source(zz, own), self.buf.at[zz, 1], self.ss.at[zz, 2], self.rx.at[zz], self.at.nx)
+
+    def to_y(self, zz, own=False):
+        return send(self.source(zz, own), self.buf.at[zz, 2], self.ss.at[zz, 3], self.ry.at[zz], self.at.ny)
+
+    def turn_y(self, zz):
+        return send(self.buf.at[zz, 1, self.A], self.buf.at[zz, 3, self.A], self.ss.at[zz, 4], self.rd.at[zz, 0], self.at.ny)
+
+    def turn_x(self, zz):
+        return send(self.buf.at[zz, 2, self.B], self.buf.at[zz, 3, self.B], self.ss.at[zz, 5], self.rd.at[zz, 1], self.at.nx)
+
+    def begin(self):
+        self.begin_z()
+        self.begin_xy()
+
+    def begin_z(self):
+        d = self.at.d
+
+        @pl.when(self.at.has_below)
+        def _():
+            self.down(d, True).start()
+
+        @pl.when(self.at.has_above)
+        def _():
+            self.up(d, True).start()
+
+    def begin_xy(self):
+        self.to_x(self.at.d, True).start()
+        self.to_y(self.at.d, True).start()
+
+    def column_z(self, zz):
+        d = self.at.d
+
+        @pl.when(zz < d)
+        def _():
+            self.up(zz).wait_recv()
+
+            @pl.when(self.at.has_above)
+            def _():
+                self.up(zz).start()
+
+        @pl.when(zz > d)
+        def _():
+            self.down(zz).wait_recv()
+
+            @pl.when(self.at.has_below)
+            def _():
+                self.down(zz).start()
+
+    def column_xy(self, zz):
+        self.to_x(zz).start()
+        self.to_y(zz).start()
+
+    def column(self, zz):
+        self.column_z(zz)
+        self.column_xy(zz)
+
+    def plane(self, zz):
+        self.to_x(zz).wait_recv()
+        self.turn_y(zz).start()
+        self.to_y(zz).wait_recv()
+        self.turn_x(zz).start()
+
+    def corner(self, zz):
+        self.turn_y(zz).wait_recv()
+        self.turn_x(zz).wait_recv()
+
+    def finish(self):
+        d = self.at.d
+
+        @pl.loop(0, self.at.n)
+        def _(zz):
+            for copy in (self.to_x, self.to_y, self.turn_y, self.turn_x):
+                copy(zz).wait_send()
+
+            @pl.when((d > 0) & (zz >= d))
+            def _():
+                self.down(zz).wait_send()
+
+            @pl.when(self.at.has_above & (zz <= d))
+            def _():
+                self.up(zz).wait_send()
+
+
+def gather_sems(n):
+    D_ = pltpu.SemaphoreType.DMA
+    return [D_((n, 6)), D_((n,)), D_((n,)), D_((n,)), D_((n, 2))]
+
+
+def add_rows(dst, src):
+    rows = dst.shape[0]
+    step = 16
+
+    @pl.loop(0, rows // step)
+    def _(r):
+        w = pl.ds(pl.multiple_of(r * step, step), step)
+        dst[w, :] = (dst[w, :].astype(jnp.float32) + src[w, :].astype(jnp.float32)).astype(dst.dtype)
+
+
+class Reduce:
+    def __init__(self, at, buf, total, r1, r2, rz, ss_1, sr_1, ss_2, sr_2, ss_z, sr_z, start=None):
+        self.start = start
+        self.at, self.buf, self.total = at, buf, total
+        self.r1, self.r2, self.rz = r1, r2, rz
+        self.sems = (ss_1, sr_1, ss_2, sr_2, ss_z, sr_z)
+        rows = total.shape[0]
+        self.A, self.B = pl.ds(0, rows // 2), pl.ds(rows // 2, rows // 2)
+
+    def first(self, zz, k):
+        ss, sr = self.sems[0], self.sems[1]
+        slot, part, dev = ((3, self.A, self.at.nx), (3, self.B, self.at.ny), (1, self.A, self.at.nx), (2, self.B, self.at.ny))[k]
+        return send(self.buf.at[zz, slot, part], self.r1.at[zz, k], ss.at[zz, k], sr.at[zz, k], dev)
+
+    def second(self, zz, k):
+        ss, sr = self.sems[2], self.sems[3]
+        slot, part, dev = ((2, self.A, self.at.ny), (1, self.B, self.at.nx))[k]
+        return send(self.buf.at[zz, slot, part], self.r2.at[zz, k], ss.at[zz, k], sr.at[zz, k], dev)
+
+    def down(self, zz):
+        return send(self.buf.at[zz, 0], self.rz.at[zz], self.sems[4].at[zz], self.sems[5].at[zz], self.at.below)
+
+    def up(self, zz):
+        slot = jnp.where(zz == self.at.d + 1, self.at.n, zz)
+        return send(self.buf.at[zz, 0], self.rz.at[slot], self.sems[4].at[zz], self.sems[5].at[slot], self.at.above)
+
+    def arrive(self, slot):
+        return send(self.buf.at[0, 0], self.rz.at[slot], self.sems[4].at[0], self.sems[5].at[slot], self.at.nx)
+
+    def s1(self, zz):
+        for k in range(4):
+            self.first(zz, k).start()
+
+    def s2(self, zz):
+        self.first(zz, 0).wait_recv()
+        add_rows(self.buf.at[zz, 2, self.A], self.r1.at[zz, 0])
+        self.second(zz, 0).start()
+        self.first(zz, 1).wait_recv()
+        add_rows(self.buf.at[zz, 1, self.B], self.r1.at[zz, 1])
+        self.second(zz, 1).start()
+        self.first(zz, 2).wait_recv()
+        add_rows(self.buf.at[zz, 0, self.A], self.r1.at[zz, 2])
+        self.first(zz, 3).wait_recv()
+        add_rows(self.buf.at[zz, 0, self.B], self.r1.at[zz, 3])
+
+    def s3(self, zz):
+        self.second(zz, 0).wait_recv()
+        add_rows(self.buf.at[zz, 0, self.A], self.r2.at[zz, 0])
+        self.second(zz, 1).wait_recv()
+        add_rows(self.buf.at[zz, 0, self.B], self.r2.at[zz, 1])
+
+    def line(self, zz):
+        d = self.at.d
+
+        @pl.when(((zz < d) & self.at.has_above) | ((zz > d) & self.at.has_below))
+        def _():
+            self.arrive(zz).wait_recv()
+            add_rows(self.buf.at[zz, 0], self.rz.at[zz])
+
+        @pl.when(zz < d)
+        def _():
+            self.down(zz).start()
+
+        @pl.when(zz > d)
+        def _():
+            self.up(zz).start()
+
+    def last(self):
+        d, n, rows, step = self.at.d, self.at.n, self.total.shape[0], 16
+
+        def over(fn):
+            @pl.loop(0, rows // step)
+            def _(r):
+                fn(pl.ds(pl.multiple_of(r * step, step), step))
+
+        def own(w):
+            first = self.buf[d, 0, w, :].astype(jnp.float32)
+            self.total[w, :] = first if self.start is None else first + self.start[w, :]
+
+        def more(slot):
+            def fn(w):
+                self.total[w, :] += self.rz[slot, w, :].astype(jnp.float32)
+
+            self.arrive(slot).wait_recv()
+            over(fn)
+
+        over(own)
+
+        @pl.when(self.at.has_above)
+        def _():
+            more(d)
+
+        @pl.when(self.at.has_below)
+        def _():
+            more(n)
+
+    def finish(self):
+        d = self.at.d
+
+        @pl.loop(0, self.at.n)
+        def _(zz):
+            for k in range(4):
+                self.first(zz, k).wait_send()
+            for k in range(2):
+                self.second(zz, k).wait_send()
+
+            @pl.when(zz != d)
+            def _():
+                self.arrive(zz)
+                send(self.buf.at[zz, 0], self.rz.at[zz], self.sems[4].at[zz], self.sems[5].at[zz], self.at.nx).wait_send()
+
+
+def reduce_scratch(n, rows, cols):
+    D_ = pltpu.SemaphoreType.DMA
+    V = lambda *s: pltpu.VMEM(s, jnp.bfloat16)
+    return [V(n, 4, rows // 2, cols), V(n, 2, rows // 2, cols), V(n + 1, rows, cols),
+            D_((n, 4)), D_((n, 4)), D_((n, 2)), D_((n, 2)), D_((n,)), D_((n + 1,))]
+
+
+def expert_kernel(n, x_ref, cot_ref, up_ref, down_ref, pick_ref, place_ref, mid_ref,
+                  out_ref, gx_ref, gup_ref, gdown_ref,
+                  xb, cb, gg, mixed, gb, wup, wdown, *rest):
+    f32, bf16 = jnp.float32, jnp.bfloat16
+    at = Place(n)
+    d = at.d
+    gather = Gather(at, x_ref, xb, *rest[:5])
+    grads = Reduce(at, gb, gx_ref, *rest[5:14])
+    outs = Reduce(at, gg, out_ref, *rest[14:23], start=mid_ref)
+    load_sem, core_ss, core_sr, free = rest[23:]
+    rows = x_ref.shape[0]
+    f2 = up_ref.shape[1]
+    f = f2 // 2
+    held = f // 128
+    loads = [
+        pltpu.make_async_copy(x_ref, xb.at[d, 0], load_sem.at[0]),
+        pltpu.make_async_copy(up_ref, wup.at[0], load_sem.at[1]),
+        pltpu.make_async_copy(down_ref, wdown.at[0], load_sem.at[2]),
+        pltpu.make_async_copy(cot_ref, cb, load_sem.at[3]),
+    ]
+    for load in loads:
+        load.start()
+    at.meet()
+    gather.begin()
+    swaps = [
+        send(up_ref, wup.at[1], core_ss.at[0], core_sr.at[0], at.sib),
+        send(down_ref, wdown.at[1], core_ss.at[1], core_sr.at[1], at.sib),
+    ]
+    for swap in swaps:
+        swap.start()
+    for load in loads:
+        load.wait()
+    for swap in swaps:
+        swap.wait_recv()
+    gather.plane(at.near(0))
+    gather.column(at.near(1))
+
+    def tokens(ref, zz, p, lo, width):
+        return ref[zz, pl.ds(2 * p, 2), :, pl.ds(lo, width)].reshape(2 * rows, width)
+
+    def half(zz, p):
+        pair = pl.ds(2 * p, 2)
+        x = tokens(xb, zz, p, 0, D)
+        cot = tokens(cb, zz, p, 0, D)
+        mix = mm(tokens(xb, zz, p, D, 128), pick_ref[...])
+        sums = jnp.zeros((2 * rows, 128), f32)
+        for h in range(2):
+            gate_up = mm(x, wup[h])
+            back = mm(cot, wdown[h], NT)
+            for j in range(held):
+                k = h * held + j
+                gate = gate_up[:, j * 256 : j * 256 + 128]
+                up = gate_up[:, j * 256 + 128 : j * 256 + 256]
+                b = back[:, j * 128 : (j + 1) * 128]
+                m = mix[:, k * 128 : (k + 1) * 128]
+                sig = 1.0 / (1.0 + jnp.exp(-gate))
+                act = gate * sig
+                hidden = (act * up).astype(bf16).astype(f32)
+                prod = hidden * b
+                high = prod.astype(bf16)
+                low = (prod - high.astype(f32)).astype(bf16)
+                sel = place_ref[k * 128 : (k + 1) * 128, :]
+                sums += mm(high, sel) + mm(low, sel)
+                mixed[zz, pair, :, pl.ds(k * 128, 128)] = (m * hidden).astype(bf16).reshape(2, rows, 128)
+                gh = m * b
+                gg[zz, pair, :, pl.ds(k * 256, 128)] = (
+                    (gh * up * sig * (1.0 + gate * (1.0 - sig))).astype(bf16).reshape(2, rows, 128))
+                gg[zz, pair, :, pl.ds(k * 256 + 128, 128)] = (gh * act).astype(bf16).reshape(2, rows, 128)
+        for q in range(D // 512):
+            cols = pl.ds(q * 512, 512)
+            part = mm(tokens(gg, zz, p, 0, f2), wup[0, cols, :], NT) + mm(tokens(gg, zz, p, f2, f2), wup[1, cols, :], NT)
+            gb[zz, pair, :, cols] = part.astype(bf16).reshape(2, rows, 512)
+        gb[zz, pair, :, pl.ds(D, 128)] = sums.astype(bf16).reshape(2, rows, 128)
+
+    @pl.loop(0, n)
+    def _(i):
+        zz = at.near(i)
+        half(zz, 0)
+
+        @pl.when(i + 1 < n)
+        def _():
+            gather.plane(at.near(i + 1))
+
+        @pl.when(i + 2 < n)
+        def _():
+            gather.column(at.near(i + 2))
+
+        gather.corner(zz)
+        half(zz, 1)
+        grads.s1(zz)
+
+        @pl.when(i >= 1)
+        def _():
+            grads.s2(at.near(i - 1))
+
+        @pl.when(i >= 2)
+        def _():
+            grads.s3(at.near(i - 2))
+
+    pl.semaphore_signal(free.at[0], inc=1, device_id=at.sib, device_id_type=MESH)
+
+    def grad_up(h, more):
+        @pl.loop(0, D // 256)
+        def _(q):
+            cols = pl.ds(pl.multiple_of(q * 256, 256), 256)
+            xs = xb[:, :, :, cols].reshape(n * 4 * rows, 256)
+            part = mm(xs, gg[:, :, :, pl.ds(h * f2, f2)].reshape(n * 4 * rows, f2), TN)
+            if more:
+                part += wup[h, cols, :].astype(f32)
+            wup[h, cols, :] = part.astype(bf16)
+
+    def grad_down(h):
+        for q in range(D // 512):
+            cols = pl.ds(q * 512, 512)
+            part = mm(mixed[:, :, :, pl.ds(h * f, f)].reshape(n * 4 * rows, f), cb[:, :, :, cols].reshape(n * 4 * rows, 512), TN)
+            if h == 0:
+                gdown_ref[:, cols] = part + wdown[0, :, cols].astype(f32)
+            else:
+                wdown[1, :, cols] = part.astype(bf16)
+
+    def output(zz):
+        @pl.loop(0, 2)
+        def _(p):
+            for q in range(D // 512):
+                cols = pl.ds(q * 512, 512)
+                part = mm(tokens(mixed, zz, p, 0, f), wdown[0, :, cols]) + mm(tokens(mixed, zz, p, f, f), wdown[1, :, cols])
+                gg[zz, pl.ds(2 * p, 2), :, cols] = part.astype(bf16).reshape(2, rows, 512)
+
+    grad_up(1, False)
+    pl.semaphore_wait(free.at[0], 1)
+    up_swap = send(wup.at[1], wup.at[0], core_ss.at[2], core_sr.at[2], at.sib)
+    for swap in swaps:
+        swap.wait_send()
+    up_swap.start()
+    grads.s2(at.near(n - 1))
+    grads.s3(at.near(n - 2))
+    up_swap.wait_recv()
+    grad_up(0, True)
+    keep = pltpu.make_async_copy(wup.at[0], gup_ref, load_sem.at[0])
+    keep.start()
+    grads.s3(at.near(n - 1))
+    for j in range(n + 3):
+        if j < n - 1:
+            grads.line(at.far(j))
+        if j < n:
+            output(at.far(j))
+            outs.s1(at.far(j))
+        if 0 <= j - 1 < n:
+            outs.s2(at.far(j - 1))
+        if 0 <= j - 2 < n:
+            outs.s3(at.far(j - 2))
+            if j - 2 < n - 1:
+                outs.line(at.far(j - 2))
+        if j == n - 1:
+            pl.semaphore_signal(free.at[1], inc=1, device_id=at.sib, device_id_type=MESH)
+            grad_down(1)
+            pl.semaphore_wait(free.at[1], 1)
+            down_swap = send(wdown.at[1], wdown.at[0], core_ss.at[3], core_sr.at[3], at.sib)
+            down_swap.start()
+        if j == n:
+            down_swap.wait_recv()
+            grad_down(0)
+    grads.last()
+    outs.last()
+    keep.wait()
+    up_swap.wait_send()
+    down_swap.wait_send()
+    gather.finish()
+    grads.finish()
+    outs.finish()
+
+
+def expert_layer(x, cot_all, up, down, pick, place, middle, n, cid):
+    rows, wide = x.shape
+    f2 = up.shape[1]
+    f = f2 // 2
+    bf16 = jnp.bfloat16
+    V = lambda *s: pltpu.VMEM(s, bf16)
+    D_ = pltpu.SemaphoreType.DMA
+    any_, vm = pl.BlockSpec(memory_space=pl.ANY), pl.BlockSpec(memory_space=pltpu.VMEM)
+    return pl.pallas_call(
+        functools.partial(expert_kernel, n),
+        out_shape=(
+            jax.ShapeDtypeStruct((rows, D), jnp.float32),
+            jax.ShapeDtypeStruct((rows, wide), jnp.float32),
+            jax.ShapeDtypeStruct((D, f2), bf16),
+            jax.ShapeDtypeStruct((f, D), jnp.float32),
+        ),
+        in_specs=[any_, any_, any_, any_, vm, vm, vm],
+        out_specs=[vm, vm, any_, vm],
+        scratch_shapes=[V(n, 4, rows, wide), V(n, 4, rows, D), V(n, 4, rows, 2 * f2), V(n, 4, rows, 2 * f), V(n, 4, rows, wide),
+                        V(2, D, f2), V(2, f, D)]
+        + gather_sems(n) + reduce_scratch(n, rows, wide) + reduce_scratch(n, rows, D)
+        + [D_((4,)), D_((4,)), D_((4,)), pltpu.SemaphoreType.REGULAR((2,))],
+        compiler_params=pltpu.CompilerParams(collective_id=cid, has_side_effects=True, vmem_limit_bytes=63 << 20),
+        name="expert_layer",
+    )(x, cot_all, up, down, pick, place, middle)
+
+
+class GatherAll:
+    def __init__(self, at, own, buf, send_sem, recv_z, recv_x, recv_y, recv_d, recv_s):
+        self.at, self.own, self.buf = at, own, buf
+        self.ss, self.rz, self.rx, self.ry, self.rd, self.rs = send_sem, recv_z, recv_x, recv_y, recv_d, recv_s
+        cols = own.shape[1]
+        half = (cols // 128 + 1) // 2 * 128
+        self.A, self.B, self.F = pl.ds(0, half), pl.ds(half, cols - half), pl.ds(0, cols)
+
+    def move(self, zz, e, cols, slot, sem, dev, own=False):
+        dst = self.buf.at[zz * 8 + e, :, cols]
+        return send(self.own.at[:, cols] if own else dst, dst, self.ss.at[zz, slot], sem, dev)
+
+    def down(self, zz, own=False):
+        return self.move(zz, self.at.e, self.F, 0, self.rz.at[zz], self.at.below, own)
+
+    def up(self, zz, own=False):
+        return self.move(zz, self.at.e, self.F, 1, self.rz.at[zz], self.at.above, own)
+
+    def spread(self, zz, own=False):
+        at = self.at
+        return (self.move(zz, at.e, self.F, 2, self.rx.at[zz], at.nx, own),
+                self.move(zz, at.e, self.F, 3, self.ry.at[zz], at.ny, own),
+                self.move(zz, at.e, self.F, 4, self.rs.at[zz, 0], at.sib, own))
+
+    def from_x(self, zz):
+        at = self.at
+        ex = at.nx[1]
+        return (self.move(zz, ex, self.F, 2, self.rx.at[zz], at.nx),
+                self.move(zz, ex, self.A, 5, self.rd.at[zz, 0], at.ny),
+                self.move(zz, ex, self.F, 6, self.rs.at[zz, 1], at.sib))
+
+    def from_y(self, zz):
+        at = self.at
+        ey = at.ny[1]
+        return (self.move(zz, ey, self.F, 3, self.ry.at[zz], at.ny),
+                self.move(zz, ey, self.B, 7, self.rd.at[zz, 1], at.nx),
+                self.move(zz, ey, self.F, 8, self.rs.at[zz, 2], at.sib))
+
+    def turned(self, zz):
+        at = self.at
+        return (self.move(zz, at.diag, self.A, 5, self.rd.at[zz, 0], at.ny),
+                self.move(zz, at.diag, self.A, 9, self.rs.at[zz, 3], at.sib),
+                self.move(zz, at.diag, self.B, 7, self.rd.at[zz, 1], at.nx),
+                self.move(zz, at.diag, self.B, 10, self.rs.at[zz, 4], at.sib))
+
+    def begin(self):
+        d = self.at.d
+
+        @pl.when(self.at.has_below)
+        def _():
+            self.down(d, True).start()
+
+        @pl.when(self.at.has_above)
+        def _():
+            self.up(d, True).start()
+
+        for copy in self.spread(d, True):
+            copy.start()
+
+    def column(self, zz):
+        d = self.at.d
+
+        @pl.when(zz < d)
+        def _():
+            self.up(zz).wait_recv()
+
+            @pl.when(self.at.has_above)
+            def _():
+                self.up(zz).start()
+
+        @pl.when(zz > d)
+        def _():
+            self.down(zz).wait_recv()
+
+            @pl.when(self.at.has_below)
+            def _():
+                self.down(zz).start()
+
+        for copy in self.spread(zz):
+            copy.start()
+
+    def plane(self, zz):
+        for arrive, turn, share in (self.from_x(zz), self.from_y(zz)):
+            arrive.wait_recv()
+            turn.start()
+            share.start()
+
+    def corner(self, zz):
+        a, share_a, b, share_b = self.turned(zz)
+        a.wait_recv()
+        share_a.start()
+        b.wait_recv()
+        share_b.start()
+
+    def siblings(self):
+        at = self.at
+        es = at.sib[1]
+        exs, eys, exys = es + at.nx[1] - at.e, es + at.ny[1] - at.e, es + at.diag - at.e
+
+        @pl.loop(0, at.n)
+        def _(zz):
+            for e, cols, k in ((es, self.F, 0), (exs, self.F, 1), (eys, self.F, 2), (exys, self.A, 3), (exys, self.B, 4)):
+                self.move(zz, e, cols, 4, self.rs.at[zz, k], at.sib).wait_recv()
+
+    def finish(self):
+        d = self.at.d
+
+        @pl.loop(0, self.at.n)
+        def _(zz):
+            for group in (self.spread(zz), self.from_x(zz)[1:], self.from_y(zz)[1:], self.turned(zz)[1::2]):
+                for copy in group:
+                    copy.wait_send()
+
+            @pl.when((d > 0) & (zz >= d))
+            def _():
+                self.down(zz).wait_send()
+
+            @pl.when(self.at.has_above & (zz <= d))
+            def _():
+                self.up(zz).wait_send()
+
+
+def lane_tile(rows):
+    return lax.broadcasted_iota(jnp.int32, (rows, 128), 1)
+
+
+def swap_halves(tile):
+    front = lax.rem(lane_tile(tile.shape[0]), HEAD) < HEAD // 2
+    return jnp.where(front, pltpu.roll(tile, 128 - HEAD // 2, 1), pltpu.roll(tile, HEAD // 2, 1))
+
+
+def inverse_rms(v):
+    return lax.rsqrt(jnp.mean(v * v, axis=1, keepdims=True) + norm_eps)
+
+
+def forward_kernel(n, experts, tok_ref, cot_ref, dense_ref, ein_ref, cos_ref, sin_ref, allowed_ref, chosen_ref,
+                   w_all, cot_all, up_all, disp_ref, mid_ref, gates_ref, gain_ref, nf_ref, q_ref, k_ref, v_ref, p_ref, mixed_ref,
+                   wv, *rest):
+    f32, bf16 = jnp.float32, jnp.bfloat16
+    at = Place(n)
+    d = at.d
+    dense = GatherAll(at, dense_ref, wv, *rest[:6])
+    cot = Gather(at, cot_ref, cot_all, *rest[6:11])
+    load_sem, part_sem, a2a_ss, a2a_sr = rest[11:]
+    q_width, k_width = HEADS * HEAD, KV_HEADS * HEAD
+    groups = HEADS // KV_HEADS
+    held, share = ein_ref.shape[:2]
+    f = FF // n
+    loads = [
+        pltpu.make_async_copy(dense_ref, wv.at[d * 8 + at.e], load_sem.at[0]),
+        pltpu.make_async_copy(cot_ref, cot_all.at[d, 0], load_sem.at[1]),
+    ]
+    for load in loads:
+        load.start()
+
+    def piece(j, to):
+        src = ein_ref.at[j // 2, :, pl.ds(pl.multiple_of((j % 2) * FF + to * f, 128), f)]
+        dst = up_all.at[pl.ds(pl.multiple_of(d * share, share), share), pl.ds(j * f, f)]
+        return src, dst
+
+    own_pieces = [pltpu.make_async_copy(*piece(j, d), part_sem.at[j]) for j in range(2 * held)]
+
+    def exchange(k, j):
+        to = lax.rem(d + k, n)
+        src, dst = piece(j, to)
+        return send(src, dst, a2a_ss.at[k, j], a2a_sr.at[d, j], (to, at.e))
+
+    at.meet(True)
+    dense.begin()
+    for i in range(1, n):
+        dense.column(at.near(i))
+        if i == n - 1:
+            cot.begin_z()
+        dense.plane(at.near(i - 1))
+        if i >= 2:
+            dense.corner(at.near(i - 2))
+    cot.begin_xy()
+    dense.plane(at.near(n - 1))
+    if n > 1:
+        dense.corner(at.near(n - 2))
+        cot.column_z(at.near(1))
+    dense.corner(at.near(n - 1))
+    for i in range(2, n):
+        cot.column_z(at.near(i))
+    for piece_copy in own_pieces:
+        piece_copy.start()
+    for k in range(1, n):
+        for j in range(2 * held):
+            exchange(k, j).start()
+    for load in loads:
+        load.wait()
+    dense.siblings()
+    keep = pltpu.make_async_copy(wv, w_all, load_sem.at[0])
+    keep.start()
+
+    def weight(lo, width):
+        return wv[:, :, lo : lo + width].reshape(D, width)
+
+    tail_at = q_width + 2 * k_width + D
+    turned = jnp.transpose(weight(tail_at, 128).astype(f32))
+    gain_ref[0:1, :] = turned[experts : experts + 1, :]
+    gain_ref[1:2, :] = turned[experts + 1 : experts + 2, :]
+    x = tok_ref[...].astype(f32)
+    nf_ref[...] = (x * inverse_rms(x) * gain_ref[0:1, :]).astype(bf16)
+    cos, sin = cos_ref[...], sin_ref[...]
+    for q in range((q_width + 2 * k_width) // 512):
+        lo = q * 512
+        part = mm(nf_ref[...], weight(lo, 512))
+        for t in range(4):
+            tile = part[:, t * 128 : (t + 1) * 128]
+            col = lo + t * 128
+            if col < q_width + k_width:
+                tile = tile * cos + swap_halves(tile) * sin
+            ref, base = (q_ref, 0) if col < q_width else (k_ref, q_width) if col < q_width + k_width else (v_ref, q_width + k_width)
+            ref[:, col - base : col - base + 128] = tile.astype(bf16)
+    cot.plane(at.near(0))
+    if n > 1:
+        cot.column_xy(at.near(1))
+    allowed = jnp.concatenate([allowed_ref[...]] * groups, axis=0) > 0
+    for g in range(KV_HEADS):
+        qs = jnp.concatenate([q_ref[:, (g * groups + j) * HEAD : (g * groups + j + 1) * HEAD] for j in range(groups)], axis=0)
+        ks, vs = k_ref[:, g * HEAD : (g + 1) * HEAD], v_ref[:, g * HEAD : (g + 1) * HEAD]
+        scores = jnp.where(allowed, mm(qs, ks, NT) * HEAD ** (-0.5), neg_large)
+        raised = jnp.exp(scores - jnp.max(scores, axis=1, keepdims=True))
+        probs = raised / jnp.sum(raised, axis=1, keepdims=True)
+        p_ref[g] = probs
+        out = mm(probs.astype(bf16), vs).astype(bf16)
+        rows = out.shape[0] // groups
+        for j in range(groups):
+            mixed_ref[:, (g * groups + j) * HEAD : (g * groups + j + 1) * HEAD] = out[j * rows : (j + 1) * rows]
+    for q in range(D // 512):
+        lo = q * 512
+        mid_ref[:, lo : lo + 512] = tok_ref[:, lo : lo + 512].astype(f32) + mm(mixed_ref[...], weight(q_width + 2 * k_width + lo, 512))
+    mid = mid_ref[...]
+    disp_ref[:, :D] = (mid * inverse_rms(mid) * gain_ref[1:2, :]).astype(bf16)
+    logits = mm(disp_ref[:, :D], weight(tail_at, 128))
+    chosen = chosen_ref[...]
+    masked = jnp.where(chosen > 0, logits, neg_large)
+    raised = jnp.where(chosen > 0, jnp.exp(masked - jnp.max(masked, axis=1, keepdims=True)), 0.0)
+    gates = raised / jnp.sum(raised, axis=1, keepdims=True)
+    gates_ref[...] = gates
+    high = gates.astype(bf16).astype(f32)
+    low = (gates - high).astype(bf16).astype(f32)
+    disp_ref[:, D:] = (high + pltpu.roll(low, experts, 1)).astype(bf16)
+
+    for i in range(1, n):
+        cot.plane(at.near(i))
+        if i + 1 < n:
+            cot.column_xy(at.near(i + 1))
+        cot.corner(at.near(i - 1))
+    cot.corner(at.near(n - 1))
+    for piece_copy in own_pieces:
+        piece_copy.wait()
+    for k in range(1, n):
+        source = lax.rem(d + k, n)
+        for j in range(2 * held):
+            exchange(k, j).wait_send()
+            src, _ = piece(j, d)
+            dst = up_all.at[pl.ds(pl.multiple_of(source * share, share), share), pl.ds(j * f, f)]
+            send(src, dst, a2a_ss.at[k, j], a2a_sr.at[source, j], (source, at.e)).wait_recv()
+    keep.wait()
+    dense.finish()
+    cot.finish()
+
+
+def forward_layer(tok, cot, dense, ein, cos, sin, allowed, chosen, n, experts, cid):
+    f32, bf16 = jnp.float32, jnp.bfloat16
+    rows = tok.shape[0]
+    shard, wide = dense.shape
+    held, share = ein.shape[:2]
+    q_width, k_width = HEADS * HEAD, KV_HEADS * HEAD
+    groups = HEADS // KV_HEADS
+    D_ = pltpu.SemaphoreType.DMA
+    any_, vm = pl.BlockSpec(memory_space=pl.ANY), pl.BlockSpec(memory_space=pltpu.VMEM)
+    S = jax.ShapeDtypeStruct
+    return pl.pallas_call(
+        functools.partial(forward_kernel, n, experts),
+        out_shape=(
+            S((n * 8, shard, wide), bf16), S((n, 4, rows, D), bf16), S((D, 2 * held * (FF // n)), bf16),
+            S((rows, D + 128), bf16), S((rows, D), f32), S((rows, 128), f32), S((8, D), f32), S((rows, D), bf16),
+            S((rows, q_width), bf16), S((rows, k_width), bf16), S((rows, k_width), bf16),
+            S((KV_HEADS, groups * rows, rows), f32), S((rows, q_width), bf16),
+        ),
+        in_specs=[vm, any_, any_, any_, vm, vm, vm, vm],
+        out_specs=[any_] * 3 + [vm] * 10,
+        scratch_shapes=[pltpu.VMEM((n * 8, shard, wide), bf16)]
+        + [D_((n, 11)), D_((n,)), D_((n,)), D_((n,)), D_((n, 2)), D_((n, 5))] + gather_sems(n)
+        + [D_((2,)), D_((2 * held,)), D_((n, 2 * held)), D_((n, 2 * held))],
+        compiler_params=pltpu.CompilerParams(collective_id=cid, has_side_effects=True, vmem_limit_bytes=60 << 20),
+        name="forward_layer",
+    )(tok, cot, dense, ein, cos, sin, allowed, chosen)
+
+
+def backward_kernel(n, experts, gs_ref, tok_ref, cot_ref, mid_ref, gates_ref, gain_ref, nf_ref, disp_ref, q_ref, k_ref, v_ref, p_ref,
+                    mixed_ref, cos_ref, sin_ref, w_ref, gup_ref,
+                    gtok_ref, gout_ref, gin_ref, gtail_ref, gup_out,
+                    wv, pout, pin, tot_out, tot_in, arrived, pair, gq, gl, sums, gb, gm, flat, *rest):
+    f32, bf16 = jnp.float32, jnp.bfloat16
+    at = Place(n)
+    d, c = at.d, at.c
+    outs = Reduce(at, pout, tot_out, *rest[:9])
+    ins = Reduce(at, pin, tot_in, *rest[9:18])
+    load_sem, pair_ss, pair_sr, a2a_ss, a2a_sr, end_ss, end_sr = rest[18:]
+    q_width, k_width = HEADS * HEAD, KV_HEADS * HEAD
+    groups = HEADS // KV_HEADS
+    qkv_width = q_width + 2 * k_width
+    tail_at = qkv_width + D
+    rows = tok_ref.shape[0]
+    shard = w_ref.shape[1]
+    share = D // n
+    f = FF // n
+    loads = []
+    for i, (lo, width) in enumerate(((tail_at, 128), (qkv_width, D), (0, qkv_width))):
+        loads.append(pltpu.make_async_copy(w_ref.at[:, :, pl.ds(lo, width)], wv.at[:, :, pl.ds(lo, width)], load_sem.at[i]))
+    for load in loads:
+        load.start()
+    own_share = pltpu.make_async_copy(gup_ref.at[pl.ds(pl.multiple_of(d * share, share), share), :], arrived.at[d], load_sem.at[3])
+    own_share.start()
+
+    def exchange(k):
+        to = lax.rem(d + k, n)
+        return send(gup_ref.at[pl.ds(pl.multiple_of(to * share, share), share), :], arrived.at[d], a2a_ss.at[k], a2a_sr.at[d], (to, at.e))
+
+    swaps = [send(src, pair.at[i], pair_ss.at[i], pair_sr.at[i], at.sib)
+             for i, src in enumerate((mixed_ref, nf_ref, disp_ref.at[:, pl.ds(0, D)], gb))]
+    swap_q = send(gq.at[0], gq.at[1], pair_ss.at[4], pair_sr.at[4], at.sib)
+    swap_l = send(gl.at[0], gl.at[1], pair_ss.at[5], pair_sr.at[5], at.sib)
+    swap_s = send(sums.at[0], sums.at[1], pair_ss.at[6], pair_sr.at[6], at.sib)
+    at.meet(True)
+    for i in range(3):
+        swaps[i].start()
+
+    def weight(lo, width):
+        return wv[:, :, lo : lo + width].reshape(D, width)
+
+    loads[0].wait()
+    mid = mid_ref[...]
+    inv_second = inverse_rms(mid)
+    unit = mid * inv_second
+    gates, gg = gates_ref[...], gs_ref[:, D:]
+    gl[0] = (gates * (gg - jnp.sum(gates * gg, axis=1, keepdims=True))).astype(bf16)
+    swap_l.start()
+    grad_second = mm(gl[0], weight(tail_at, 128), NT) + gs_ref[:, :D]
+    pull = grad_second * gain_ref[1:2, :]
+    sums[0, 1:2, :] = jnp.sum(grad_second * unit, axis=0, keepdims=True)
+    grad_middle = cot_ref[...].astype(f32) + inv_second * (pull - unit * jnp.mean(pull * unit, axis=1, keepdims=True))
+    gtok_ref[...] = grad_middle
+    gb[...] = grad_middle.astype(bf16)
+    swaps[3].start()
+    loads[1].wait()
+    for q in range(q_width // 512):
+        gm[:, q * 512 : (q + 1) * 512] = mm(gb[...], wv[:, :, qkv_width : qkv_width + D].reshape(D, D)[q * 512 : (q + 1) * 512], NT).astype(bf16)
+
+    def both(own, other, cols):
+        return jnp.concatenate([own[:, cols], other[:, cols]], axis=0)
+
+    def store(buf, zz, lo, value):
+        blocks = value.astype(bf16).reshape(4, 2 * shard, value.shape[1])
+        for a in range(4):
+            slot = 2 * lax.rem(a // 2 + at.y, 2) + lax.rem(a % 2 + at.x, 2)
+            buf[zz, slot, :, lo : lo + value.shape[1]] = blocks[a]
+
+    def row_cols(zz):
+        return pl.ds(pl.multiple_of(zz * share, 128), share)
+
+    half_out, half_in = D // 2, qkv_width // 2
+    swaps[0].wait_recv()
+    swaps[3].wait_recv()
+
+    @pl.loop(0, n)
+    def _(j):
+        zz = at.far(j)
+        branch = both(gb, pair.at[3], pl.ds(pl.multiple_of(c * half_out, 128), half_out))
+        store(pout, zz, 0, mm(both(mixed_ref, pair.at[0], row_cols(zz)), branch, TN))
+        outs.s1(zz)
+
+    for k in range(1, n):
+        exchange(k).start()
+    scale = HEAD ** (-0.5)
+    for g in range(KV_HEADS):
+        heads = [slice((g * groups + j) * HEAD, (g * groups + j + 1) * HEAD) for j in range(groups)]
+        kv = slice(g * HEAD, (g + 1) * HEAD)
+        qs = jnp.concatenate([q_ref[:, h] for h in heads], axis=0)
+        ms = jnp.concatenate([gm[:, h] for h in heads], axis=0)
+        ks, vs = k_ref[:, kv], v_ref[:, kv]
+        probs = p_ref[g]
+        grad_values = mm(probs.astype(bf16), ms, TN)
+        grad_probs = mm(ms, vs, NT)
+        grad_scores = (probs * (grad_probs - jnp.sum(probs * grad_probs, axis=1, keepdims=True))).astype(bf16)
+        grad_query = mm(grad_scores, ks) * scale
+        for j, h in enumerate(heads):
+            flat[:, h] = grad_query[j * rows : (j + 1) * rows]
+        flat[:, q_width + kv.start : q_width + kv.stop] = mm(grad_scores, qs, TN) * scale
+        flat[:, q_width + k_width + kv.start : q_width + k_width + kv.stop] = grad_values
+    cos, sin = cos_ref[...], sin_ref[...]
+    for t in range(qkv_width // 128):
+        tile = flat[:, t * 128 : (t + 1) * 128]
+        if t * 128 < q_width + k_width:
+            tile = tile * cos - swap_halves(tile) * sin
+        gq[0, :, t * 128 : (t + 1) * 128] = tile.astype(bf16)
+    swap_q.start()
+    loads[2].wait()
+    x = tok_ref[...].astype(f32)
+    inv_first = inverse_rms(x)
+    unit = x * inv_first
+    grad_first = jnp.concatenate(
+        [mm(gq[0], wv[8 * i : 8 * (i + 1), :, :qkv_width].reshape(8 * shard, qkv_width), NT) for i in range(n)], axis=1)
+    pull = grad_first * gain_ref[0:1, :]
+    sums[0, 0:1, :] = jnp.sum(grad_first * unit, axis=0, keepdims=True)
+    sums[0, 2:, :] = jnp.zeros((6, D), f32)
+    swap_s.start()
+    gtok_ref[...] += inv_first * (pull - unit * jnp.mean(pull * unit, axis=1, keepdims=True))
+    for i in (1, 2):
+        swaps[i].wait_recv()
+    swap_l.wait_recv()
+    swap_q.wait_recv()
+    swap_s.wait_recv()
+    gains = sums[0] + sums[1]
+    high = gains.astype(bf16)
+    low = (gains - high.astype(f32)).astype(bf16)
+    swap_s.wait_send()
+    sums[0] = high.astype(f32)
+    sums[1] = low.astype(f32)
+    line = lax.rem(lax.broadcasted_iota(jnp.int32, (16, 128), 0), 8)
+    where = (((line == 0) & (lane_tile(16) == experts)) | ((line == 1) & (lane_tile(16) == experts + 1))).astype(bf16)
+
+    @pl.loop(0, n)
+    def _(j):
+        zz = at.far(j)
+        cols = row_cols(zz)
+        normed = both(nf_ref, pair.at[1], cols)
+        for q in range(2):
+            part = pl.ds(pl.multiple_of(c * half_in + q * (half_in // 2), 128), half_in // 2)
+            grad = jnp.concatenate([gq[0, :, part], gq[1, :, part]], axis=0)
+            store(pin, zz, q * (half_in // 2), mm(normed, grad, TN))
+        tail = mm(both(disp_ref, pair.at[2], cols), jnp.concatenate([gl[0], gl[1]], axis=0), TN)
+        rows_now = jnp.concatenate([sums[0, :, cols], sums[1, :, cols]], axis=0).astype(bf16)
+        store(pin, zz, half_in, tail + mm(rows_now, where, TN))
+        ins.s1(zz)
+
+        outs.s2(zz)
+
+    for j in range(n + 1):
+        if j < n:
+            outs.s3(at.far(j))
+            if j < n - 1:
+                outs.line(at.far(j))
+            ins.s2(at.far(j))
+        if j >= 1:
+            ins.s3(at.far(j - 1))
+            if j - 1 < n - 1:
+                ins.line(at.far(j - 1))
+    outs.last()
+    mine, theirs = pl.ds(pl.multiple_of(c * shard, 8), shard), pl.ds(pl.multiple_of((1 - c) * shard, 8), shard)
+    cols_out, cols_in = pl.ds(pl.multiple_of(c * half_out, 128), half_out), pl.ds(pl.multiple_of(c * half_in, 128), half_in)
+    end_out = send(tot_out.at[theirs, :], gout_ref.at[:, cols_out], end_ss.at[0], end_sr.at[0], at.sib)
+    end_out.start()
+    gout_ref[:, cols_out] = tot_out[mine, :]
+    ins.last()
+    end_in = send(tot_in.at[theirs, pl.ds(0, half_in)], gin_ref.at[:, cols_in], end_ss.at[1], end_sr.at[1], at.sib)
+    end_in.start()
+    gin_ref[:, cols_in] = tot_in[mine, :half_in]
+    gtail_ref[...] = tot_in[mine, half_in:]
+    own_share.wait()
+    for k in range(1, n):
+        exchange(k).wait_send()
+        source = lax.rem(d + k, n)
+        send(gup_ref.at[pl.ds(0, share), :], arrived.at[source], a2a_ss.at[k], a2a_sr.at[source], (source, at.e)).wait_recv()
+
+    @pl.loop(0, share // 32)
+    def _(r):
+        w = pl.ds(pl.multiple_of(r * 32, 32), 32)
+        for q in range(n):
+            for j in range(arrived.shape[2] // f):
+                lo = (j % 2) * FF + q * f
+                gup_out[j // 2, w, lo : lo + f] = arrived[q, w, j * f : (j + 1) * f].astype(f32)
+
+    end_out.wait()
+    end_in.wait()
+    for swap in swaps + [swap_q, swap_l]:
+        swap.wait_send()
+    outs.finish()
+    ins.finish()
+
+
+def backward_layer(gs, tok, cot, mid, gates, gain, nf, disp, q, k, v, p, mixed, cos, sin, w_all, gup, held, n, experts, cid):
+    f32, bf16 = jnp.float32, jnp.bfloat16
+    rows = tok.shape[0]
+    shard, wide = w_all.shape[1:]
+    qkv_width = (HEADS + 2 * KV_HEADS) * HEAD
+    share = D // n
+    D_ = pltpu.SemaphoreType.DMA
+    V = lambda *s: pltpu.VMEM(s, bf16)
+    W = lambda *s: pltpu.VMEM(s, f32)
+    any_, vm = pl.BlockSpec(memory_space=pl.ANY), pl.BlockSpec(memory_space=pltpu.VMEM)
+    S = jax.ShapeDtypeStruct
+    width_out, width_in = D // 2, qkv_width // 2 + 128
+    return pl.pallas_call(
+        functools.partial(backward_kernel, n, experts),
+        out_shape=(S((rows, D), f32), S((shard, D), f32), S((shard, qkv_width), f32), S((shard, 128), f32), S((held, share, 2 * FF), f32)),
+        in_specs=[vm] * 15 + [any_, any_],
+        out_specs=[vm] * 5,
+        scratch_shapes=[V(n * 8, shard, wide), V(n, 4, 2 * shard, width_out), V(n, 4, 2 * shard, width_in),
+                        W(2 * shard, width_out), W(2 * shard, width_in), V(n, share, gup.shape[1]),
+                        V(4, rows, D), V(2, rows, qkv_width), V(2, rows, 128), W(2, 8, D), V(rows, D), V(rows, D), W(rows, qkv_width)]
+        + reduce_scratch(n, 2 * shard, width_out) + reduce_scratch(n, 2 * shard, width_in)
+        + [D_((4,)), D_((7,)), D_((7,)), D_((n,)), D_((n,)), D_((2,)), D_((2,))],
+        compiler_params=pltpu.CompilerParams(collective_id=cid, has_side_effects=True, vmem_limit_bytes=62 << 20),
+        name="backward_layer",
+    )(gs, tok, cot, mid, gates, gain, nf, disp, q, k, v, p, mixed, cos, sin, w_all, gup)
+
+
+def per_device_fast(n, tokens, segments, routes, cotangent, gain_attn, attn_in, attn_out, gain_ffn, router, expert_in, expert_out):
+    f32, bf16 = jnp.float32, jnp.bfloat16
+    micro, rows = tokens.shape[:2]
+    total = micro * rows
+    held = expert_in.shape[0]
+    experts = held * 8
+    f = FF // n
+    shard = attn_in.shape[0]
+    x = tokens.reshape(total, D)
+    cot = cotangent.reshape(total, D)
+    tail = jnp.concatenate([router, gain_attn[:, None], gain_ffn[:, None], jnp.zeros((shard, 126 - experts), bf16)], axis=1)
+    dense = jnp.concatenate([attn_in, attn_out, tail], axis=1)
+
+    segment = (segments[:, 0, :] + 2 * rows * jnp.arange(micro, dtype=jnp.int32)[:, None]).reshape(total)
+    cosine, sine_table, causal = rope_tables(segment, HEAD // 2)
+    cos = jnp.tile(cosine, (1, 128 * 2 // HEAD))
+    sin = jnp.tile(jnp.concatenate([-sine_table, sine_table], axis=1), (1, 128 // HEAD))
+    route = routes.reshape(total, TOP_K)
+    chosen = jnp.any(route[:, :, None] == jnp.arange(128, dtype=jnp.int32)[None, None, :], axis=1).astype(f32)
+    w_all, cot_all, up, disp, middle, gates, gain, nf, q, k, v, p, mixed = forward_layer(
+        x, cot, dense, expert_in, cos, sin, causal.astype(f32), chosen, n, experts, 0)
+
+    mine = lax.axis_index("expert")
+    order = jnp.stack([mine, mine + 1 - 2 * lax.rem(mine, 2)])
+    owner = (order[:, None] * held + jnp.arange(held, dtype=jnp.int32)[None, :]).reshape(-1)
+    owner = jnp.repeat(owner, f)[None, :]
+    lane = jnp.arange(128, dtype=jnp.int32)[:, None]
+    pick = ((lane == owner) | (lane == owner + experts)).astype(bf16)
+    place = (lane == owner).astype(bf16).T
+    out, grad_sum, grad_up, grad_down = expert_layer(
+        disp, cot_all, up, expert_out.reshape(held * f, D), pick, place, middle, n, 1)
+    grad_tokens, grad_out, grad_in, grad_tail, grad_up = backward_layer(
+        grad_sum, x, cot, middle, gates, gain, nf, disp, q, k, v, p, mixed, cos, sin, w_all, grad_up, held, n, experts, 2)
+    return (
+        out.astype(bf16).reshape(micro, rows, D),
+        grad_tokens.reshape(micro, rows, D),
+        grad_tail[:, experts],
+        grad_in,
+        grad_out,
+        grad_tail[:, experts + 1],
+        grad_tail[:, :experts],
+        grad_up,
+        grad_down.reshape(held, f, D),
+    )
+
+
 def solution(mesh):
     placed = (
         P(None, ("dp", "expert"), None),
@@ -415,8 +1477,10 @@
         P("expert", "dp", None),
         P("expert", "dp", None),
     )
+    fast = mesh.shape["expert"] == 8 and FF // mesh.shape["dp"] == 128
+    body = functools.partial(per_device_fast, mesh.shape["dp"]) if fast else per_device
     return jax.shard_map(
-        per_device,
+        body,
         mesh=mesh,
         in_specs=placed,
         out_specs=(

time: 1660 us -> 459 us (0.28)
  waiting for transfers between devices: 1100 us -> 0 us
  Pallas kernels: 0 us -> 428 us
  blocking collectives: 203 us -> 0 us
  matrix products: 163 us -> 0 us
  other arithmetic: 51.6 us -> 5.89 us
  starting transfers between devices: 44.3 us -> 0 us
  local copies, waits for them, and re-layouts: 60.9 us -> 20.6 us
    reduce_scatter x4 -> x0, waiting for transfers between devices: 729 us -> none  [the longest x1 315 us: expert_reduce(): lax.psum_scatter(grad_set[0], 'dp', scatter_dimension=1, tiled=True)]
    pallas_call x0 -> x3, Pallas kernels: none -> 428 us  [the longest x1 210 us: expert_layer(): pl.pallas_call(functools.partial(expert_kernel, n), out_shape=(jax.ShapeD...]
    all_gather x4 -> x0, waiting for transfers between devices: 309 us -> none  [the longest x1 139 us: expert_fetch(): lax.all_gather(expert_in, 'dp', axis=1, tiled=True)]
    dot_general x46 -> x0, matrix products: 163 us -> none  [the longest x2 27.5 us: backward_micro(): jnp.einsum('secd,secf->edf', received, grad_gate_up, preferred_element_ty...]
    unnamed x2 -> x0, blocking collectives: 84.2 us -> none
    all_to_all x2 -> x0, blocking collectives: 64.2 us -> none  [the longest x1 32.2 us: backward_micro(): lax.all_to_all(grad_buffer, 'expert', split_axis=0, concat_axis=0, tiled=...]
    all_to_all x6 -> x0, waiting for transfers between devices: 63.3 us -> none  [the longest x2 25.7 us: backward_micro(): lax.all_to_all(grad_rows, 'expert', split_axis=0, concat_axis=0, tiled=True)]
    all_gather x1 -> x0, blocking collectives: 54.2 us -> none  [dense_fetch(): lax.all_gather(router, ('dp', 'expert'), axis=0, tiled=True)]
  transfers between devices with their start and end apart: 15 -> 0, of which waited for: 12 -> 0; matrix products, arithmetic and copies ran while one was open for 12% -> 0% of each run, Pallas kernels for 0% -> 0%
where the time goes in v3:
time: 459 us; the launch traced here: 455 us
  Pallas kernels  428 us (93%)
  local copies, waits for them, and re-layouts  20.6 us (4%)
  other arithmetic  5.89 us (1%)
    pallas_call x1, Pallas kernels, expert_layer(): pl.pallas_call(functools.partial(expert_kernel, n), out_shape=(jax.ShapeD...  210 us
    pallas_call x1, Pallas kernels, forward_layer(): pl.pallas_call(functools.partial(forward_kernel, n, experts), out_shape=(...  125 us
    pallas_call x1, Pallas kernels, backward_layer(): pl.pallas_call(functools.partial(backward_kernel, n, experts), out_shape=...  92.4 us
    unnamed x16, local copies, waits for them, and re-layouts  13.1 us

profile of v3, /device:TPU:11, one launch (start us, length us, event | category | flops | bytes accessed | tf_op | source)
XLA Modules:
  0.0 455.5 jit_solution(5651929876503231890)
XLA Ops:
  0.6 0.1 add_multiply_fusion
  0.7 0.5 broadcast.73
  1.2 1.3 reduce.7
  2.6 0.1 squeeze.9
  2.7 0.1 iota_add_fusion
  2.7 0.1 add.56
  2.8 0.1 add.49
  2.9 0.1 add.50
  3.0 0.2 fusion.4
  3.2 0.1 broadcast_bitcast_fusion
  3.3 0.1 bitcast_add_fusion
  3.3 0.8 copy.35
  4.1 0.8 copy.36
  4.8 0.8 copy.34
  5.6 0.1 fusion.6
  5.8 0.7 copy.40.sin_ref
  6.5 0.7 fusion.5.allowed_ref
  7.3 0.7 copy.39.cos_ref
  8.0 0.8 copy.44
  8.8 0.3 fusion
  9.0 0.6 convert_element_type.25.chosen_ref
  9.7 0.7 fusion.2.pick_ref
  10.4 0.8 fusion.3.place_ref
  11.3 1.9 concatenate.10.dense_ref
  13.1 125.4 %forward_layer.1 = (bf16[32,48,4224]{2,1,0:T(8,128)(2,1)}, bf16[4,4,128,1536]{3,2,1,0:T(8,128)(2,1)}, bf16[1536,768]{1,0:T(8,128)(2,1)}, bf16[128,1664]{1,0:T(8,...) custom-call(bf16[128,1536]{1,0:T(8,128)(2,1)} %bitcast.18, ...), custom_call_target="tpu_custom_call" | custom-call | tf_op jit(solution)/shard_map/forward_layer/pallas_call | solution.py:1183
  138.5 210.4 %expert_layer.1 = (f32[128,1536]{1,0:T(8,128)}, f32[128,1664]{1,0:T(8,128)}, bf16[1536,768]{1,0:T(8,128)(2,1)}, f32[384,1536]{1,0:T(8,128)}) custom-call(bf16[128,1664]{1,0:T(8,128)(2,1)} %get-tuple-element.31.x_ref.disp_ref, bf16[4,4,128,1536]{3,2,1,0:T(8,128)(2,1)} %get-tuple-element.32.cot_ref, bf16[1536,768]{1,0:T(8,128)(2,1)} %get-tuple-element.33.up_ref, ...), custom_call_target="tpu_custom_call" | custom-call | tf_op jit(solution)/shard_map/expert_layer/pallas_call | solution.py:889
  349.0 0.0 copy-start.1
  349.0 92.4 %backward_layer.1 = (f32[128,1536]{1,0:T(8,128)}, f32[48,1536]{1,0:T(8,128)}, f32[48,2560]{1,0:T(8,128)}, f32[48,128]{1,0:T(8,128)}, f32[3,384,1024]{2,1,0:T(8,128)}) custom-call(f32[128,1664]{1,0:T(8,128)} %get-tuple-element.36.gs_ref, bf16[128,1536]{1,0:T(8,128)(2,1)} %bitcast.19, bf16[128,1536]{1,0:T(8,128)(2,1)} %bitcast.21, ...), custom_call_target="tpu_custom_call" | custom-call | tf_op jit(solution)/shard_map/backward_layer/pallas_call | solution.py:1405
  441.3 0.0 copy-start.2
  441.4 0.0 copy-start.3
  441.4 0.0 copy-done.1
  441.4 0.8 convert_element_type.28
  442.2 1.5 slice_reduce_fusion
  443.7 1.4 copy.43
  445.1 2.1 copy.51
  447.2 0.0 copy-done.2
  447.2 0.8 copy.52
  447.9 0.0 copy-done.3
  447.9 0.7 copy.53
  448.7 0.0 copy-start
  448.7 5.4 %copy.54 = f32[3,384,1024]{2,1,0:T(8,128)} copy(f32[3,384,1024]{2,1,0:T(8,128)} %get-tuple-element.101) | data formatting | bytes 9437184
  454.1 0.0 copy-done
  454.1 1.4 copy.55
  (8 shorter events, 0.0 us)
Async XLA Ops:
  349.0 92.4 %copy-start.1 = (f32[128,1536]{1,0:T(8,128)S(1)}, f32[128,1536]{1,0:T(8,128)}, u32[]{:S(2)}) copy-start(f32[128,1536]{1,0:T(8,128)} %get-tuple-element.35) | copy-start | bytes 2359300
  441.3 5.8 %copy-start.2 = (f32[48,2560]{1,0:T(8,128)S(1)}, f32[48,2560]{1,0:T(8,128)}, u32[]{:S(2)}) copy-start(f32[48,2560]{1,0:T(8,128)} %get-tuple-element.97) | copy-start | bytes 1474564
  441.4 6.6 %copy-start.3 = (f32[48,1536]{1,0:T(8,128)S(1)}, f32[48,1536]{1,0:T(8,128)}, u32[]{:S(2)}) copy-start(f32[48,1536]{1,0:T(8,128)} %get-tuple-element.98) | copy-start | bytes 884740
  448.7 5.4 %copy-start = (f32[384,1536]{1,0:T(8,128)S(1)}, f32[384,1536]{1,0:T(8,128)}, u32[]{:S(2)}) copy-start(f32[384,1536]{1,0:T(8,128)} %get-tuple-element.52) | copy-start | bytes 7077892

commit v4 on v3

--- a/solution.py
+++ b/solution.py
@@ -617,20 +617,46 @@
         return send(self.buf.at[0, 0], self.rz.at[slot], self.sems[4].at[0], self.sems[5].at[slot], self.at.nx)
 
     def s1(self, zz):
-        for k in range(4):
-            self.first(zz, k).start()
-
-    def s2(self, zz):
+        self.corners(zz)
+        self.sides(zz)
+
+    def corners(self, zz):
+        self.first(zz, 0).start()
+        self.first(zz, 1).start()
+
+    def sides(self, zz):
+        self.first(zz, 2).start()
+        self.first(zz, 3).start()
+
+    def turn(self, zz):
         self.first(zz, 0).wait_recv()
         add_rows(self.buf.at[zz, 2, self.A], self.r1.at[zz, 0])
         self.second(zz, 0).start()
         self.first(zz, 1).wait_recv()
         add_rows(self.buf.at[zz, 1, self.B], self.r1.at[zz, 1])
         self.second(zz, 1).start()
+
+    def take_sides(self, zz):
         self.first(zz, 2).wait_recv()
         add_rows(self.buf.at[zz, 0, self.A], self.r1.at[zz, 2])
         self.first(zz, 3).wait_recv()
         add_rows(self.buf.at[zz, 0, self.B], self.r1.at[zz, 3])
+
+    def s2(self, zz):
+        self.turn(zz)
+        self.take_sides(zz)
+
+    def step(self, j):
+        at = self.at
+        if j < at.n:
+            self.turn(at.far(j))
+            self.sides(at.far(j))
+            if j + 2 < at.n:
+                self.corners(at.far(j + 2))
+        if j >= 1:
+            self.take_sides(at.far(j - 1))
+            self.s3(at.far(j - 1))
+            self.lines(j - 1)
 
     def s3(self, zz):
         self.second(zz, 0).wait_recv()
@@ -638,21 +664,41 @@
         self.second(zz, 1).wait_recv()
         add_rows(self.buf.at[zz, 0, self.B], self.r2.at[zz, 1])
 
-    def line(self, zz):
+    def push(self, zz):
         d = self.at.d
 
-        @pl.when(((zz < d) & self.at.has_above) | ((zz > d) & self.at.has_below))
+        @pl.when(zz < d)
+        def _():
+            self.down(zz).start()
+
+        @pl.when(zz > d)
+        def _():
+            self.up(zz).start()
+
+    def line_head(self, zz):
+        @pl.when(jnp.logical_not(self.passes(zz)))
+        def _():
+            self.push(zz)
+
+    def passes(self, zz):
+        d = self.at.d
+        return ((zz < d) & self.at.has_above) | ((zz > d) & self.at.has_below)
+
+    def line_rest(self, zz):
+        @pl.when(self.passes(zz))
         def _():
             self.arrive(zz).wait_recv()
             add_rows(self.buf.at[zz, 0], self.rz.at[zz])
-
-        @pl.when(zz < d)
-        def _():
-            self.down(zz).start()
-
-        @pl.when(zz > d)
-        def _():
-            self.up(zz).start()
+            self.push(zz)
+
+    def lines(self, j):
+        n = self.at.n
+        if j < n - 1:
+            self.line_head(self.at.far(j))
+        if 0 <= j - 1 < n - 2:
+            self.line_rest(self.at.far(j - 1))
+        if j == n - 2:
+            self.line_rest(self.at.far(j))
 
     def last(self):
         d, n, rows, step = self.at.d, self.at.n, self.total.shape[0], 16
@@ -706,9 +752,9 @@
             D_((n, 4)), D_((n, 4)), D_((n, 2)), D_((n, 2)), D_((n,)), D_((n + 1,))]
 
 
-def expert_kernel(n, x_ref, cot_ref, up_ref, down_ref, pick_ref, place_ref, mid_ref,
+def expert_kernel(n, experts, x_ref, cot_ref, up_ref, down_ref, mid_ref,
                   out_ref, gx_ref, gup_ref, gdown_ref,
-                  xb, cb, gg, mixed, gb, wup, wdown, *rest):
+                  xb, cb, gg, mixed, gb, wup, wdown, pick_ref, place_ref, *rest):
     f32, bf16 = jnp.float32, jnp.bfloat16
     at = Place(n)
     d = at.d
@@ -736,12 +782,18 @@
     ]
     for swap in swaps:
         swap.start()
+    for h, owner in ((0, at.e), (1, at.sib[1])):
+        for j in range(held):
+            expert, cols = owner * held + j, slice((h * held + j) * 128, (h * held + j + 1) * 128)
+            gate_row = lax.broadcasted_iota(jnp.int32, (128, 128), 0)
+            pick_ref[:, cols] = ((gate_row == expert) | (gate_row == expert + experts)).astype(bf16)
+            place_ref[cols, :] = (lane_tile(128) == expert).astype(bf16)
+    gather.plane(at.near(0))
+    gather.column(at.near(1))
     for load in loads:
         load.wait()
     for swap in swaps:
         swap.wait_recv()
-    gather.plane(at.near(0))
-    gather.column(at.near(1))
 
     def tokens(ref, zz, p, lo, width):
         return ref[zz, pl.ds(2 * p, 2), :, pl.ds(lo, width)].reshape(2 * rows, width)
@@ -785,13 +837,13 @@
         zz = at.near(i)
         half(zz, 0)
 
+        @pl.when(i + 2 < n)
+        def _():
+            gather.column(at.near(i + 2))
+
         @pl.when(i + 1 < n)
         def _():
             gather.plane(at.near(i + 1))
-
-        @pl.when(i + 2 < n)
-        def _():
-            gather.column(at.near(i + 2))
 
         gather.corner(zz)
         half(zz, 1)
@@ -804,6 +856,7 @@
         @pl.when(i >= 2)
         def _():
             grads.s3(at.near(i - 2))
+            grads.line_head(at.near(i - 2))
 
     pl.semaphore_signal(free.at[0], inc=1, device_id=at.sib, device_id_type=MESH)
 
@@ -842,32 +895,28 @@
     up_swap.start()
     grads.s2(at.near(n - 1))
     grads.s3(at.near(n - 2))
+    grads.line_head(at.near(n - 2))
     up_swap.wait_recv()
     grad_up(0, True)
     keep = pltpu.make_async_copy(wup.at[0], gup_ref, load_sem.at[0])
     keep.start()
     grads.s3(at.near(n - 1))
-    for j in range(n + 3):
+    grads.line_head(at.near(n - 1))
+    for j in range(n):
+        output(at.far(j))
+        if j < 2:
+            outs.corners(at.far(j))
+    pl.semaphore_signal(free.at[1], inc=1, device_id=at.sib, device_id_type=MESH)
+    grad_down(1)
+    pl.semaphore_wait(free.at[1], 1)
+    down_swap = send(wdown.at[1], wdown.at[0], core_ss.at[3], core_sr.at[3], at.sib)
+    down_swap.start()
+    for j in range(n + 1):
+        outs.step(j)
         if j < n - 1:
-            grads.line(at.far(j))
-        if j < n:
-            output(at.far(j))
-            outs.s1(at.far(j))
-        if 0 <= j - 1 < n:
-            outs.s2(at.far(j - 1))
-        if 0 <= j - 2 < n:
-            outs.s3(at.far(j - 2))
-            if j - 2 < n - 1:
-                outs.line(at.far(j - 2))
-        if j == n - 1:
-            pl.semaphore_signal(free.at[1], inc=1, device_id=at.sib, device_id_type=MESH)
-            grad_down(1)
-            pl.semaphore_wait(free.at[1], 1)
-            down_swap = send(wdown.at[1], wdown.at[0], core_ss.at[3], core_sr.at[3], at.sib)
-            down_swap.start()
-        if j == n:
-            down_swap.wait_recv()
-            grad_down(0)
+            grads.line_rest(at.far(j))
+    down_swap.wait_recv()
+    grad_down(0)
     grads.last()
     outs.last()
     keep.wait()
@@ -878,7 +927,7 @@
     outs.finish()
 
 
-def expert_layer(x, cot_all, up, down, pick, place, middle, n, cid):
+def expert_layer(x, cot_all, up, down, middle, n, experts, cid):
     rows, wide = x.shape
     f2 = up.shape[1]
     f = f2 // 2
@@ -887,22 +936,22 @@
     D_ = pltpu.SemaphoreType.DMA
     any_, vm = pl.BlockSpec(memory_space=pl.ANY), pl.BlockSpec(memory_space=pltpu.VMEM)
     return pl.pallas_call(
-        functools.partial(expert_kernel, n),
+        functools.partial(expert_kernel, n, experts),
         out_shape=(
             jax.ShapeDtypeStruct((rows, D), jnp.float32),
             jax.ShapeDtypeStruct((rows, wide), jnp.float32),
             jax.ShapeDtypeStruct((D, f2), bf16),
             jax.ShapeDtypeStruct((f, D), jnp.float32),
         ),
-        in_specs=[any_, any_, any_, any_, vm, vm, vm],
+        in_specs=[any_, any_, any_, any_, vm],
         out_specs=[vm, vm, any_, vm],
         scratch_shapes=[V(n, 4, rows, wide), V(n, 4, rows, D), V(n, 4, rows, 2 * f2), V(n, 4, rows, 2 * f), V(n, 4, rows, wide),
-                        V(2, D, f2), V(2, f, D)]
+                        V(2, D, f2), V(2, f, D), V(128, 2 * f), V(2 * f, 128)]
         + gather_sems(n) + reduce_scratch(n, rows, wide) + reduce_scratch(n, rows, D)
         + [D_((4,)), D_((4,)), D_((4,)), pltpu.SemaphoreType.REGULAR((2,))],
         compiler_params=pltpu.CompilerParams(collective_id=cid, has_side_effects=True, vmem_limit_bytes=63 << 20),
         name="expert_layer",
-    )(x, cot_all, up, down, pick, place, middle)
+    )(x, cot_all, up, down, middle)
 
 
 class GatherAll:
@@ -1040,19 +1089,41 @@
     return lax.rsqrt(jnp.mean(v * v, axis=1, keepdims=True) + norm_eps)
 
 
-def forward_kernel(n, experts, tok_ref, cot_ref, dense_ref, ein_ref, cos_ref, sin_ref, allowed_ref, chosen_ref,
-                   w_all, cot_all, up_all, disp_ref, mid_ref, gates_ref, gain_ref, nf_ref, q_ref, k_ref, v_ref, p_ref, mixed_ref,
-                   wv, *rest):
+def rope_lanes(seg_ref, freq_ref, cos_ref, sin_ref):
+    f32 = jnp.float32
+    packs, rows = seg_ref.shape[0], seg_ref.shape[2]
+    row = jnp.concatenate([seg_ref[i].astype(f32) + float(2 * rows * i) for i in range(packs)], axis=1)
+    total = packs * rows
+    across = jnp.broadcast_to(row, (total, total))
+    same = across == jnp.transpose(across)
+    source = lax.broadcasted_iota(jnp.int32, (total, total), 1)
+    target = lax.broadcasted_iota(jnp.int32, (total, total), 0)
+    start = jnp.min(jnp.where(same, source.astype(f32), float(total)), axis=1, keepdims=True)
+    angle = (target.astype(f32) - start) * freq_ref[...]
+    cos_ref[...] = jnp.cos(angle)
+    front = lax.rem(source, HEAD) < HEAD // 2
+    sine = jnp.sin(angle)
+    sin_ref[...] = jnp.where(front, -sine, sine)
+    return (same & (source <= target)).astype(f32)
+
+
+def forward_kernel(n, experts, tok_ref, cot_ref, qkv_ref, proj_ref, tail_ref, ein_ref, seg_ref, route_ref, freq_ref,
+                   w_all, cot_all, up_all, disp_ref, mid_ref, gates_ref, gain_ref, nf_ref, q_ref, k_ref, v_ref, p_ref, mixed_ref, cos_ref, sin_ref,
+                   wv, pieces, dense_ref, *rest):
     f32, bf16 = jnp.float32, jnp.bfloat16
     at = Place(n)
     d = at.d
     dense = GatherAll(at, dense_ref, wv, *rest[:6])
     cot = Gather(at, cot_ref, cot_all, *rest[6:11])
-    load_sem, part_sem, a2a_ss, a2a_sr = rest[11:]
+    load_sem, a2a_ss, a2a_sr = rest[11:]
     q_width, k_width = HEADS * HEAD, KV_HEADS * HEAD
     groups = HEADS // KV_HEADS
     held, share = ein_ref.shape[:2]
     f = FF // n
+    qkv_width = q_width + 2 * k_width
+    dense_ref[:, :qkv_width] = qkv_ref[...]
+    dense_ref[:, qkv_width : qkv_width + D] = proj_ref[...]
+    dense_ref[:, qkv_width + D :] = tail_ref[...]
     loads = [
         pltpu.make_async_copy(dense_ref, wv.at[d * 8 + at.e], load_sem.at[0]),
         pltpu.make_async_copy(cot_ref, cot_all.at[d, 0], load_sem.at[1]),
@@ -1060,24 +1131,29 @@
     for load in loads:
         load.start()
 
-    def piece(j, to):
-        src = ein_ref.at[j // 2, :, pl.ds(pl.multiple_of((j % 2) * FF + to * f, 128), f)]
-        dst = up_all.at[pl.ds(pl.multiple_of(d * share, share), share), pl.ds(j * f, f)]
-        return src, dst
-
-    own_pieces = [pltpu.make_async_copy(*piece(j, d), part_sem.at[j]) for j in range(2 * held)]
-
-    def exchange(k, j):
+    def rows_of(z):
+        return up_all.at[pl.ds(pl.multiple_of(z * share, share), share), :]
+
+    own_piece = pltpu.make_async_copy(pieces.at[d], rows_of(d), load_sem.at[2])
+
+    def exchange(k):
         to = lax.rem(d + k, n)
-        src, dst = piece(j, to)
-        return send(src, dst, a2a_ss.at[k, j], a2a_sr.at[d, j], (to, at.e))
+        return send(pieces.at[to], rows_of(d), a2a_ss.at[k], a2a_sr.at[d], (to, at.e))
 
     at.meet(True)
     dense.begin()
+    for q in range(n):
+        for j in range(2 * held):
+            lo = (j % 2) * FF + q * f
+            pieces[q, :, j * f : (j + 1) * f] = ein_ref[j // 2, :, lo : lo + f]
+    own_piece.start()
+    allowed = rope_lanes(seg_ref, freq_ref, cos_ref, sin_ref)
     for i in range(1, n):
         dense.column(at.near(i))
         if i == n - 1:
             cot.begin_z()
+            for k in range(1, n):
+                exchange(k).start()
         dense.plane(at.near(i - 1))
         if i >= 2:
             dense.corner(at.near(i - 2))
@@ -1085,15 +1161,10 @@
     dense.plane(at.near(n - 1))
     if n > 1:
         dense.corner(at.near(n - 2))
-        cot.column_z(at.near(1))
+        cot.column(at.near(1))
     dense.corner(at.near(n - 1))
     for i in range(2, n):
-        cot.column_z(at.near(i))
-    for piece_copy in own_pieces:
-        piece_copy.start()
-    for k in range(1, n):
-        for j in range(2 * held):
-            exchange(k, j).start()
+        cot.column(at.near(i))
     for load in loads:
         load.wait()
     dense.siblings()
@@ -1121,9 +1192,7 @@
             ref, base = (q_ref, 0) if col < q_width else (k_ref, q_width) if col < q_width + k_width else (v_ref, q_width + k_width)
             ref[:, col - base : col - base + 128] = tile.astype(bf16)
     cot.plane(at.near(0))
-    if n > 1:
-        cot.column_xy(at.near(1))
-    allowed = jnp.concatenate([allowed_ref[...]] * groups, axis=0) > 0
+    allowed = jnp.concatenate([allowed] * groups, axis=0) > 0
     for g in range(KV_HEADS):
         qs = jnp.concatenate([q_ref[:, (g * groups + j) * HEAD : (g * groups + j + 1) * HEAD] for j in range(groups)], axis=0)
         ks, vs = k_ref[:, g * HEAD : (g + 1) * HEAD], v_ref[:, g * HEAD : (g + 1) * HEAD]
@@ -1141,7 +1210,10 @@
     mid = mid_ref[...]
     disp_ref[:, :D] = (mid * inverse_rms(mid) * gain_ref[1:2, :]).astype(bf16)
     logits = mm(disp_ref[:, :D], weight(tail_at, 128))
-    chosen = chosen_ref[...]
+    lanes = lane_tile(mid.shape[0])
+    chosen = jnp.zeros(lanes.shape, f32)
+    for k in range(TOP_K):
+        chosen += (route_ref[:, k : k + 1] == lanes).astype(f32)
     masked = jnp.where(chosen > 0, logits, neg_large)
     raised = jnp.where(chosen > 0, jnp.exp(masked - jnp.max(masked, axis=1, keepdims=True)), 0.0)
     gates = raised / jnp.sum(raised, axis=1, keepdims=True)
@@ -1152,32 +1224,30 @@
 
     for i in range(1, n):
         cot.plane(at.near(i))
-        if i + 1 < n:
-            cot.column_xy(at.near(i + 1))
         cot.corner(at.near(i - 1))
     cot.corner(at.near(n - 1))
-    for piece_copy in own_pieces:
-        piece_copy.wait()
+    own_piece.wait()
     for k in range(1, n):
+        exchange(k).wait_send()
         source = lax.rem(d + k, n)
-        for j in range(2 * held):
-            exchange(k, j).wait_send()
-            src, _ = piece(j, d)
-            dst = up_all.at[pl.ds(pl.multiple_of(source * share, share), share), pl.ds(j * f, f)]
-            send(src, dst, a2a_ss.at[k, j], a2a_sr.at[source, j], (source, at.e)).wait_recv()
+        send(pieces.at[0], rows_of(source), a2a_ss.at[k], a2a_sr.at[source], (source, at.e)).wait_recv()
     keep.wait()
     dense.finish()
     cot.finish()
 
 
-def forward_layer(tok, cot, dense, ein, cos, sin, allowed, chosen, n, experts, cid):
+def forward_layer(tok, cot, attn_in, attn_out, tail, ein, segments, routes, n, experts, cid):
     f32, bf16 = jnp.float32, jnp.bfloat16
     rows = tok.shape[0]
-    shard, wide = dense.shape
+    shard = attn_in.shape[0]
     held, share = ein.shape[:2]
     q_width, k_width = HEADS * HEAD, KV_HEADS * HEAD
+    wide = q_width + 2 * k_width + D + 128
     groups = HEADS // KV_HEADS
+    half = HEAD // 2
+    freq = jnp.tile(rope_base ** (-jnp.arange(half, dtype=f32) / half), 128 // half)[None, :]
     D_ = pltpu.SemaphoreType.DMA
+    V = lambda *s: pltpu.VMEM(s, bf16)
     any_, vm = pl.BlockSpec(memory_space=pl.ANY), pl.BlockSpec(memory_space=pltpu.VMEM)
     S = jax.ShapeDtypeStruct
     return pl.pallas_call(
@@ -1186,22 +1256,22 @@
             S((n * 8, shard, wide), bf16), S((n, 4, rows, D), bf16), S((D, 2 * held * (FF // n)), bf16),
             S((rows, D + 128), bf16), S((rows, D), f32), S((rows, 128), f32), S((8, D), f32), S((rows, D), bf16),
             S((rows, q_width), bf16), S((rows, k_width), bf16), S((rows, k_width), bf16),
-            S((KV_HEADS, groups * rows, rows), f32), S((rows, q_width), bf16),
+            S((KV_HEADS, groups * rows, rows), f32), S((rows, q_width), bf16), S((rows, 128), f32), S((rows, 128), f32),
         ),
-        in_specs=[vm, any_, any_, any_, vm, vm, vm, vm],
-        out_specs=[any_] * 3 + [vm] * 10,
-        scratch_shapes=[pltpu.VMEM((n * 8, shard, wide), bf16)]
+        in_specs=[vm, any_] + [vm] * 7,
+        out_specs=[any_] * 3 + [vm] * 12,
+        scratch_shapes=[V(n * 8, shard, wide), V(n, share, 2 * held * (FF // n)), V(shard, wide)]
         + [D_((n, 11)), D_((n,)), D_((n,)), D_((n,)), D_((n, 2)), D_((n, 5))] + gather_sems(n)
-        + [D_((2,)), D_((2 * held,)), D_((n, 2 * held)), D_((n, 2 * held))],
+        + [D_((3,)), D_((n,)), D_((n,))],
         compiler_params=pltpu.CompilerParams(collective_id=cid, has_side_effects=True, vmem_limit_bytes=60 << 20),
         name="forward_layer",
-    )(tok, cot, dense, ein, cos, sin, allowed, chosen)
+    )(tok, cot, attn_in, attn_out, tail, ein, segments, routes, freq)
 
 
 def backward_kernel(n, experts, gs_ref, tok_ref, cot_ref, mid_ref, gates_ref, gain_ref, nf_ref, disp_ref, q_ref, k_ref, v_ref, p_ref,
                     mixed_ref, cos_ref, sin_ref, w_ref, gup_ref,
-                    gtok_ref, gout_ref, gin_ref, gtail_ref, gup_out,
-                    wv, pout, pin, tot_out, tot_in, arrived, pair, gq, gl, sums, gb, gm, flat, *rest):
+                    gtok_ref, gout_ref, gin_ref, gtail_ref, arrived,
+                    wv, pout, pin, tot_out, tot_in, pair, gq, gl, sums, gb, gm, flat, *rest):
     f32, bf16 = jnp.float32, jnp.bfloat16
     at = Place(n)
     d, c = at.d, at.c
@@ -1236,6 +1306,8 @@
     at.meet(True)
     for i in range(3):
         swaps[i].start()
+    for k in range(1, n):
+        exchange(k).start()
 
     def weight(lo, width):
         return wv[:, :, lo : lo + width].reshape(D, width)
@@ -1281,8 +1353,6 @@
         store(pout, zz, 0, mm(both(mixed_ref, pair.at[0], row_cols(zz)), branch, TN))
         outs.s1(zz)
 
-    for k in range(1, n):
-        exchange(k).start()
     scale = HEAD ** (-0.5)
     for g in range(KV_HEADS):
         heads = [slice((g * groups + j) * HEAD, (g * groups + j + 1) * HEAD) for j in range(groups)]
@@ -1299,6 +1369,8 @@
             flat[:, h] = grad_query[j * rows : (j + 1) * rows]
         flat[:, q_width + kv.start : q_width + kv.stop] = mm(grad_scores, qs, TN) * scale
         flat[:, q_width + k_width + kv.start : q_width + k_width + kv.stop] = grad_values
+    for j in range(n):
+        outs.s2(at.far(j))
     cos, sin = cos_ref[...], sin_ref[...]
     for t in range(qkv_width // 128):
         tile = flat[:, t * 128 : (t + 1) * 128]
@@ -1343,20 +1415,16 @@
         tail = mm(both(disp_ref, pair.at[2], cols), jnp.concatenate([gl[0], gl[1]], axis=0), TN)
         rows_now = jnp.concatenate([sums[0, :, cols], sums[1, :, cols]], axis=0).astype(bf16)
         store(pin, zz, half_in, tail + mm(rows_now, where, TN))
-        ins.s1(zz)
-
-        outs.s2(zz)
+
+        @pl.when(j < 2)
+        def _():
+            ins.corners(zz)
 
     for j in range(n + 1):
+        ins.step(j)
         if j < n:
             outs.s3(at.far(j))
-            if j < n - 1:
-                outs.line(at.far(j))
-            ins.s2(at.far(j))
-        if j >= 1:
-            ins.s3(at.far(j - 1))
-            if j - 1 < n - 1:
-                ins.line(at.far(j - 1))
+            outs.lines(j)
     outs.last()
     mine, theirs = pl.ds(pl.multiple_of(c * shard, 8), shard), pl.ds(pl.multiple_of((1 - c) * shard, 8), shard)
     cols_out, cols_in = pl.ds(pl.multiple_of(c * half_out, 128), half_out), pl.ds(pl.multiple_of(c * half_in, 128), half_in)
@@ -1374,14 +1442,6 @@
         source = lax.rem(d + k, n)
         send(gup_ref.at[pl.ds(0, share), :], arrived.at[source], a2a_ss.at[k], a2a_sr.at[source], (source, at.e)).wait_recv()
 
-    @pl.loop(0, share // 32)
-    def _(r):
-        w = pl.ds(pl.multiple_of(r * 32, 32), 32)
-        for q in range(n):
-            for j in range(arrived.shape[2] // f):
-                lo = (j % 2) * FF + q * f
-                gup_out[j // 2, w, lo : lo + f] = arrived[q, w, j * f : (j + 1) * f].astype(f32)
-
     end_out.wait()
     end_in.wait()
     for swap in swaps + [swap_q, swap_l]:
@@ -1390,7 +1450,7 @@
     ins.finish()
 
 
-def backward_layer(gs, tok, cot, mid, gates, gain, nf, disp, q, k, v, p, mixed, cos, sin, w_all, gup, held, n, experts, cid):
+def backward_layer(gs, tok, cot, mid, gates, gain, nf, disp, q, k, v, p, mixed, cos, sin, w_all, gup, n, experts, cid):
     f32, bf16 = jnp.float32, jnp.bfloat16
     rows = tok.shape[0]
     shard, wide = w_all.shape[1:]
@@ -1404,17 +1464,56 @@
     width_out, width_in = D // 2, qkv_width // 2 + 128
     return pl.pallas_call(
         functools.partial(backward_kernel, n, experts),
-        out_shape=(S((rows, D), f32), S((shard, D), f32), S((shard, qkv_width), f32), S((shard, 128), f32), S((held, share, 2 * FF), f32)),
+        out_shape=(S((rows, D), f32), S((shard, D), f32), S((shard, qkv_width), f32), S((shard, 128), f32), S((n, share, gup.shape[1]), bf16)),
         in_specs=[vm] * 15 + [any_, any_],
-        out_specs=[vm] * 5,
+        out_specs=[vm] * 4 + [any_],
         scratch_shapes=[V(n * 8, shard, wide), V(n, 4, 2 * shard, width_out), V(n, 4, 2 * shard, width_in),
-                        W(2 * shard, width_out), W(2 * shard, width_in), V(n, share, gup.shape[1]),
+                        W(2 * shard, width_out), W(2 * shard, width_in),
                         V(4, rows, D), V(2, rows, qkv_width), V(2, rows, 128), W(2, 8, D), V(rows, D), V(rows, D), W(rows, qkv_width)]
         + reduce_scratch(n, 2 * shard, width_out) + reduce_scratch(n, 2 * shard, width_in)
         + [D_((4,)), D_((7,)), D_((7,)), D_((n,)), D_((n,)), D_((2,)), D_((2,))],
         compiler_params=pltpu.CompilerParams(collective_id=cid, has_side_effects=True, vmem_limit_bytes=62 << 20),
         name="backward_layer",
     )(gs, tok, cot, mid, gates, gain, nf, disp, q, k, v, p, mixed, cos, sin, w_all, gup)
+
+
+def results_kernel(experts, arrived, tok_in, down_in, out_in, qkv_in, tail_in,
+                   up_ref, tok_ref, down_ref, proj_ref, qkv_ref, router_ref, gains_ref):
+    n, width = arrived.shape[0], arrived.shape[2]
+    f = FF // n
+    for q in range(n):
+        for j in range(width // f):
+            lo = (j % 2) * FF + q * f
+            up_ref[j // 2, :, lo : lo + f] = arrived[q, :, j * f : (j + 1) * f].astype(jnp.float32)
+
+    @pl.when(pl.program_id(0) == 0)
+    def _():
+        tok_ref[...] = tok_in[...]
+        down_ref[...] = down_in[...]
+        proj_ref[...] = out_in[...]
+        qkv_ref[...] = qkv_in[...]
+        router_ref[...] = tail_in[:, :experts]
+        turned = jnp.transpose(jnp.concatenate([tail_in[...], jnp.zeros((128 - tail_in.shape[0], 128), jnp.float32)], axis=0))
+        gains_ref[...] = turned[experts : experts + 8, : tail_in.shape[0]]
+
+
+def results(arrived, tok, down, proj, qkv, tail, held, experts):
+    n, share, width = arrived.shape
+    f32 = jnp.float32
+    steps = 4
+    rows = share // steps
+    whole = lambda a: pl.BlockSpec(a.shape, lambda i: (0,) * len(a.shape))
+    shapes = [jax.ShapeDtypeStruct(a.shape, f32) for a in (tok, down, proj, qkv)]
+    shapes += [jax.ShapeDtypeStruct((tail.shape[0], experts), f32), jax.ShapeDtypeStruct((8, tail.shape[0]), f32)]
+    return pl.pallas_call(
+        functools.partial(results_kernel, experts),
+        grid=(steps,),
+        out_shape=[jax.ShapeDtypeStruct((held, share, 2 * FF), f32)] + shapes,
+        in_specs=[pl.BlockSpec((n, rows, width), lambda i: (0, i, 0))] + [whole(a) for a in (tok, down, proj, qkv, tail)],
+        out_specs=[pl.BlockSpec((held, rows, 2 * FF), lambda i: (0, i, 0))] + [whole(a) for a in shapes],
+        compiler_params=pltpu.CompilerParams(vmem_limit_bytes=62 << 20),
+        name="results",
+    )(arrived, tok, down, proj, qkv, tail)
 
 
 def per_device_fast(n, tokens, segments, routes, cotangent, gain_attn, attn_in, attn_out, gain_ffn, router, expert_in, expert_out):
@@ -1428,36 +1527,21 @@
     x = tokens.reshape(total, D)
     cot = cotangent.reshape(total, D)
     tail = jnp.concatenate([router, gain_attn[:, None], gain_ffn[:, None], jnp.zeros((shard, 126 - experts), bf16)], axis=1)
-    dense = jnp.concatenate([attn_in, attn_out, tail], axis=1)
-
-    segment = (segments[:, 0, :] + 2 * rows * jnp.arange(micro, dtype=jnp.int32)[:, None]).reshape(total)
-    cosine, sine_table, causal = rope_tables(segment, HEAD // 2)
-    cos = jnp.tile(cosine, (1, 128 * 2 // HEAD))
-    sin = jnp.tile(jnp.concatenate([-sine_table, sine_table], axis=1), (1, 128 // HEAD))
-    route = routes.reshape(total, TOP_K)
-    chosen = jnp.any(route[:, :, None] == jnp.arange(128, dtype=jnp.int32)[None, None, :], axis=1).astype(f32)
-    w_all, cot_all, up, disp, middle, gates, gain, nf, q, k, v, p, mixed = forward_layer(
-        x, cot, dense, expert_in, cos, sin, causal.astype(f32), chosen, n, experts, 0)
-
-    mine = lax.axis_index("expert")
-    order = jnp.stack([mine, mine + 1 - 2 * lax.rem(mine, 2)])
-    owner = (order[:, None] * held + jnp.arange(held, dtype=jnp.int32)[None, :]).reshape(-1)
-    owner = jnp.repeat(owner, f)[None, :]
-    lane = jnp.arange(128, dtype=jnp.int32)[:, None]
-    pick = ((lane == owner) | (lane == owner + experts)).astype(bf16)
-    place = (lane == owner).astype(bf16).T
-    out, grad_sum, grad_up, grad_down = expert_layer(
-        disp, cot_all, up, expert_out.reshape(held * f, D), pick, place, middle, n, 1)
+    w_all, cot_all, up, disp, middle, gates, gain, nf, q, k, v, p, mixed, cos, sin = forward_layer(
+        x, cot, attn_in, attn_out, tail, expert_in, segments, routes.reshape(total, TOP_K), n, experts, 0)
+    out, grad_sum, grad_up, grad_down = expert_layer(disp, cot_all, up, expert_out.reshape(held * f, D), middle, n, experts, 1)
     grad_tokens, grad_out, grad_in, grad_tail, grad_up = backward_layer(
-        grad_sum, x, cot, middle, gates, gain, nf, disp, q, k, v, p, mixed, cos, sin, w_all, grad_up, held, n, experts, 2)
+        grad_sum, x, cot, middle, gates, gain, nf, disp, q, k, v, p, mixed, cos, sin, w_all, grad_up, n, experts, 2)
+    grad_up, grad_tokens, grad_down, grad_out, grad_in, grad_router, grad_gains = results(
+        grad_up, grad_tokens, grad_down, grad_out, grad_in, grad_tail, held, experts)
     return (
         out.astype(bf16).reshape(micro, rows, D),
         grad_tokens.reshape(micro, rows, D),
-        grad_tail[:, experts],
+        grad_gains[0],
         grad_in,
         grad_out,
-        grad_tail[:, experts + 1],
-        grad_tail[:, :experts],
+        grad_gains[1],
+        grad_router,
         grad_up,
         grad_down.reshape(held, f, D),
     )

time: 459 us -> 406 us (0.88)
  Pallas kernels: 428 us -> 396 us
  local copies, waits for them, and re-layouts: 20.6 us -> 7.09 us
    pallas_call x1 -> x2, Pallas kernels: 210 us -> 193 us  [the longest x1 186 us: expert_layer(): pl.pallas_call(functools.partial(expert_kernel, n, experts), out_shape=(j...]
    pallas_call x1, Pallas kernels: 92.4 us -> 82.6 us  [backward_layer(): pl.pallas_call(functools.partial(backward_kernel, n, experts), out_shape=...]
    unnamed x16 -> x5, local copies, waits for them, and re-layouts: 13.1 us -> 3.62 us
    pallas_call x1, Pallas kernels: 125 us -> 121 us  [forward_layer(): pl.pallas_call(functools.partial(forward_kernel, n, experts), out_shape=(...]
where the time goes in v4:
time: 406 us; the launch traced here: 405 us
  Pallas kernels  396 us (98%)
  local copies, waits for them, and re-layouts  7.09 us (2%)
    pallas_call x1, Pallas kernels, expert_layer(): pl.pallas_call(functools.partial(expert_kernel, n, experts), out_shape=(j...  186 us
    pallas_call x1, Pallas kernels, forward_layer(): pl.pallas_call(functools.partial(forward_kernel, n, experts), out_shape=(...  121 us
    pallas_call x1, Pallas kernels, backward_layer(): pl.pallas_call(functools.partial(backward_kernel, n, experts), out_shape=...  82.6 us

profile of v4, /device:TPU:11, one launch (start us, length us, event | category | flops | bytes accessed | tf_op | source)
XLA Modules:
  0.0 405.4 jit_solution(13489883878954018290)
XLA Ops:
  0.7 0.1 pad.3.clone
  0.7 0.6 broadcast_in_dim_tile.3.freq_ref
  1.3 0.8 copy.21
  2.1 0.8 copy.22
  2.9 0.8 copy.20
  3.6 0.7 maximum_maximum_fusion.tail_ref
  4.3 1.4 copy.23
  5.8 120.6 %forward_layer.1 = (bf16[32,48,4224]{2,1,0:T(8,128)(2,1)}, bf16[4,4,128,1536]{3,2,1,0:T(8,128)(2,1)}, bf16[1536,768]{1,0:T(8,128)(2,1)}, bf16[128,1664]{1,0:T(8,...) custom-call(bf16[128,1536]{1,0:T(8,128)(2,1)} %bitcast.13, ...), custom_call_target="tpu_custom_call" | custom-call | tf_op jit(solution)/shard_map/forward_layer/pallas_call | solution.py:1253
  126.4 185.7 %expert_layer.1 = (f32[128,1536]{1,0:T(8,128)}, f32[128,1664]{1,0:T(8,128)}, bf16[1536,768]{1,0:T(8,128)(2,1)}, f32[384,1536]{1,0:T(8,128)}) custom-call(bf16[128,1664]{1,0:T(8,128)(2,1)} %get-tuple-element.40.x_ref.disp_ref, bf16[4,4,128,1536]{3,2,1,0:T(8,128)(2,1)} %get-tuple-element.41.cot_ref, bf16[1536,768]{1,0:T(8,128)(2,1)} %get-tuple-element.42.up_ref, ...), custom_call_target="tpu_custom_call" | custom-call | tf_op jit(solution)/shard_map/expert_layer/pallas_call | solution.py:938
  312.1 0.0 copy-start
  312.1 82.6 %backward_layer.1 = (f32[128,1536]{1,0:T(8,128)}, f32[48,1536]{1,0:T(8,128)}, f32[48,2560]{1,0:T(8,128)}, f32[48,128]{1,0:T(8,128)}, bf16[4,384,768]{2,1,0:T(8,128)(2,1)}) custom-call(f32[128,1664]{1,0:T(8,128)} %get-tuple-element.45.gs_ref, bf16[128,1536]{1,0:T(8,128)(2,1)} %bitcast.14, bf16[128,1536]{1,0:T(8,128)(2,1)} %bitcast.16, ...), custom_call_target="tpu_custom_call" | custom-call | tf_op jit(solution)/shard_map/backward_layer/pallas_call | solution.py:1465
  394.7 0.0 copy-done
  394.7 0.8 convert_element_type.3
  395.5 7.2 %results.1 = (f32[3,384,1024]{2,1,0:T(8,128)}, f32[128,1536]{1,0:T(8,128)}, f32[384,1536]{1,0:T(8,128)}, f32[48,1536]{1,0:T(8,128)}, f32[48,2560]{1,0:T(8,128)}, /*index=5*/f32[48,24]{1,0:T(8,128)}, f32[8,48]{1,0:T(8,128)}) custom-call(bf16[4,384,768]{2,1,0:T(8,128)(2,1)} %get-tuple-element.58.arrived, f32[128,1536]{1,0:T(8,128)} %get-tuple-element.59.tok_in, ...), custom_call_target="tpu_custom_call" | custom-call | tf_op jit(solution)/shard_map/results/pallas_call | solution.py:1508
  402.7 1.3 slice_bitcast_fusion
  404.0 1.4 copy.24
  (3 shorter events, 0.0 us)
Async XLA Ops:
  312.1 82.6 %copy-start = (f32[128,1536]{1,0:T(8,128)S(1)}, f32[128,1536]{1,0:T(8,128)}, u32[]{:S(2)}) copy-start(f32[128,1536]{1,0:T(8,128)} %get-tuple-element.44) | copy-start | bytes 2359300

commit v5 on v4

--- a/solution.py
+++ b/solution.py
@@ -472,26 +472,26 @@
 
 
 class Gather:
-    def __init__(self, at, own, buf, send_sem, recv_z, recv_x, recv_y, recv_d):
+    def __init__(self, at, own, buf, send_sem, recv_z, recv_x, recv_y, recv_d, rows=None):
         self.at, self.own, self.buf = at, own, buf
         self.ss, self.rz, self.rx, self.ry, self.rd = send_sem, recv_z, recv_x, recv_y, recv_d
-        rows = own.shape[0]
-        self.A, self.B = pl.ds(0, rows // 2), pl.ds(rows // 2, rows // 2)
+        rows = rows or own.shape[0]
+        self.F, self.A, self.B = pl.ds(0, rows), pl.ds(0, rows // 2), pl.ds(rows // 2, rows // 2)
 
     def source(self, zz, own):
-        return self.own if own else self.buf.at[zz, 0]
+        return self.own.at[self.F] if own else self.buf.at[zz, 0, self.F]
 
     def down(self, zz, own=False):
-        return send(self.source(zz, own), self.buf.at[zz, 0], self.ss.at[zz, 0], self.rz.at[zz], self.at.below)
+        return send(self.source(zz, own), self.buf.at[zz, 0, self.F], self.ss.at[zz, 0], self.rz.at[zz], self.at.below)
 
     def up(self, zz, own=False):
-        return send(self.source(zz, own), self.buf.at[zz, 0], self.ss.at[zz, 1], self.rz.at[zz], self.at.above)
+        return send(self.source(zz, own), self.buf.at[zz, 0, self.F], self.ss.at[zz, 1], self.rz.at[zz], self.at.above)
 
     def to_x(self, zz, own=False):
-        return send(self.source(zz, own), self.buf.at[zz, 1], self.ss.at[zz, 2], self.rx.at[zz], self.at.nx)
+        return send(self.source(zz, own), self.buf.at[zz, 1, self.F], self.ss.at[zz, 2], self.rx.at[zz], self.at.nx)
 
     def to_y(self, zz, own=False):
-        return send(self.source(zz, own), self.buf.at[zz, 2], self.ss.at[zz, 3], self.ry.at[zz], self.at.ny)
+        return send(self.source(zz, own), self.buf.at[zz, 2, self.F], self.ss.at[zz, 3], self.ry.at[zz], self.at.ny)
 
     def turn_y(self, zz):
         return send(self.buf.at[zz, 1, self.A], self.buf.at[zz, 3, self.A], self.ss.at[zz, 4], self.rd.at[zz, 0], self.at.ny)
@@ -570,6 +570,78 @@
             @pl.when(self.at.has_above & (zz <= d))
             def _():
                 self.up(zz).wait_send()
+
+
+class LineGather:
+    def __init__(self, at, own, buf, lo, ss, sr, zs, zr):
+        self.at, self.own, self.buf = at, own, buf
+        self.ss, self.sr, self.zs, self.zr = ss, sr, zs, zr
+        rows = own.shape[0] - lo
+        self.P, self.A, self.B = pl.ds(lo, rows), pl.ds(lo, rows // 2), pl.ds(lo + rows // 2, rows // 2)
+
+    def inside(self, k):
+        at, buf, d = self.at, self.buf, self.at.d
+        src, slot, part, dev = (
+            (self.own.at[self.P], 1, self.P, at.nx), (self.own.at[self.P], 2, self.P, at.ny),
+            (buf.at[d, 1, self.A], 3, self.A, at.ny), (buf.at[d, 2, self.B], 3, self.B, at.nx))[k]
+        return send(src, buf.at[d, slot, part], self.ss.at[k], self.sr.at[k], dev)
+
+    def along(self, zz, up):
+        part = self.buf.at[zz, :, self.P]
+        return send(part, part, self.zs.at[zz, up], self.zr.at[zz], self.at.above if up else self.at.below)
+
+    def begin(self):
+        self.inside(0).start()
+        self.inside(1).start()
+
+    def plane(self):
+        self.inside(0).wait_recv()
+        self.inside(2).start()
+        self.inside(1).wait_recv()
+        self.inside(3).start()
+
+    def corner(self):
+        self.inside(2).wait_recv()
+        self.inside(3).wait_recv()
+
+        @pl.when(self.at.has_below)
+        def _():
+            self.along(self.at.d, 0).start()
+
+        @pl.when(self.at.has_above)
+        def _():
+            self.along(self.at.d, 1).start()
+
+    def line(self, zz):
+        self.along(zz, 0).wait_recv()
+
+        @pl.when((zz < self.at.d) & self.at.has_above)
+        def _():
+            self.along(zz, 1).start()
+
+        @pl.when((zz > self.at.d) & self.at.has_below)
+        def _():
+            self.along(zz, 0).start()
+
+    def finish(self):
+        d = self.at.d
+        for k in range(4):
+            self.inside(k).wait_send()
+
+        @pl.loop(0, self.at.n)
+        def _(zz):
+            @pl.when(self.at.has_below & (zz >= d))
+            def _():
+                self.along(zz, 0).wait_send()
+
+            @pl.when(self.at.has_above & (zz <= d))
+            def _():
+                self.along(zz, 1).wait_send()
+
+
+def line_gather_sems(n):
+    D_ = pltpu.SemaphoreType.DMA
+    return [D_((4,)), D_((4,)), D_((n, 2)), D_((n,))]
 
 
 def gather_sems(n):
@@ -753,15 +825,17 @@
 
 
 def expert_kernel(n, experts, x_ref, cot_ref, up_ref, down_ref, mid_ref,
-                  out_ref, gx_ref, gup_ref, gdown_ref,
-                  xb, cb, gg, mixed, gb, wup, wdown, pick_ref, place_ref, *rest):
+                  out_ref, gx_ref, gup_ref, gdown_out,
+                  gdown_ref, xb, cb, gg, mixed, gb, wup, wdown, pick_ref, place_ref, *rest):
     f32, bf16 = jnp.float32, jnp.bfloat16
     at = Place(n)
     d = at.d
-    gather = Gather(at, x_ref, xb, *rest[:5])
+    lo = x_ref.shape[0] * 3 // 4
+    gather = Gather(at, x_ref, xb, *rest[:5], rows=lo)
+    tail = LineGather(at, x_ref, xb, lo, *rest[-4:])
     grads = Reduce(at, gb, gx_ref, *rest[5:14])
     outs = Reduce(at, gg, out_ref, *rest[14:23], start=mid_ref)
-    load_sem, core_ss, core_sr, free = rest[23:]
+    load_sem, core_ss, core_sr, free = rest[23:-4]
     rows = x_ref.shape[0]
     f2 = up_ref.shape[1]
     f = f2 // 2
@@ -775,7 +849,9 @@
     for load in loads:
         load.start()
     at.meet()
-    gather.begin()
+    gather.begin_z()
+    tail.begin()
+    gather.begin_xy()
     swaps = [
         send(up_ref, wup.at[1], core_ss.at[0], core_sr.at[0], at.sib),
         send(down_ref, wdown.at[1], core_ss.at[1], core_sr.at[1], at.sib),
@@ -788,9 +864,12 @@
             gate_row = lax.broadcasted_iota(jnp.int32, (128, 128), 0)
             pick_ref[:, cols] = ((gate_row == expert) | (gate_row == expert + experts)).astype(bf16)
             place_ref[cols, :] = (lane_tile(128) == expert).astype(bf16)
+    loads[0].wait()
+    tail.plane()
+    tail.corner()
     gather.plane(at.near(0))
     gather.column(at.near(1))
-    for load in loads:
+    for load in loads[1:]:
         load.wait()
     for swap in swaps:
         swap.wait_recv()
@@ -843,6 +922,7 @@
 
         @pl.when(i + 1 < n)
         def _():
+            tail.line(at.near(i + 1))
             gather.plane(at.near(i + 1))
 
         gather.corner(zz)
@@ -899,6 +979,7 @@
     up_swap.wait_recv()
     grad_up(0, True)
     keep = pltpu.make_async_copy(wup.at[0], gup_ref, load_sem.at[0])
+    keep_down = pltpu.make_async_copy(gdown_ref, gdown_out, load_sem.at[1])
     keep.start()
     grads.s3(at.near(n - 1))
     grads.line_head(at.near(n - 1))
@@ -912,17 +993,22 @@
     down_swap = send(wdown.at[1], wdown.at[0], core_ss.at[3], core_sr.at[3], at.sib)
     down_swap.start()
     for j in range(n + 1):
+        if j == n:
+            grads.last()
         outs.step(j)
         if j < n - 1:
             grads.line_rest(at.far(j))
-    down_swap.wait_recv()
-    grad_down(0)
-    grads.last()
+        if j == 0:
+            down_swap.wait_recv()
+            grad_down(0)
+            keep_down.start()
     outs.last()
+    keep_down.wait()
     keep.wait()
     up_swap.wait_send()
     down_swap.wait_send()
     gather.finish()
+    tail.finish()
     grads.finish()
     outs.finish()
 
@@ -944,11 +1030,11 @@
             jax.ShapeDtypeStruct((f, D), jnp.float32),
         ),
         in_specs=[any_, any_, any_, any_, vm],
-        out_specs=[vm, vm, any_, vm],
-        scratch_shapes=[V(n, 4, rows, wide), V(n, 4, rows, D), V(n, 4, rows, 2 * f2), V(n, 4, rows, 2 * f), V(n, 4, rows, wide),
+        out_specs=[vm, vm, any_, any_],
+        scratch_shapes=[pltpu.VMEM((f, D), jnp.float32), V(n, 4, rows, wide), V(n, 4, rows, D), V(n, 4, rows, 2 * f2), V(n, 4, rows, 2 * f), V(n, 4, rows, wide),
                         V(2, D, f2), V(2, f, D), V(128, 2 * f), V(2 * f, 128)]
         + gather_sems(n) + reduce_scratch(n, rows, wide) + reduce_scratch(n, rows, D)
-        + [D_((4,)), D_((4,)), D_((4,)), pltpu.SemaphoreType.REGULAR((2,))],
+        + [D_((4,)), D_((4,)), D_((4,)), pltpu.SemaphoreType.REGULAR((2,))] + line_gather_sems(n),
         compiler_params=pltpu.CompilerParams(collective_id=cid, has_side_effects=True, vmem_limit_bytes=63 << 20),
         name="expert_layer",
     )(x, cot_all, up, down, middle)
@@ -1108,14 +1194,15 @@
 
 
 def forward_kernel(n, experts, tok_ref, cot_ref, qkv_ref, proj_ref, tail_ref, ein_ref, seg_ref, route_ref, freq_ref,
-                   w_all, cot_all, up_all, disp_ref, mid_ref, gates_ref, gain_ref, nf_ref, q_ref, k_ref, v_ref, p_ref, mixed_ref, cos_ref, sin_ref,
+                   w_all, cot_all, up_all, disp_out, mid_out, gates_out, gain_out, nf_out, q_out, k_out, v_out, p_out, mixed_out, cos_out, sin_out,
+                   disp_ref, mid_ref, gates_ref, gain_ref, nf_ref, q_ref, k_ref, v_ref, p_ref, mixed_ref, cos_ref, sin_ref,
                    wv, pieces, dense_ref, *rest):
     f32, bf16 = jnp.float32, jnp.bfloat16
     at = Place(n)
     d = at.d
     dense = GatherAll(at, dense_ref, wv, *rest[:6])
     cot = Gather(at, cot_ref, cot_all, *rest[6:11])
-    load_sem, a2a_ss, a2a_sr = rest[11:]
+    load_sem, a2a_ss, a2a_sr, keep_sem = rest[11:]
     q_width, k_width = HEADS * HEAD, KV_HEADS * HEAD
     groups = HEADS // KV_HEADS
     held, share = ein_ref.shape[:2]
@@ -1222,6 +1309,11 @@
     low = (gates - high).astype(bf16).astype(f32)
     disp_ref[:, D:] = (high + pltpu.roll(low, experts, 1)).astype(bf16)
 
+    keeps = [pltpu.make_async_copy(src, dst, keep_sem.at[i]) for i, (src, dst) in enumerate((
+        (disp_ref, disp_out), (mid_ref, mid_out), (gates_ref, gates_out), (gain_ref, gain_out), (nf_ref, nf_out), (q_ref, q_out),
+        (k_ref, k_out), (v_ref, v_out), (p_ref, p_out), (mixed_ref, mixed_out), (cos_ref, cos_out), (sin_ref, sin_out)))]
+    for copy in keeps:
+        copy.start()
     for i in range(1, n):
         cot.plane(at.near(i))
         cot.corner(at.near(i - 1))
@@ -1234,6 +1326,8 @@
     keep.wait()
     dense.finish()
     cot.finish()
+    for copy in keeps:
+        copy.wait()
 
 
 def forward_layer(tok, cot, attn_in, attn_out, tail, ein, segments, routes, n, experts, cid):
@@ -1250,34 +1344,35 @@
     V = lambda *s: pltpu.VMEM(s, bf16)
     any_, vm = pl.BlockSpec(memory_space=pl.ANY), pl.BlockSpec(memory_space=pltpu.VMEM)
     S = jax.ShapeDtypeStruct
+    saved = (
+        S((rows, D + 128), bf16), S((rows, D), f32), S((rows, 128), f32), S((8, D), f32), S((rows, D), bf16),
+        S((rows, q_width), bf16), S((rows, k_width), bf16), S((rows, k_width), bf16),
+        S((KV_HEADS, groups * rows, rows), f32), S((rows, q_width), bf16), S((rows, 128), f32), S((rows, 128), f32),
+    )
     return pl.pallas_call(
         functools.partial(forward_kernel, n, experts),
-        out_shape=(
-            S((n * 8, shard, wide), bf16), S((n, 4, rows, D), bf16), S((D, 2 * held * (FF // n)), bf16),
-            S((rows, D + 128), bf16), S((rows, D), f32), S((rows, 128), f32), S((8, D), f32), S((rows, D), bf16),
-            S((rows, q_width), bf16), S((rows, k_width), bf16), S((rows, k_width), bf16),
-            S((KV_HEADS, groups * rows, rows), f32), S((rows, q_width), bf16), S((rows, 128), f32), S((rows, 128), f32),
-        ),
+        out_shape=(S((n * 8, shard, wide), bf16), S((n, 4, rows, D), bf16), S((D, 2 * held * (FF // n)), bf16)) + saved,
         in_specs=[vm, any_] + [vm] * 7,
-        out_specs=[any_] * 3 + [vm] * 12,
-        scratch_shapes=[V(n * 8, shard, wide), V(n, share, 2 * held * (FF // n)), V(shard, wide)]
+        out_specs=[any_] * 15,
+        scratch_shapes=[pltpu.VMEM(a.shape, a.dtype) for a in saved]
+        + [V(n * 8, shard, wide), V(n, share, 2 * held * (FF // n)), V(shard, wide)]
         + [D_((n, 11)), D_((n,)), D_((n,)), D_((n,)), D_((n, 2)), D_((n, 5))] + gather_sems(n)
-        + [D_((3,)), D_((n,)), D_((n,))],
+        + [D_((3,)), D_((n,)), D_((n,)), D_((len(saved),))],
         compiler_params=pltpu.CompilerParams(collective_id=cid, has_side_effects=True, vmem_limit_bytes=60 << 20),
         name="forward_layer",
     )(tok, cot, attn_in, attn_out, tail, ein, segments, routes, freq)
 
 
-def backward_kernel(n, experts, gs_ref, tok_ref, cot_ref, mid_ref, gates_ref, gain_ref, nf_ref, disp_ref, q_ref, k_ref, v_ref, p_ref,
-                    mixed_ref, cos_ref, sin_ref, w_ref, gup_ref,
+def backward_kernel(n, experts, gs_in, tok_in, cot_in, mid_in, gates_in, gain_in, nf_in, disp_in, q_in, k_in, v_in, p_in, mixed_in, cos_in, sin_in, w_ref, gup_ref,
                     gtok_ref, gout_ref, gin_ref, gtail_ref, arrived,
+                    gs_ref, tok_ref, cot_ref, mid_ref, gates_ref, gain_ref, nf_ref, disp_ref, q_ref, k_ref, v_ref, p_ref, mixed_ref, cos_ref, sin_ref,
                     wv, pout, pin, tot_out, tot_in, pair, gq, gl, sums, gb, gm, flat, *rest):
     f32, bf16 = jnp.float32, jnp.bfloat16
     at = Place(n)
     d, c = at.d, at.c
     outs = Reduce(at, pout, tot_out, *rest[:9])
     ins = Reduce(at, pin, tot_in, *rest[9:18])
-    load_sem, pair_ss, pair_sr, a2a_ss, a2a_sr, end_ss, end_sr = rest[18:]
+    load_sem, pair_ss, pair_sr, a2a_ss, a2a_sr, end_ss, end_sr, in_sem = rest[18:]
     q_width, k_width = HEADS * HEAD, KV_HEADS * HEAD
     groups = HEADS // KV_HEADS
     qkv_width = q_width + 2 * k_width
@@ -1286,11 +1381,17 @@
     shard = w_ref.shape[1]
     share = D // n
     f = FF // n
+    fetched = [pltpu.make_async_copy(src, dst, in_sem.at[i]) for i, (src, dst) in enumerate((
+        (mid_in, mid_ref), (gates_in, gates_ref), (gs_in, gs_ref), (gain_in, gain_ref), (cot_in, cot_ref), (mixed_in, mixed_ref), (nf_in, nf_ref), (disp_in, disp_ref), (q_in, q_ref), (k_in, k_ref), (v_in, v_ref), (p_in, p_ref), (tok_in, tok_ref), (cos_in, cos_ref), (sin_in, sin_ref)))]
+    for copy in fetched[:8]:
+        copy.start()
     loads = []
     for i, (lo, width) in enumerate(((tail_at, 128), (qkv_width, D), (0, qkv_width))):
         loads.append(pltpu.make_async_copy(w_ref.at[:, :, pl.ds(lo, width)], wv.at[:, :, pl.ds(lo, width)], load_sem.at[i]))
     for load in loads:
         load.start()
+    for copy in fetched[8:]:
+        copy.start()
     own_share = pltpu.make_async_copy(gup_ref.at[pl.ds(pl.multiple_of(d * share, share), share), :], arrived.at[d], load_sem.at[3])
     own_share.start()
 
@@ -1304,10 +1405,12 @@
     swap_l = send(gl.at[0], gl.at[1], pair_ss.at[5], pair_sr.at[5], at.sib)
     swap_s = send(sums.at[0], sums.at[1], pair_ss.at[6], pair_sr.at[6], at.sib)
     at.meet(True)
+    for k in range(1, n):
+        exchange(k).start()
+    for copy in fetched[:8]:
+        copy.wait()
     for i in range(3):
         swaps[i].start()
-    for k in range(1, n):
-        exchange(k).start()
 
     def weight(lo, width):
         return wv[:, :, lo : lo + width].reshape(D, width)
@@ -1353,6 +1456,8 @@
         store(pout, zz, 0, mm(both(mixed_ref, pair.at[0], row_cols(zz)), branch, TN))
         outs.s1(zz)
 
+    for copy in fetched[8:]:
+        copy.wait()
     scale = HEAD ** (-0.5)
     for g in range(KV_HEADS):
         heads = [slice((g * groups + j) * HEAD, (g * groups + j + 1) * HEAD) for j in range(groups)]
@@ -1465,13 +1570,14 @@
     return pl.pallas_call(
         functools.partial(backward_kernel, n, experts),
         out_shape=(S((rows, D), f32), S((shard, D), f32), S((shard, qkv_width), f32), S((shard, 128), f32), S((n, share, gup.shape[1]), bf16)),
-        in_specs=[vm] * 15 + [any_, any_],
+        in_specs=[any_] * 17,
         out_specs=[vm] * 4 + [any_],
-        scratch_shapes=[V(n * 8, shard, wide), V(n, 4, 2 * shard, width_out), V(n, 4, 2 * shard, width_in),
+        scratch_shapes=[pltpu.VMEM(a.shape, a.dtype) for a in (gs, tok, cot, mid, gates, gain, nf, disp, q, k, v, p, mixed, cos, sin)]
+        + [V(n * 8, shard, wide), V(n, 4, 2 * shard, width_out), V(n, 4, 2 * shard, width_in),
                         W(2 * shard, width_out), W(2 * shard, width_in),
                         V(4, rows, D), V(2, rows, qkv_width), V(2, rows, 128), W(2, 8, D), V(rows, D), V(rows, D), W(rows, qkv_width)]
         + reduce_scratch(n, 2 * shard, width_out) + reduce_scratch(n, 2 * shard, width_in)
-        + [D_((4,)), D_((7,)), D_((7,)), D_((n,)), D_((n,)), D_((2,)), D_((2,))],
+        + [D_((4,)), D_((7,)), D_((7,)), D_((n,)), D_((n,)), D_((2,)), D_((2,)), D_((15,))],
         compiler_params=pltpu.CompilerParams(collective_id=cid, has_side_effects=True, vmem_limit_bytes=62 << 20),
         name="backward_layer",
     )(gs, tok, cot, mid, gates, gain, nf, disp, q, k, v, p, mixed, cos, sin, w_all, gup)
@@ -1486,10 +1592,11 @@
             lo = (j % 2) * FF + q * f
             up_ref[j // 2, :, lo : lo + f] = arrived[q, :, j * f : (j + 1) * f].astype(jnp.float32)
 
+    tok_ref[...] = tok_in[...]
+    down_ref[...] = down_in[...]
+
     @pl.when(pl.program_id(0) == 0)
     def _():
-        tok_ref[...] = tok_in[...]
-        down_ref[...] = down_in[...]
         proj_ref[...] = out_in[...]
         qkv_ref[...] = qkv_in[...]
         router_ref[...] = tail_in[:, :experts]
@@ -1503,14 +1610,15 @@
     steps = 4
     rows = share // steps
     whole = lambda a: pl.BlockSpec(a.shape, lambda i: (0,) * len(a.shape))
+    part = lambda a: pl.BlockSpec((a.shape[0] // steps, a.shape[1]), lambda i: (i, 0))
     shapes = [jax.ShapeDtypeStruct(a.shape, f32) for a in (tok, down, proj, qkv)]
     shapes += [jax.ShapeDtypeStruct((tail.shape[0], experts), f32), jax.ShapeDtypeStruct((8, tail.shape[0]), f32)]
     return pl.pallas_call(
         functools.partial(results_kernel, experts),
         grid=(steps,),
         out_shape=[jax.ShapeDtypeStruct((held, share, 2 * FF), f32)] + shapes,
-        in_specs=[pl.BlockSpec((n, rows, width), lambda i: (0, i, 0))] + [whole(a) for a in (tok, down, proj, qkv, tail)],
-        out_specs=[pl.BlockSpec((held, rows, 2 * FF), lambda i: (0, i, 0))] + [whole(a) for a in shapes],
+        in_specs=[pl.BlockSpec((n, rows, width), lambda i: (0, i, 0))] + [part(a) for a in (tok, down)] + [whole(a) for a in (proj, qkv, tail)],
+        out_specs=[pl.BlockSpec((held, rows, 2 * FF), lambda i: (0, i, 0))] + [part(a) for a in (tok, down)] + [whole(a) for a in shapes[2:]],
         compiler_params=pltpu.CompilerParams(vmem_limit_bytes=62 << 20),
         name="results",
     )(arrived, tok, down, proj, qkv, tail)

time: 406 us -> 391 us (0.963)
  Pallas kernels: 396 us -> 378 us
    pallas_call x1, Pallas kernels: 186 us -> 173 us  [expert_layer(): pl.pallas_call(functools.partial(expert_kernel, n, experts), out_shape=(j...]
where the time goes in v5:
time: 391 us; the launch traced here: 387 us
  Pallas kernels  378 us (97%)
  local copies, waits for them, and re-layouts  7.09 us (2%)
    pallas_call x1, Pallas kernels, expert_layer(): pl.pallas_call(functools.partial(expert_kernel, n, experts), out_shape=(j...  173 us
    pallas_call x1, Pallas kernels, forward_layer(): pl.pallas_call(functools.partial(forward_kernel, n, experts), out_shape=(...  119 us
    pallas_call x1, Pallas kernels, backward_layer(): pl.pallas_call(functools.partial(backward_kernel, n, experts), out_shape=...  79.6 us

profile of v5, /device:TPU:11, one launch (start us, length us, event | category | flops | bytes accessed | tf_op | source)
XLA Modules:
  0.0 387.2 jit_solution(8423328226715270329)
XLA Ops:
  0.7 0.1 pad.3.clone
  0.7 0.6 broadcast_in_dim_tile.3.freq_ref
  1.3 0.8 copy.21
  2.1 0.8 copy.22
  2.9 0.8 copy.20
  3.6 0.7 maximum_maximum_fusion.tail_ref
  4.3 1.4 copy.23
  5.8 118.7 %forward_layer.1 = (bf16[32,48,4224]{2,1,0:T(8,128)(2,1)}, bf16[4,4,128,1536]{3,2,1,0:T(8,128)(2,1)}, bf16[1536,768]{1,0:T(8,128)(2,1)}, bf16[128,1664]{1,0:T(8,...) custom-call(bf16[128,1536]{1,0:T(8,128)(2,1)} %bitcast.13, ...), custom_call_target="tpu_custom_call" | custom-call | tf_op jit(solution)/shard_map/forward_layer/pallas_call | solution.py:1352
  124.4 172.8 %expert_layer.1 = (f32[128,1536]{1,0:T(8,128)}, f32[128,1664]{1,0:T(8,128)}, bf16[1536,768]{1,0:T(8,128)(2,1)}, f32[384,1536]{1,0:T(8,128)}) custom-call(bf16[128,1664]{1,0:T(8,128)(2,1)} %get-tuple-element.40.x_ref.disp_in, bf16[4,4,128,1536]{3,2,1,0:T(8,128)(2,1)} %get-tuple-element.41.cot_ref, bf16[1536,768]{1,0:T(8,128)(2,1)} %get-tuple-element.42.up_ref, ...), custom_call_target="tpu_custom_call" | custom-call | tf_op jit(solution)/shard_map/expert_layer/pallas_call | solution.py:1024
  297.3 0.0 copy-start
  297.3 79.6 %backward_layer.1 = (f32[128,1536]{1,0:T(8,128)}, f32[48,1536]{1,0:T(8,128)}, f32[48,2560]{1,0:T(8,128)}, f32[48,128]{1,0:T(8,128)}, bf16[4,384,768]{2,1,0:T(8,128)(2,1)}) custom-call(f32[128,1664]{1,0:T(8,128)} %get-tuple-element.45.gs_in, bf16[128,1536]{1,0:T(8,128)(2,1)} %bitcast.14, bf16[128,1536]{1,0:T(8,128)(2,1)} %bitcast.16, ...), custom_call_target="tpu_custom_call" | custom-call | tf_op jit(solution)/shard_map/backward_layer/pallas_call | solution.py:1570
  376.9 0.0 copy-done
  376.9 0.8 convert_element_type.3
  377.7 6.8 %results.1 = (f32[3,384,1024]{2,1,0:T(8,128)}, f32[128,1536]{1,0:T(8,128)}, f32[384,1536]{1,0:T(8,128)}, f32[48,1536]{1,0:T(8,128)}, f32[48,2560]{1,0:T(8,128)}, /*index=5*/f32[48,24]{1,0:T(8,128)}, f32[8,48]{1,0:T(8,128)}) custom-call(bf16[4,384,768]{2,1,0:T(8,128)(2,1)} %get-tuple-element.58.arrived, f32[128,1536]{1,0:T(8,128)} %get-tuple-element.59.tok_in, ...), custom_call_target="tpu_custom_call" | custom-call | tf_op jit(solution)/shard_map/results/pallas_call | solution.py:1616
  384.5 1.3 slice_bitcast_fusion
  385.8 1.4 copy.24
  (3 shorter events, 0.0 us)
Async XLA Ops:
  297.3 79.6 %copy-start = (f32[128,1536]{1,0:T(8,128)S(1)}, f32[128,1536]{1,0:T(8,128)}, u32[]{:S(2)}) copy-start(f32[128,1536]{1,0:T(8,128)} %get-tuple-element.44) | copy-start | bytes 2359300

commit v6 on v5

--- a/solution.py
+++ b/solution.py
@@ -1223,9 +1223,19 @@
 
     own_piece = pltpu.make_async_copy(pieces.at[d], rows_of(d), load_sem.at[2])
 
-    def exchange(k):
+    parts = 3
+    third = share // parts
+
+    def third_of(z, r):
+        return up_all.at[pl.ds(pl.multiple_of(z * share + r * third, third), third), :]
+
+    def exchange(k, r):
         to = lax.rem(d + k, n)
-        return send(pieces.at[to], rows_of(d), a2a_ss.at[k], a2a_sr.at[d], (to, at.e))
+        return send(pieces.at[to, pl.ds(r * third, third), :], third_of(d, r), a2a_ss.at[k, r], a2a_sr.at[d, r], (to, at.e))
+
+    def exchange_part(r):
+        for k in range(1, n):
+            exchange(k, r).start()
 
     at.meet(True)
     dense.begin()
@@ -1239,19 +1249,18 @@
         dense.column(at.near(i))
         if i == n - 1:
             cot.begin_z()
-            for k in range(1, n):
-                exchange(k).start()
+            exchange_part(0)
         dense.plane(at.near(i - 1))
         if i >= 2:
             dense.corner(at.near(i - 2))
     cot.begin_xy()
     dense.plane(at.near(n - 1))
-    if n > 1:
-        dense.corner(at.near(n - 2))
-        cot.column(at.near(1))
+    dense.corner(at.near(n - 2))
+    cot.column(at.near(1))
+    cot.column(at.near(2))
+    exchange_part(1)
+    exchange_part(2)
     dense.corner(at.near(n - 1))
-    for i in range(2, n):
-        cot.column(at.near(i))
     for load in loads:
         load.wait()
     dense.siblings()
@@ -1317,12 +1326,15 @@
     for i in range(1, n):
         cot.plane(at.near(i))
         cot.corner(at.near(i - 1))
+        if i + 2 < n:
+            cot.column(at.near(i + 2))
     cot.corner(at.near(n - 1))
     own_piece.wait()
     for k in range(1, n):
-        exchange(k).wait_send()
         source = lax.rem(d + k, n)
-        send(pieces.at[0], rows_of(source), a2a_ss.at[k], a2a_sr.at[source], (source, at.e)).wait_recv()
+        for r in range(parts):
+            exchange(k, r).wait_send()
+            send(pieces.at[0, pl.ds(r * third, third), :], third_of(source, r), a2a_ss.at[k, r], a2a_sr.at[source, r], (source, at.e)).wait_recv()
     keep.wait()
     dense.finish()
     cot.finish()
@@ -1357,7 +1369,7 @@
         scratch_shapes=[pltpu.VMEM(a.shape, a.dtype) for a in saved]
         + [V(n * 8, shard, wide), V(n, share, 2 * held * (FF // n)), V(shard, wide)]
         + [D_((n, 11)), D_((n,)), D_((n,)), D_((n,)), D_((n, 2)), D_((n, 5))] + gather_sems(n)
-        + [D_((3,)), D_((n,)), D_((n,)), D_((len(saved),))],
+        + [D_((3,)), D_((n, 3)), D_((n, 3)), D_((len(saved),))],
         compiler_params=pltpu.CompilerParams(collective_id=cid, has_side_effects=True, vmem_limit_bytes=60 << 20),
         name="forward_layer",
     )(tok, cot, attn_in, attn_out, tail, ein, segments, routes, freq)

time: 391 us -> 384 us (0.982)
    pallas_call x1, Pallas kernels: 119 us -> 112 us  [forward_layer(): pl.pallas_call(functools.partial(forward_kernel, n, experts), out_shape=(...]
where the time goes in v6:
time: 384 us
  Pallas kernels  375 us (98%)
  local copies, waits for them, and re-layouts  7.09 us (2%)
    pallas_call x1, Pallas kernels, expert_layer(): pl.pallas_call(functools.partial(expert_kernel, n, experts), out_shape=(j...  173 us
    pallas_call x1, Pallas kernels, forward_layer(): pl.pallas_call(functools.partial(forward_kernel, n, experts), out_shape=(...  112 us
    pallas_call x1, Pallas kernels, backward_layer(): pl.pallas_call(functools.partial(backward_kernel, n, experts), out_shape=...  83.3 us

profile of v6, /device:TPU:11, one launch (start us, length us, event | category | flops | bytes accessed | tf_op | source)
XLA Modules:
  0.0 384.0 jit_solution(2891622315135232429)
XLA Ops:
  0.7 0.1 pad.3.clone
  0.7 0.6 broadcast_in_dim_tile.3.freq_ref
  1.3 0.8 copy.21
  2.1 0.8 copy.22
  2.9 0.8 copy.20
  3.6 0.7 maximum_maximum_fusion.tail_ref
  4.3 1.4 copy.23
  5.8 111.6 %forward_layer.1 = (bf16[32,48,4224]{2,1,0:T(8,128)(2,1)}, bf16[4,4,128,1536]{3,2,1,0:T(8,128)(2,1)}, bf16[1536,768]{1,0:T(8,128)(2,1)}, bf16[128,1664]{1,0:T(8,...) custom-call(bf16[128,1536]{1,0:T(8,128)(2,1)} %bitcast.13, ...), custom_call_target="tpu_custom_call" | custom-call | tf_op jit(solution)/shard_map/forward_layer/pallas_call | solution.py:1364
  117.3 173.0 %expert_layer.1 = (f32[128,1536]{1,0:T(8,128)}, f32[128,1664]{1,0:T(8,128)}, bf16[1536,768]{1,0:T(8,128)(2,1)}, f32[384,1536]{1,0:T(8,128)}) custom-call(bf16[128,1664]{1,0:T(8,128)(2,1)} %get-tuple-element.40.x_ref.disp_in, bf16[4,4,128,1536]{3,2,1,0:T(8,128)(2,1)} %get-tuple-element.41.cot_ref, bf16[1536,768]{1,0:T(8,128)(2,1)} %get-tuple-element.42.up_ref, ...), custom_call_target="tpu_custom_call" | custom-call | tf_op jit(solution)/shard_map/expert_layer/pallas_call | solution.py:1024
  290.3 0.0 copy-start
  290.3 83.3 %backward_layer.1 = (f32[128,1536]{1,0:T(8,128)}, f32[48,1536]{1,0:T(8,128)}, f32[48,2560]{1,0:T(8,128)}, f32[48,128]{1,0:T(8,128)}, bf16[4,384,768]{2,1,0:T(8,128)(2,1)}) custom-call(f32[128,1664]{1,0:T(8,128)} %get-tuple-element.45.gs_in, bf16[128,1536]{1,0:T(8,128)(2,1)} %bitcast.14, bf16[128,1536]{1,0:T(8,128)(2,1)} %bitcast.16, ...), custom_call_target="tpu_custom_call" | custom-call | tf_op jit(solution)/shard_map/backward_layer/pallas_call | solution.py:1582
  373.7 0.0 copy-done
  373.7 0.8 convert_element_type.3
  374.5 6.8 %results.1 = (f32[3,384,1024]{2,1,0:T(8,128)}, f32[128,1536]{1,0:T(8,128)}, f32[384,1536]{1,0:T(8,128)}, f32[48,1536]{1,0:T(8,128)}, f32[48,2560]{1,0:T(8,128)}, /*index=5*/f32[48,24]{1,0:T(8,128)}, f32[8,48]{1,0:T(8,128)}) custom-call(bf16[4,384,768]{2,1,0:T(8,128)(2,1)} %get-tuple-element.58.arrived, f32[128,1536]{1,0:T(8,128)} %get-tuple-element.59.tok_in, ...), custom_call_target="tpu_custom_call" | custom-call | tf_op jit(solution)/shard_map/results/pallas_call | solution.py:1628
  381.3 1.3 slice_bitcast_fusion
  382.6 1.4 copy.24
  (3 shorter events, 0.0 us)
Async XLA Ops:
  290.3 83.4 %copy-start = (f32[128,1536]{1,0:T(8,128)S(1)}, f32[128,1536]{1,0:T(8,128)}, u32[]{:S(2)}) copy-start(f32[128,1536]{1,0:T(8,128)} %get-tuple-element.44) | copy-start | bytes 2359300

commit v7 on v6

--- a/solution.py
+++ b/solution.py
@@ -2,6 +2,7 @@
 
 import jax
 import jax.numpy as jnp
+import numpy as np
 from jax import lax
 from jax.experimental import pallas as pl
 from jax.experimental.pallas import tpu as pltpu
@@ -1193,10 +1194,10 @@
     return (same & (source <= target)).astype(f32)
 
 
-def forward_kernel(n, experts, tok_ref, cot_ref, qkv_ref, proj_ref, tail_ref, ein_ref, seg_ref, route_ref, freq_ref,
+def forward_kernel(n, experts, tok_ref, cot_ref, qkv_ref, proj_ref, router_ref, gain_a_ref, gain_f_ref, ein_ref, seg_ref, route_ref, freq_ref,
                    w_all, cot_all, up_all, disp_out, mid_out, gates_out, gain_out, nf_out, q_out, k_out, v_out, p_out, mixed_out, cos_out, sin_out,
                    disp_ref, mid_ref, gates_ref, gain_ref, nf_ref, q_ref, k_ref, v_ref, p_ref, mixed_ref, cos_ref, sin_ref,
-                   wv, pieces, dense_ref, *rest):
+                   wv, pieces, dense_ref, small_ref, *rest):
     f32, bf16 = jnp.float32, jnp.bfloat16
     at = Place(n)
     d = at.d
@@ -1210,7 +1211,12 @@
     qkv_width = q_width + 2 * k_width
     dense_ref[:, :qkv_width] = qkv_ref[...]
     dense_ref[:, qkv_width : qkv_width + D] = proj_ref[...]
-    dense_ref[:, qkv_width + D :] = tail_ref[...]
+    shard = dense_ref.shape[0]
+    small_ref[...] = jnp.zeros(small_ref.shape, f32)
+    small_ref[:experts, :shard] = router_ref[...].astype(f32)
+    small_ref[experts : experts + 1, :shard] = gain_a_ref[...].astype(f32)
+    small_ref[experts + 1 : experts + 2, :shard] = gain_f_ref[...].astype(f32)
+    dense_ref[:, qkv_width + D :] = jnp.transpose(small_ref[...])[:shard].astype(bf16)
     loads = [
         pltpu.make_async_copy(dense_ref, wv.at[d * 8 + at.e], load_sem.at[0]),
         pltpu.make_async_copy(cot_ref, cot_all.at[d, 0], load_sem.at[1]),
@@ -1306,10 +1312,11 @@
     mid = mid_ref[...]
     disp_ref[:, :D] = (mid * inverse_rms(mid) * gain_ref[1:2, :]).astype(bf16)
     logits = mm(disp_ref[:, :D], weight(tail_at, 128))
-    lanes = lane_tile(mid.shape[0])
-    chosen = jnp.zeros(lanes.shape, f32)
-    for k in range(TOP_K):
-        chosen += (route_ref[:, k : k + 1] == lanes).astype(f32)
+    hits = []
+    for i in range(route_ref.shape[0]):
+        expert = lax.broadcasted_iota(jnp.int32, (128, route_ref.shape[2]), 0)
+        hits.append(sum((route_ref[i, k : k + 1, :] == expert).astype(f32) for k in range(TOP_K)))
+    chosen = jnp.transpose(jnp.concatenate(hits, axis=1))
     masked = jnp.where(chosen > 0, logits, neg_large)
     raised = jnp.where(chosen > 0, jnp.exp(masked - jnp.max(masked, axis=1, keepdims=True)), 0.0)
     gates = raised / jnp.sum(raised, axis=1, keepdims=True)
@@ -1342,7 +1349,7 @@
         copy.wait()
 
 
-def forward_layer(tok, cot, attn_in, attn_out, tail, ein, segments, routes, n, experts, cid):
+def forward_layer(tok, cot, attn_in, attn_out, router, gain_attn, gain_ffn, ein, segments, routes, n, experts, cid):
     f32, bf16 = jnp.float32, jnp.bfloat16
     rows = tok.shape[0]
     shard = attn_in.shape[0]
@@ -1351,7 +1358,7 @@
     wide = q_width + 2 * k_width + D + 128
     groups = HEADS // KV_HEADS
     half = HEAD // 2
-    freq = jnp.tile(rope_base ** (-jnp.arange(half, dtype=f32) / half), 128 // half)[None, :]
+    freq = np.tile(np.float32(rope_base) ** (-np.arange(half, dtype=np.float32) / np.float32(half)), 128 // half)[None, :]
     D_ = pltpu.SemaphoreType.DMA
     V = lambda *s: pltpu.VMEM(s, bf16)
     any_, vm = pl.BlockSpec(memory_space=pl.ANY), pl.BlockSpec(memory_space=pltpu.VMEM)
@@ -1364,15 +1371,15 @@
     return pl.pallas_call(
         functools.partial(forward_kernel, n, experts),
         out_shape=(S((n * 8, shard, wide), bf16), S((n, 4, rows, D), bf16), S((D, 2 * held * (FF // n)), bf16)) + saved,
-        in_specs=[vm, any_] + [vm] * 7,
+        in_specs=[vm, any_] + [vm] * 9,
         out_specs=[any_] * 15,
         scratch_shapes=[pltpu.VMEM(a.shape, a.dtype) for a in saved]
-        + [V(n * 8, shard, wide), V(n, share, 2 * held * (FF // n)), V(shard, wide)]
+        + [V(n * 8, shard, wide), V(n, share, 2 * held * (FF // n)), V(shard, wide), pltpu.VMEM((128, 128), f32)]
         + [D_((n, 11)), D_((n,)), D_((n,)), D_((n,)), D_((n, 2)), D_((n, 5))] + gather_sems(n)
         + [D_((3,)), D_((n, 3)), D_((n, 3)), D_((len(saved),))],
         compiler_params=pltpu.CompilerParams(collective_id=cid, has_side_effects=True, vmem_limit_bytes=60 << 20),
         name="forward_layer",
-    )(tok, cot, attn_in, attn_out, tail, ein, segments, routes, freq)
+    )(tok, cot, attn_in, attn_out, router.T, gain_attn[None, :], gain_ffn[None, :], ein, segments, routes.transpose(0, 2, 1), freq)
 
 
 def backward_kernel(n, experts, gs_in, tok_in, cot_in, mid_in, gates_in, gain_in, nf_in, disp_in, q_in, k_in, v_in, p_in, mixed_in, cos_in, sin_in, w_ref, gup_ref,
@@ -1611,8 +1618,8 @@
     def _():
         proj_ref[...] = out_in[...]
         qkv_ref[...] = qkv_in[...]
-        router_ref[...] = tail_in[:, :experts]
         turned = jnp.transpose(jnp.concatenate([tail_in[...], jnp.zeros((128 - tail_in.shape[0], 128), jnp.float32)], axis=0))
+        router_ref[...] = turned[:experts, : tail_in.shape[0]]
         gains_ref[...] = turned[experts : experts + 8, : tail_in.shape[0]]
 
 
@@ -1624,7 +1631,7 @@
     whole = lambda a: pl.BlockSpec(a.shape, lambda i: (0,) * len(a.shape))
     part = lambda a: pl.BlockSpec((a.shape[0] // steps, a.shape[1]), lambda i: (i, 0))
     shapes = [jax.ShapeDtypeStruct(a.shape, f32) for a in (tok, down, proj, qkv)]
-    shapes += [jax.ShapeDtypeStruct((tail.shape[0], experts), f32), jax.ShapeDtypeStruct((8, tail.shape[0]), f32)]
+    shapes += [jax.ShapeDtypeStruct((experts, tail.shape[0]), f32), jax.ShapeDtypeStruct((8, tail.shape[0]), f32)]
     return pl.pallas_call(
         functools.partial(results_kernel, experts),
         grid=(steps,),
@@ -1643,12 +1650,10 @@
     held = expert_in.shape[0]
     experts = held * 8
     f = FF // n
-    shard = attn_in.shape[0]
     x = tokens.reshape(total, D)
     cot = cotangent.reshape(total, D)
-    tail = jnp.concatenate([router, gain_attn[:, None], gain_ffn[:, None], jnp.zeros((shard, 126 - experts), bf16)], axis=1)
     w_all, cot_all, up, disp, middle, gates, gain, nf, q, k, v, p, mixed, cos, sin = forward_layer(
-        x, cot, attn_in, attn_out, tail, expert_in, segments, routes.reshape(total, TOP_K), n, experts, 0)
+        x, cot, attn_in, attn_out, router, gain_attn, gain_ffn, expert_in, segments, routes, n, experts, 0)
     out, grad_sum, grad_up, grad_down = expert_layer(disp, cot_all, up, expert_out.reshape(held * f, D), middle, n, experts, 1)
     grad_tokens, grad_out, grad_in, grad_tail, grad_up = backward_layer(
         grad_sum, x, cot, middle, gates, gain, nf, disp, q, k, v, p, mixed, cos, sin, w_all, grad_up, n, experts, 2)
@@ -1661,7 +1666,7 @@
         grad_in,
         grad_out,
         grad_gains[1],
-        grad_router,
+        grad_router.T,
         grad_up,
         grad_down.reshape(held, f, D),
     )

time: 384 us -> 378 us (0.984)
  local copies, waits for them, and re-layouts: 7.09 us -> 1.28 us
where the time goes in v7:
time: 378 us
  Pallas kernels  375 us (99%)
    pallas_call x1, Pallas kernels, expert_layer(): pl.pallas_call(functools.partial(expert_kernel, n, experts), out_shape=(j...  173 us
    pallas_call x1, Pallas kernels, forward_layer(): pl.pallas_call(functools.partial(forward_kernel, n, experts), out_shape=(...  112 us
    pallas_call x1, Pallas kernels, backward_layer(): pl.pallas_call(functools.partial(backward_kernel, n, experts), out_shape=...  83.4 us

profile of v7, /device:TPU:11, one launch (start us, length us, event | category | flops | bytes accessed | tf_op | source)
XLA Modules:
  0.0 377.6 jit_solution(18375213238253147177)
XLA Ops:
  0.6 111.7 %forward_layer.1 = (bf16[32,48,4224]{2,1,0:T(8,128)(2,1)}, bf16[4,4,128,1536]{3,2,1,0:T(8,128)(2,1)}, bf16[1536,768]{1,0:T(8,128)(2,1)}, bf16[128,1664]{1,0:T(8,...) custom-call(bf16[128,1536]{1,0:T(8,128)(2,1)} %bitcast.15, ...), custom_call_target="tpu_custom_call" | custom-call | tf_op jit(solution)/shard_map/forward_layer/pallas_call | solution.py:1371
  112.4 172.9 %expert_layer.1 = (f32[128,1536]{1,0:T(8,128)}, f32[128,1664]{1,0:T(8,128)}, bf16[1536,768]{1,0:T(8,128)(2,1)}, f32[384,1536]{1,0:T(8,128)}) custom-call(bf16[128,1664]{1,0:T(8,128)(2,1)} %get-tuple-element.40.x_ref.disp_in, bf16[4,4,128,1536]{3,2,1,0:T(8,128)(2,1)} %get-tuple-element.41.cot_ref, bf16[1536,768]{1,0:T(8,128)(2,1)} %get-tuple-element.42.up_ref, ...), custom_call_target="tpu_custom_call" | custom-call | tf_op jit(solution)/shard_map/expert_layer/pallas_call | solution.py:1025
  285.3 0.0 copy-start
  285.3 83.4 %backward_layer.1 = (f32[128,1536]{1,0:T(8,128)}, f32[48,1536]{1,0:T(8,128)}, f32[48,2560]{1,0:T(8,128)}, f32[48,128]{1,0:T(8,128)}, bf16[4,384,768]{2,1,0:T(8,128)(2,1)}) custom-call(f32[128,1664]{1,0:T(8,128)} %get-tuple-element.45.gs_in, bf16[128,1536]{1,0:T(8,128)(2,1)} %bitcast.16, bf16[128,1536]{1,0:T(8,128)(2,1)} %bitcast.18, ...), custom_call_target="tpu_custom_call" | custom-call | tf_op jit(solution)/shard_map/backward_layer/pallas_call | solution.py:1589
  368.7 0.0 copy-done
  368.7 0.8 convert_element_type.3
  369.5 6.8 %results.1 = (f32[3,384,1024]{2,1,0:T(8,128)}, f32[128,1536]{1,0:T(8,128)}, f32[384,1536]{1,0:T(8,128)}, f32[48,1536]{1,0:T(8,128)}, f32[48,2560]{1,0:T(8,128)}, /*index=5*/f32[24,48]{1,0:T(8,128)}, f32[8,48]{1,0:T(8,128)}) custom-call(bf16[4,384,768]{2,1,0:T(8,128)(2,1)} %get-tuple-element.58.arrived, f32[128,1536]{1,0:T(8,128)} %get-tuple-element.59.tok_in, ...), custom_call_target="tpu_custom_call" | custom-call | tf_op jit(solution)/shard_map/results/pallas_call | solution.py:1635
  376.3 1.3 slice_bitcast_fusion
Async XLA Ops:
  285.3 83.4 %copy-start = (f32[128,1536]{1,0:T(8,128)S(1)}, f32[128,1536]{1,0:T(8,128)}, u32[]{:S(2)}) copy-start(f32[128,1536]{1,0:T(8,128)} %get-tuple-element.44) | copy-start | bytes 2359300

commit v8 on v7

--- a/solution.py
+++ b/solution.py
@@ -652,7 +652,7 @@
 
 def add_rows(dst, src):
     rows = dst.shape[0]
-    step = 16
+    step = 32 if rows % 32 == 0 else 48 if rows % 48 == 0 else 16
 
     @pl.loop(0, rows // step)
     def _(r):
@@ -1602,8 +1602,8 @@
     )(gs, tok, cot, mid, gates, gain, nf, disp, q, k, v, p, mixed, cos, sin, w_all, gup)
 
 
-def results_kernel(experts, arrived, tok_in, down_in, out_in, qkv_in, tail_in,
-                   up_ref, tok_ref, down_ref, proj_ref, qkv_ref, router_ref, gains_ref):
+def results_kernel(experts, arrived, layer_in, tok_in, down_in, out_in, qkv_in, tail_in,
+                   up_ref, layer_ref, tok_ref, down_ref, proj_ref, qkv_ref, router_ref, gains_ref):
     n, width = arrived.shape[0], arrived.shape[2]
     f = FF // n
     for q in range(n):
@@ -1611,6 +1611,7 @@
             lo = (j % 2) * FF + q * f
             up_ref[j // 2, :, lo : lo + f] = arrived[q, :, j * f : (j + 1) * f].astype(jnp.float32)
 
+    layer_ref[...] = layer_in[...].astype(jnp.bfloat16)
     tok_ref[...] = tok_in[...]
     down_ref[...] = down_in[...]
 
@@ -1623,7 +1624,7 @@
         gains_ref[...] = turned[experts : experts + 8, : tail_in.shape[0]]
 
 
-def results(arrived, tok, down, proj, qkv, tail, held, experts):
+def results(arrived, layer, tok, down, proj, qkv, tail, held, experts):
     n, share, width = arrived.shape
     f32 = jnp.float32
     steps = 4
@@ -1635,16 +1636,15 @@
     return pl.pallas_call(
         functools.partial(results_kernel, experts),
         grid=(steps,),
-        out_shape=[jax.ShapeDtypeStruct((held, share, 2 * FF), f32)] + shapes,
-        in_specs=[pl.BlockSpec((n, rows, width), lambda i: (0, i, 0))] + [part(a) for a in (tok, down)] + [whole(a) for a in (proj, qkv, tail)],
-        out_specs=[pl.BlockSpec((held, rows, 2 * FF), lambda i: (0, i, 0))] + [part(a) for a in (tok, down)] + [whole(a) for a in shapes[2:]],
+        out_shape=[jax.ShapeDtypeStruct((held, share, 2 * FF), f32), jax.ShapeDtypeStruct(layer.shape, jnp.bfloat16)] + shapes,
+        in_specs=[pl.BlockSpec((n, rows, width), lambda i: (0, i, 0))] + [part(a) for a in (layer, tok, down)] + [whole(a) for a in (proj, qkv, tail)],
+        out_specs=[pl.BlockSpec((held, rows, 2 * FF), lambda i: (0, i, 0))] + [part(a) for a in (layer, tok, down)] + [whole(a) for a in shapes[2:]],
         compiler_params=pltpu.CompilerParams(vmem_limit_bytes=62 << 20),
         name="results",
-    )(arrived, tok, down, proj, qkv, tail)
+    )(arrived, layer, tok, down, proj, qkv, tail)
 
 
 def per_device_fast(n, tokens, segments, routes, cotangent, gain_attn, attn_in, attn_out, gain_ffn, router, expert_in, expert_out):
-    f32, bf16 = jnp.float32, jnp.bfloat16
     micro, rows = tokens.shape[:2]
     total = micro * rows
     held = expert_in.shape[0]
@@ -1657,10 +1657,10 @@
     out, grad_sum, grad_up, grad_down = expert_layer(disp, cot_all, up, expert_out.reshape(held * f, D), middle, n, experts, 1)
     grad_tokens, grad_out, grad_in, grad_tail, grad_up = backward_layer(
         grad_sum, x, cot, middle, gates, gain, nf, disp, q, k, v, p, mixed, cos, sin, w_all, grad_up, n, experts, 2)
-    grad_up, grad_tokens, grad_down, grad_out, grad_in, grad_router, grad_gains = results(
-        grad_up, grad_tokens, grad_down, grad_out, grad_in, grad_tail, held, experts)
+    grad_up, out, grad_tokens, grad_down, grad_out, grad_in, grad_router, grad_gains = results(
+        grad_up, out, grad_tokens, grad_down, grad_out, grad_in, grad_tail, held, experts)
     return (
-        out.astype(bf16).reshape(micro, rows, D),
+        out.reshape(micro, rows, D),
         grad_tokens.reshape(micro, rows, D),
         grad_gains[0],
         grad_in,

time: 378 us -> 377 us (level)
  no operation moved by 1% of the time
where the time goes in v8:
time: 377 us
  Pallas kernels  375 us (99%)
    pallas_call x1, Pallas kernels, expert_layer(): pl.pallas_call(functools.partial(expert_kernel, n, experts), out_shape=(j...  173 us
    pallas_call x1, Pallas kernels, forward_layer(): pl.pallas_call(functools.partial(forward_kernel, n, experts), out_shape=(...  112 us
    pallas_call x1, Pallas kernels, backward_layer(): pl.pallas_call(functools.partial(backward_kernel, n, experts), out_shape=...  83.4 us

profile of v8, /device:TPU:11, one launch (start us, length us, event | category | flops | bytes accessed | tf_op | source)
XLA Modules:
  0.0 377.1 jit_solution(7438632357230368240)
XLA Ops:
  0.6 111.7 %forward_layer.1 = (bf16[32,48,4224]{2,1,0:T(8,128)(2,1)}, bf16[4,4,128,1536]{3,2,1,0:T(8,128)(2,1)}, bf16[1536,768]{1,0:T(8,128)(2,1)}, bf16[128,1664]{1,0:T(8,...) custom-call(bf16[128,1536]{1,0:T(8,128)(2,1)} %bitcast.15, ...), custom_call_target="tpu_custom_call" | custom-call | tf_op jit(solution)/shard_map/forward_layer/pallas_call | solution.py:1371
  112.4 172.7 %expert_layer.1 = (f32[128,1536]{1,0:T(8,128)}, f32[128,1664]{1,0:T(8,128)}, bf16[1536,768]{1,0:T(8,128)(2,1)}, f32[384,1536]{1,0:T(8,128)}) custom-call(bf16[128,1664]{1,0:T(8,128)(2,1)} %get-tuple-element.41.x_ref.disp_in, bf16[4,4,128,1536]{3,2,1,0:T(8,128)(2,1)} %get-tuple-element.42.cot_ref, bf16[1536,768]{1,0:T(8,128)(2,1)} %get-tuple-element.43.up_ref, ...), custom_call_target="tpu_custom_call" | custom-call | tf_op jit(solution)/shard_map/expert_layer/pallas_call | solution.py:1025
  285.1 83.4 %backward_layer.1 = (f32[128,1536]{1,0:T(8,128)}, f32[48,1536]{1,0:T(8,128)}, f32[48,2560]{1,0:T(8,128)}, f32[48,128]{1,0:T(8,128)}, bf16[4,384,768]{2,1,0:T(8,128)(2,1)}) custom-call(f32[128,1664]{1,0:T(8,128)} %get-tuple-element.45.gs_in, bf16[128,1536]{1,0:T(8,128)(2,1)} %bitcast.16, bf16[128,1536]{1,0:T(8,128)(2,1)} %bitcast.18, ...), custom_call_target="tpu_custom_call" | custom-call | tf_op jit(solution)/shard_map/backward_layer/pallas_call | solution.py:1589
  368.6 7.2 %results.1 = (f32[3,384,1024]{2,1,0:T(8,128)}, bf16[128,1536]{1,0:T(8,128)(2,1)}, f32[128,1536]{1,0:T(8,128)}, f32[384,1536]{1,0:T(8,128)}, f32[48,1536]{1,0:T(8...) custom-call(bf16[4,384,768]{2,1,0:T(8,128)(2,1)} %get-tuple-element.58.arrived, ...), custom_call_target="tpu_custom_call" | custom-call | tf_op jit(solution)/shard_map/results/pallas_call | solution.py:1636
  375.8 1.3 slice_bitcast_fusion
